TPU v7x, 128 devices: a whole 4x4x4 slice. The times are simulated.
128 devices in a mesh: fsdp: 4 (over y), ctx: 32 (over z, x, core).
Axes of the slice: x: 4, y: 4, z: 4, core: 2. Of those that a mesh axis runs over, the one named last changes fastest.
Arguments:
- tokens: bfloat16 [12, 4096, 2560], P('fsdp', 'ctx'), may hold values from -6 to 6
- doc_ids: int32 [12, 4096], P('fsdp', 'ctx'), may hold values from 0 to 15, never falling along the last dimension, each value on 1 to 2048 neighbouring positions
- cotangent: bfloat16 [12, 4096, 2560], P('fsdp', 'ctx'), may hold values from -6 to 6
- input_gain: float32 [2560], replicated, may hold values from 0.5 to 1.5
- query_weight: bfloat16 [2560, 1024], P('fsdp'), may hold values from -1 to 1
- key_weight: bfloat16 [2560, 512], P('fsdp'), may hold values from -1 to 1
- value_weight: bfloat16 [2560, 512], P('fsdp'), may hold values from -0.125 to 0.125
- output_weight: bfloat16 [1024, 2560], P('fsdp'), may hold values from -0.1875 to 0.1875
- query_gain: float32 [256], replicated, may hold values from 0 to 8
- key_gain: float32 [256], replicated, may hold values from 0 to 8
- post_gain: float32 [2560], replicated, may hold values from 0.25 to 1.75
Outputs:
- layer_out: bfloat16 [12, 4096, 2560], P('fsdp', 'ctx')
- tokens_grad: bfloat16 [12, 4096, 2560], P('fsdp', 'ctx')
- query_grad: float32 [2560, 1024], P('ctx', 'fsdp')
- key_grad: float32 [2560, 512], P('ctx', 'fsdp')
- value_grad: float32 [2560, 512], P('ctx', 'fsdp')
- output_grad: float32 [1024, 2560], P('ctx', 'fsdp')
Inputs may be any that keep to these rules, and one draw needn't show every extreme that they name: `doc_ids`: along each sequence the document number never falls from one position to the next.
All inputs are finite; a program needn't handle non-finite values.
Results may differ from a plain program's by a relative error of at most 0.024.
The roundings to bfloat16 on the way count: a program that leaves them out, or rounds other values in their place, can miss the bound.
Values may be sent and summed in bfloat16 or wider, within the bound.
A program may use at most 192 MiB of HBM per device.

v0:
```python
import jax
import jax.numpy as jnp
from jax import lax
from jax.sharding import PartitionSpec as P

DH = 256
WINDOW = 1024


epsilon = 1e-06
rope_base = 10000.0
query_factor = 0.0625


def shifted(block, axis, distance):
    devices = range(lax.axis_size(axis))
    route = [(i - distance, i) for i in devices if i - distance in devices]
    return lax.ppermute(block, axis, route)


def norm_scale(values, gain):
    mean_square = jnp.mean(values * values, axis=-1, keepdims=True)
    return values * lax.rsqrt(mean_square + epsilon) * gain


def rotate(values, positions):
    half_width = values.shape[-1] // 2
    exponents = jnp.arange(half_width, dtype=jnp.int32).astype(jnp.float32) * (
        2.0 / values.shape[-1]
    )
    angles = positions.astype(jnp.float32)[..., None] * rope_base ** (-exponents)
    cosine = jnp.cos(angles)[..., None, :]
    sine = jnp.sin(angles)[..., None, :]
    first_half = values[..., :half_width]
    second_half = values[..., half_width:]
    return jnp.concatenate(
        [first_half * cosine - second_half * sine, second_half * cosine + first_half * sine],
        axis=-1,
    )


def head_norm(raw, gain, positions, factor):
    shaped = raw.reshape(raw.shape[:-1] + (raw.shape[-1] // gain.shape[0], gain.shape[0]))
    return (rotate(norm_scale(shaped, gain), positions) * factor).reshape(raw.shape)


def split_heads(queries, keys, values):
    batch, rows, _ = queries.shape
    columns = keys.shape[1]
    kv_heads = keys.shape[-1] // DH
    ratio = queries.shape[-1] // keys.shape[-1]
    query_heads = queries.reshape(batch, rows, kv_heads, ratio, DH)
    key_heads = keys.reshape(batch, columns, kv_heads, DH)
    value_heads = values.reshape(batch, columns, kv_heads, DH)
    return (query_heads, key_heads, value_heads)


def attend(queries, keys, values, allowed):
    batch, rows, _ = queries.shape
    query_heads, key_heads, value_heads = split_heads(queries, keys, values)
    scores = jnp.einsum(
        "bsgrd,bkgd->bgrsk", query_heads, key_heads, preferred_element_type=jnp.float32
    )
    mask = allowed[:, None, None]
    masked = jnp.where(mask, scores, -1e30)
    highest = jnp.max(masked, axis=-1, keepdims=True)
    raised = jnp.where(mask, jnp.exp(masked - highest), 0.0)
    probabilities = raised / jnp.sum(raised, axis=-1, keepdims=True)
    soft_weights = probabilities.astype(jnp.bfloat16)
    attended = jnp.einsum(
        "bgrsk,bkgd->bsgrd", soft_weights, value_heads, preferred_element_type=jnp.float32
    )
    return (attended.reshape(batch, rows, -1).astype(jnp.bfloat16), probabilities, soft_weights)


def attend_back(queries, keys, values, probabilities, soft_weights, grad_attended):
    batch, rows, _ = queries.shape
    columns = keys.shape[1]
    query_heads, key_heads, value_heads = split_heads(queries, keys, values)
    grad_heads = grad_attended.reshape(query_heads.shape)
    grad_values = jnp.einsum(
        "bgrsk,bsgrd->bkgd", soft_weights, grad_heads, preferred_element_type=jnp.float32
    )
    grad_weights = jnp.einsum(
        "bsgrd,bkgd->bgrsk", grad_heads, value_heads, preferred_element_type=jnp.float32
    )
    grad_scores = probabilities * (
        grad_weights - jnp.sum(probabilities * grad_weights, axis=-1, keepdims=True)
    )
    score_grads = grad_scores.astype(jnp.bfloat16)
    grad_queries = jnp.einsum(
        "bgrsk,bkgd->bsgrd", score_grads, key_heads, preferred_element_type=jnp.float32
    )
    grad_keys = jnp.einsum(
        "bgrsk,bsgrd->bkgd", score_grads, query_heads, preferred_element_type=jnp.float32
    )
    return (
        grad_queries.reshape(batch, rows, -1),
        grad_keys.reshape(batch, columns, -1),
        grad_values.reshape(batch, columns, -1),
    )


def fetch_before(own_block, reach_blocks):
    before = []
    current = own_block
    for hop_number in range(reach_blocks):
        current = shifted(current, "ctx", 1)
        before.append(current)
    return before


def return_after(outgoing, reach_blocks):
    returned = jnp.zeros(outgoing[0].shape, jnp.float32)
    for distance in range(1, reach_blocks + 1):
        arrived = shifted(outgoing[distance - 1], "ctx", -distance)
        returned = returned + arrived.astype(jnp.float32)
    return returned


def per_device(
    tokens,
    doc_ids,
    cotangent,
    input_gain,
    query_weight,
    key_weight,
    value_weight,
    output_weight,
    query_gain,
    key_gain,
    post_gain,
):
    seq_count, shard_size, width = tokens.shape
    block_index = lax.axis_index("ctx")
    reach_blocks = WINDOW // shard_size
    wq_all, wk_all, wv_all, wo_all = (
        lax.all_gather(query_weight, "fsdp", axis=0, tiled=True),
        lax.all_gather(key_weight, "fsdp", axis=0, tiled=True),
        lax.all_gather(value_weight, "fsdp", axis=0, tiled=True),
        lax.all_gather(output_weight, "fsdp", axis=0, tiled=True),
    )
    tokens_wide = tokens.astype(jnp.float32)
    normed = norm_scale(tokens_wide, input_gain).astype(jnp.bfloat16)
    flat_rows = normed.reshape(seq_count * shard_size, width)
    query_raw = jnp.dot(flat_rows, wq_all, preferred_element_type=jnp.float32).reshape(
        seq_count, shard_size, -1
    )
    key_raw = jnp.dot(flat_rows, wk_all, preferred_element_type=jnp.float32).reshape(
        seq_count, shard_size, -1
    )
    values = (
        jnp.dot(flat_rows, wv_all, preferred_element_type=jnp.float32)
        .astype(jnp.bfloat16)
        .reshape(seq_count, shard_size, -1)
    )
    offsets = jnp.arange(shard_size, dtype=jnp.int32)
    positions = jnp.broadcast_to(block_index * shard_size + offsets, (seq_count, shard_size))

    def prepare_query(raw):
        return head_norm(raw, query_gain, positions, query_factor)

    def prepare_key(raw):
        return head_norm(raw, key_gain, positions, 1.0)

    queries = prepare_query(query_raw).astype(jnp.bfloat16)
    keys = prepare_key(key_raw).astype(jnp.bfloat16)
    own_block = jnp.stack([keys, values])
    before = fetch_before(own_block, reach_blocks)
    window = jnp.concatenate(before[::-1] + [own_block], axis=2)
    doc_parts = []
    for distance in range(reach_blocks, 0, -1):
        doc_parts.append(shifted(doc_ids, "ctx", distance))
    key_docs = jnp.concatenate(doc_parts + [doc_ids], axis=1)
    span_keys = (reach_blocks + 1) * shard_size
    key_positions = (
        block_index * shard_size
        - reach_blocks * shard_size
        + jnp.arange(span_keys, dtype=jnp.int32)
    )
    allowed = (
        (key_docs[:, None, :] == doc_ids[:, :, None])
        & (key_positions[None, None, :] >= 0)
        & (key_positions[None, None, :] <= positions[:, :, None])
        & (key_positions[None, None, :] > positions[:, :, None] - WINDOW)
    )
    attended, probabilities, soft_weights = attend(queries, window[0], window[1], allowed)
    heads_width = attended.shape[-1]
    attended_rows = attended.reshape(-1, heads_width)
    projected = jnp.dot(attended_rows, wo_all, preferred_element_type=jnp.float32).reshape(
        seq_count, shard_size, width
    )
    layer_out = (tokens_wide + norm_scale(projected, post_gain)).astype(jnp.bfloat16)
    upstream = cotangent.astype(jnp.float32)
    _, post_back = jax.vjp(lambda inner: norm_scale(inner, post_gain), projected)
    grad_projected = post_back(upstream)[0].astype(jnp.bfloat16).reshape(-1, width)
    contract = (((1,), (1,)), ((), ()))
    grad_attended = lax.dot_general(
        grad_projected, wo_all, contract, preferred_element_type=jnp.float32
    )
    grad_attended = grad_attended.astype(jnp.bfloat16).reshape(seq_count, shard_size, heads_width)
    grad_queries, grad_keys, grad_values = attend_back(
        queries, window[0], window[1], probabilities, soft_weights, grad_attended
    )
    kv_width = keys.shape[-1]
    grad_pairs = jnp.stack([grad_keys, grad_values]).reshape(
        2, seq_count, reach_blocks + 1, shard_size, kv_width
    )
    outgoing = [
        grad_pairs[:, :, reach_blocks - distance].astype(jnp.bfloat16)
        for distance in range(1, reach_blocks + 1)
    ]
    pair_total = grad_pairs[:, :, reach_blocks] + return_after(outgoing, reach_blocks)
    _, query_back = jax.vjp(prepare_query, query_raw)
    _, key_back = jax.vjp(prepare_key, key_raw)
    query_delta = query_back(grad_queries)[0].astype(jnp.bfloat16).reshape(-1, heads_width)
    key_delta = key_back(pair_total[0])[0].astype(jnp.bfloat16).reshape(-1, kv_width)
    value_delta = pair_total[1].astype(jnp.bfloat16).reshape(-1, kv_width)
    grad_normed = (
        lax.dot_general(query_delta, wq_all, contract, preferred_element_type=jnp.float32)
        + lax.dot_general(key_delta, wk_all, contract, preferred_element_type=jnp.float32)
        + lax.dot_general(value_delta, wv_all, contract, preferred_element_type=jnp.float32)
    )
    _, input_back = jax.vjp(lambda inner: norm_scale(inner, input_gain), tokens_wide)
    tokens_grad = (
        upstream + input_back(grad_normed.reshape(seq_count, shard_size, width))[0]
    ).astype(jnp.bfloat16)
    across = (((0,), (0,)), ((), ()))
    query_term = lax.dot_general(flat_rows, query_delta, across, preferred_element_type=jnp.float32)
    key_term = lax.dot_general(flat_rows, key_delta, across, preferred_element_type=jnp.float32)
    value_term = lax.dot_general(flat_rows, value_delta, across, preferred_element_type=jnp.float32)
    output_term = lax.dot_general(
        attended_rows, grad_projected, across, preferred_element_type=jnp.float32
    )
    part_query, part_key, part_value, part_output = (
        lax.psum_scatter(
            query_term.astype(jnp.bfloat16), "fsdp", scatter_dimension=1, tiled=True
        ).astype(jnp.float32),
        lax.psum_scatter(
            key_term.astype(jnp.bfloat16), "fsdp", scatter_dimension=1, tiled=True
        ).astype(jnp.float32),
        lax.psum_scatter(
            value_term.astype(jnp.bfloat16), "fsdp", scatter_dimension=1, tiled=True
        ).astype(jnp.float32),
        lax.psum_scatter(
            output_term.astype(jnp.bfloat16), "fsdp", scatter_dimension=1, tiled=True
        ).astype(jnp.float32),
    )
    query_grad, key_grad, value_grad, output_grad = (
        lax.psum_scatter(
            part_query.astype(jnp.bfloat16), "ctx", scatter_dimension=0, tiled=True
        ).astype(jnp.float32),
        lax.psum_scatter(
            part_key.astype(jnp.bfloat16), "ctx", scatter_dimension=0, tiled=True
        ).astype(jnp.float32),
        lax.psum_scatter(
            part_value.astype(jnp.bfloat16), "ctx", scatter_dimension=0, tiled=True
        ).astype(jnp.float32),
        lax.psum_scatter(
            part_output.astype(jnp.bfloat16), "ctx", scatter_dimension=0, tiled=True
        ).astype(jnp.float32),
    )
    return (layer_out, tokens_grad, query_grad, key_grad, value_grad, output_grad)


def solution(mesh):
    placed = (
        P("fsdp", "ctx", None),
        P("fsdp", "ctx"),
        P("fsdp", "ctx", None),
        P(),
        P("fsdp", None),
        P("fsdp", None),
        P("fsdp", None),
        P("fsdp", None),
        P(),
        P(),
        P(),
    )
    return jax.shard_map(
        per_device,
        mesh=mesh,
        in_specs=placed,
        out_specs=(
            P("fsdp", "ctx", None),
            P("fsdp", "ctx", None),
            P("ctx", "fsdp"),
            P("ctx", "fsdp"),
            P("ctx", "fsdp"),
            P("ctx", "fsdp"),
        ),
        check_vma=False,
    )
```

profile of v0, /device:TPU:1, one launch (start us, length us, event | category | flops | bytes accessed | tf_op | source)
XLA Modules:
  0.0 1011.1 jit_solution(10391798821774372180)
XLA Ops:
  12.9 34.9 %all-gather.7.cloned.1.call-done = bf16[2560,512]{1,0:T(8,128)(2,1)} async-done(((bf16[640,512]{1,0:T(8,128)(2,1)}), bf16[2560,512]{1,0:T(8,128)(2,1)}) %all-gather.7.cloned.1.call-update) | async-done | bytes 2621456 | tf_op jit(solution)/shard_map/all_gather | solution.py:140
  51.6 33.2 %all-gather.5.cloned.1.call-done = bf16[2560,512]{1,0:T(8,128)(2,1)} async-done(((bf16[640,512]{1,0:T(8,128)(2,1)}), bf16[2560,512]{1,0:T(8,128)(2,1)}) %all-gather.5.cloned.1.call-update) | async-done | bytes 2621456 | tf_op jit(solution)/shard_map/all_gather | solution.py:139
  98.3 8.9 collective-permute-done
  112.5 8.9 collective-permute-done.1
  126.7 8.9 collective-permute-done.2
  140.0 8.8 collective-permute-done.3
  158.4 13.5 %collective-permute-start.13 = (s32[3,128]{1,0:T(4,128)S(1)}, s32[3,128]{1,0:T(4,128)S(1)}, u32[]{:S(2)}, u32[]{:S(2)}) collective-permute-start(s32[3,128]{1,0:T(4,128)S(1)} %copy-done.40), channel_id=1, source_target_pairs={{0,3},{1,4},{2,5},{3,6},{4,7},{5,8},{6,9},{7,10},{8,11},{9,12},{10... | collective-permute-start | bytes 4616 | tf_op jit(solution)/shard_map/ppermute | solution.py:18
  238.7 9.1 fusion.47
  298.2 10.1 %reshape.197 = f32[1,3,9,128,512]{3,2,4,1,0:T(8,128)} reshape(f32[3,1152,2,256]{1,3,2,0:T(8,128)} %convolution_bitcast_fusion.1) | data formatting | bytes 14155776 | tf_op jit(solution)/shard_map/stack | solution.py:206
  308.3 11.5 %copy.85 = f32[1,3,9,128,512]{4,3,1,0,2:T(8,128)} copy(f32[1,3,9,128,512]{3,2,4,1,0:T(8,128)} %reshape.197) | data formatting | bytes 14155776 | tf_op jit(solution)/shard_map/stack | solution.py:206
  319.8 10.1 %reshape.198 = f32[1,3,9,128,512]{3,2,4,1,0:T(8,128)} reshape(f32[3,1152,2,256]{1,3,2,0:T(8,128)} %convolution_bitcast_fusion) | data formatting | bytes 14155776 | tf_op jit(solution)/shard_map/stack | solution.py:206
  330.0 11.7 %copy.86 = f32[1,3,9,128,512]{4,3,1,0,2:T(8,128)} copy(f32[1,3,9,128,512]{3,2,4,1,0:T(8,128)} %reshape.198) | data formatting | bytes 14155776 | tf_op jit(solution)/shard_map/stack | solution.py:206
  341.6 8.7 fusion.1
  369.4 15.2 %collective-permute-done.23 = bf16[2,3,128,512]{3,2,1,0:T(8,128)(2,1)S(1)} collective-permute-done((bf16[2,3,128,512]{3,2,1,0:T(8,128)(2,1)S(1)}, bf16[2,3,128,512]{3,2,1,0:T(8,128)(2,1)S(1)}, u32[]{:S(2)}, u32[]{:S(2)}) %collective-permute-start.23) | collective-permute-done | bytes 786464 | tf_op jit(solution)/shard_map/ppermute | solution.py:18
  394.6 30.9 %collective-permute-done.21 = bf16[2,3,128,512]{3,2,1,0:T(8,128)(2,1)S(1)} collective-permute-done((bf16[2,3,128,512]{3,2,1,0:T(8,128)(2,1)S(1)}, bf16[2,3,128,512]{3,2,1,0:T(8,128)(2,1)S(1)}, u32[]{:S(2)}, u32[]{:S(2)}) %collective-permute-start.21) | collective-permute-done | bytes 786464 | tf_op jit(solution)/shard_map/ppermute | solution.py:18
  425.7 28.5 %collective-permute-done.18 = bf16[2,3,128,512]{3,2,1,0:T(8,128)(2,1)S(1)} collective-permute-done((bf16[2,3,128,512]{3,2,1,0:T(8,128)(2,1)S(1)}, bf16[2,3,128,512]{3,2,1,0:T(8,128)(2,1)S(1)}, u32[]{:S(2)}, u32[]{:S(2)}) %collective-permute-start.18) | collective-permute-done | bytes 786464 | tf_op jit(solution)/shard_map/ppermute | solution.py:18
  526.4 12.6 %reduce-scatter.27.cloned.1.call-done = bf16[128,2560]{1,0:T(8,128)(2,1)} async-done(((bf16[512,2560]{1,0:T(8,128)(2,1)}), bf16[128,2560]{1,0:T(8,128)(2,1)}) %reduce-scatter.27.cloned.1.call-update) | async-done | bytes 655376
  541.3 33.8 %reduce-scatter.25.cloned.1.call-done = bf16[128,2560]{1,0:T(8,128)(2,1)} async-done(((bf16[512,2560]{1,0:T(8,128)(2,1)}), bf16[128,2560]{1,0:T(8,128)(2,1)}) %reduce-scatter.25.cloned.1.call-update) | async-done | bytes 655376
  577.4 55.3 %reduce-scatter.15.cloned.1.call-done = bf16[2560,256]{1,0:T(8,128)(2,1)} async-done(((bf16[2560,1024]{1,0:T(8,128)(2,1)}), bf16[2560,256]{1,0:T(8,128)(2,1)}) %reduce-scatter.15.cloned.1.call-update) | async-done | bytes 1310736 | tf_op jit(solution)/shard_map/reduce_scatter | solution.py:236
  643.4 46.9 %reduce-scatter.29.cloned.1.call-done = bf16[640,1024]{1,0:T(8,128)(2,1)} async-done(((bf16[2560,1024]{1,0:T(8,128)(2,1)}), bf16[640,1024]{1,0:T(8,128)(2,1)}) %reduce-scatter.29.cloned.1.call-update) | async-done | bytes 1310736
  701.3 63.0 %reduce-scatter.21.cloned.1.call-done = bf16[80,128]{1,0:T(8,128)(2,1)} async-done(((bf16[2560,128]{1,0:T(8,128)(2,1)}), bf16[80,128]{1,0:T(8,128)(2,1)}) %reduce-scatter.21.cloned.1.call-update) | async-done | bytes 20496 | tf_op jit(solution)/shard_map/reduce_scatter | solution.py:256
  765.7 74.1 %reduce-scatter.19.cloned.1.call-done = bf16[80,128]{1,0:T(8,128)(2,1)} async-done(((bf16[2560,128]{1,0:T(8,128)(2,1)}), bf16[80,128]{1,0:T(8,128)(2,1)}) %reduce-scatter.19.cloned.1.call-update) | async-done | bytes 20496 | tf_op jit(solution)/shard_map/reduce_scatter | solution.py:253
  841.1 80.2 %reduce-scatter.17.cloned.1.call-done = bf16[80,256]{1,0:T(8,128)(2,1)} async-done(((bf16[2560,256]{1,0:T(8,128)(2,1)}), bf16[80,256]{1,0:T(8,128)(2,1)}) %reduce-scatter.17.cloned.1.call-update) | async-done | bytes 40976 | tf_op jit(solution)/shard_map/reduce_scatter | solution.py:250
  922.7 79.7 %reduce-scatter.23.cloned.1.call-done = bf16[32,640]{1,0:T(8,128)(2,1)} async-done(((bf16[1024,640]{1,0:T(8,128)(2,1)}), bf16[32,640]{1,0:T(8,128)(2,1)}) %reduce-scatter.23.cloned.1.call-update) | async-done | bytes 40976 | tf_op jit(solution)/shard_map/reduce_scatter | solution.py:259
  (254 shorter events, 296.8 us)
Async XLA Ops:
  7.2 40.7 %all-gather.7.cloned.1.call-start = ((), (), s32[]{:S(2)}) async-start(), calls=%async_computation.9 | async-start | bytes 3276800 | tf_op jit(solution)/shard_map/all_gather | solution.py:140
  7.9 76.9 %all-gather.5.cloned.1.call-start = ((), (), s32[]{:S(2)}) async-start(), calls=%async_computation.8 | async-start | bytes 3276800 | tf_op jit(solution)/shard_map/all_gather | solution.py:139
  8.7 195.4 %all-gather.9.cloned.1.call-start = ((), (), s32[]{:S(2)}) async-start(), calls=%async_computation.10 | async-start | bytes 6553600 | tf_op jit(solution)/shard_map/all_gather | solution.py:138
  9.4 244.5 %all-gather.11.cloned.1.call-start = ((), (), s32[]{:S(2)}) async-start(), calls=%async_computation.11 | async-start | bytes 6553600 | tf_op jit(solution)/shard_map/all_gather | solution.py:141
  140.0 399.1 %reduce-scatter.27.cloned.1.call-start = ((), (), s32[]{:S(2)}) async-start(), calls=%async_computation.18 | async-start | bytes 3276800
  148.9 33.5 %collective-permute-start.4 = (bf16[2,3,128,512]{2,3,1,0:T(8,128)(2,1)}, bf16[2,3,128,512]{2,3,1,0:T(8,128)(2,1)}, u32[]{:S(2)}, u32[]{:S(2)}) collective-permute-start(bf16[2,3,128,512]{2,3,1,0:T(8,128)(2,1)} %collective-permute-done.3), channel_id=1, source_target_pairs={{0,1},{1,2},{2,3},{3,4},{4,5},{5,6},{6,7},{7,8},{8,9},{9,10},{10,1... | collective-permute-start | bytes 2359304 | tf_op jit(solution)/shard_map/ppermute | solution.py:18
  153.4 45.0 %collective-permute-start.15 = (s32[3,128]{1,0:T(4,128)S(1)}, s32[3,128]{1,0:T(4,128)S(1)}, u32[]{:S(2)}, u32[]{:S(2)}) collective-permute-start(s32[3,128]{1,0:T(4,128)S(1)} %copy-done.40), channel_id=1, source_target_pairs={{0,1},{1,2},{2,3},{3,4},{4,5},{5,6},{6,7},{7,8},{8,9},{9,10},{10,1... | collective-permute-start | bytes 4616 | tf_op jit(solution)/shard_map/ppermute | solution.py:18
  155.3 43.0 %collective-permute-start.14 = (s32[3,128]{1,0:T(4,128)S(1)}, s32[3,128]{1,0:T(4,128)S(1)}, u32[]{:S(2)}, u32[]{:S(2)}) collective-permute-start(s32[3,128]{1,0:T(4,128)S(1)} %copy-done.40), channel_id=1, source_target_pairs={{0,2},{1,3},{2,4},{3,5},{4,6},{5,7},{6,8},{7,9},{8,10},{9,11},{10,... | collective-permute-start | bytes 4616 | tf_op jit(solution)/shard_map/ppermute | solution.py:18
  158.4 39.9 %collective-permute-start.13 = (s32[3,128]{1,0:T(4,128)S(1)}, s32[3,128]{1,0:T(4,128)S(1)}, u32[]{:S(2)}, u32[]{:S(2)}) collective-permute-start(s32[3,128]{1,0:T(4,128)S(1)} %copy-done.40), channel_id=1, source_target_pairs={{0,3},{1,4},{2,5},{3,6},{4,7},{5,8},{6,9},{7,10},{8,11},{9,12},{10... | collective-permute-start | bytes 4616 | tf_op jit(solution)/shard_map/ppermute | solution.py:18
  198.4 19.1 %collective-permute-start.6 = (bf16[2,3,128,512]{2,3,1,0:T(8,128)(2,1)}, bf16[2,3,128,512]{2,3,1,0:T(8,128)(2,1)}, u32[]{:S(2)}, u32[]{:S(2)}) collective-permute-start(bf16[2,3,128,512]{2,3,1,0:T(8,128)(2,1)} %collective-permute-done.5), channel_id=1, source_target_pairs={{0,1},{1,2},{2,3},{3,4},{4,5},{5,6},{6,7},{7,8},{8,9},{9,10},{10,1... | collective-permute-start | bytes 2359304 | tf_op jit(solution)/shard_map/ppermute | solution.py:18
  355.8 28.8 %collective-permute-start.23 = (bf16[2,3,128,512]{3,2,1,0:T(8,128)(2,1)S(1)}, bf16[2,3,128,512]{3,2,1,0:T(8,128)(2,1)S(1)}, u32[]{:S(2)}, u32[]{:S(2)}) collective-permute-start(bf16[2,3,128,512]{3,2,1,0:T(8,128)(2,1)S(1)} %get-tuple-element.9), channel_id=1, source_target_pairs={{8,0},{9,1},{10,2},{11,3},{12,4},{13,5},{14,6},{15,7},{16,8},{17,9... | collective-permute-start | bytes 2359304 | tf_op jit(solution)/shard_map/ppermute | solution.py:18
  357.1 36.1 %collective-permute-start.22 = (bf16[2,3,128,512]{3,2,1,0:T(8,128)(2,1)S(1)}, bf16[2,3,128,512]{3,2,1,0:T(8,128)(2,1)S(1)}, u32[]{:S(2)}, u32[]{:S(2)}) collective-permute-start(bf16[2,3,128,512]{3,2,1,0:T(8,128)(2,1)S(1)} %get-tuple-element.10), channel_id=1, source_target_pairs={{7,0},{8,1},{9,2},{10,3},{11,4},{12,5},{13,6},{14,7},{15,8},{16,9}... | collective-permute-start | bytes 2359304 | tf_op jit(solution)/shard_map/ppermute | solution.py:18
  358.4 67.1 %collective-permute-start.21 = (bf16[2,3,128,512]{3,2,1,0:T(8,128)(2,1)S(1)}, bf16[2,3,128,512]{3,2,1,0:T(8,128)(2,1)S(1)}, u32[]{:S(2)}, u32[]{:S(2)}) collective-permute-start(bf16[2,3,128,512]{3,2,1,0:T(8,128)(2,1)S(1)} %get-tuple-element.11), channel_id=1, source_target_pairs={{6,0},{7,1},{8,2},{9,3},{10,4},{11,5},{12,6},{13,7},{14,8},{15,9},... | collective-permute-start | bytes 2359304 | tf_op jit(solution)/shard_map/ppermute | solution.py:18
  359.7 66.0 %collective-permute-start.20 = (bf16[2,3,128,512]{3,2,1,0:T(8,128)(2,1)S(1)}, bf16[2,3,128,512]{3,2,1,0:T(8,128)(2,1)S(1)}, u32[]{:S(2)}, u32[]{:S(2)}) collective-permute-start(bf16[2,3,128,512]{3,2,1,0:T(8,128)(2,1)S(1)} %get-tuple-element.12), channel_id=1, source_target_pairs={{5,0},{6,1},{7,2},{8,3},{9,4},{10,5},{11,6},{12,7},{13,8},{14,9},{... | collective-permute-start | bytes 2359304 | tf_op jit(solution)/shard_map/ppermute | solution.py:18
  368.1 57.6 %collective-permute-start.19 = (bf16[2,3,128,512]{3,2,1,0:T(8,128)(2,1)S(1)}, bf16[2,3,128,512]{3,2,1,0:T(8,128)(2,1)S(1)}, u32[]{:S(2)}, u32[]{:S(2)}) collective-permute-start(bf16[2,3,128,512]{3,2,1,0:T(8,128)(2,1)S(1)} %get-tuple-element.13), channel_id=1, source_target_pairs={{4,0},{5,1},{6,2},{7,3},{8,4},{9,5},{10,6},{11,7},{12,8},{13,9},{1... | collective-permute-start | bytes 2359304 | tf_op jit(solution)/shard_map/ppermute | solution.py:18
  384.5 69.7 %collective-permute-start.18 = (bf16[2,3,128,512]{3,2,1,0:T(8,128)(2,1)S(1)}, bf16[2,3,128,512]{3,2,1,0:T(8,128)(2,1)S(1)}, u32[]{:S(2)}, u32[]{:S(2)}) collective-permute-start(bf16[2,3,128,512]{3,2,1,0:T(8,128)(2,1)S(1)} %get-tuple-element.14), channel_id=1, source_target_pairs={{3,0},{4,1},{5,2},{6,3},{7,4},{8,5},{9,6},{10,7},{11,8},{12,9},{13... | collective-permute-start | bytes 2359304 | tf_op jit(solution)/shard_map/ppermute | solution.py:18
  393.2 61.1 %collective-permute-start.17 = (bf16[2,3,128,512]{3,2,1,0:T(8,128)(2,1)S(1)}, bf16[2,3,128,512]{3,2,1,0:T(8,128)(2,1)S(1)}, u32[]{:S(2)}, u32[]{:S(2)}) collective-permute-start(bf16[2,3,128,512]{3,2,1,0:T(8,128)(2,1)S(1)} %get-tuple-element.15), channel_id=1, source_target_pairs={{2,0},{3,1},{4,2},{5,3},{6,4},{7,5},{8,6},{9,7},{10,8},{11,9},{12,... | collective-permute-start | bytes 2359304 | tf_op jit(solution)/shard_map/ppermute | solution.py:18
  465.1 110.0 %reduce-scatter.25.cloned.1.call-start = ((), (), s32[]{:S(2)}) async-start(), calls=%async_computation.17 | async-start | bytes 3276800
  490.9 141.8 %reduce-scatter.15.cloned.1.call-start = ((), (), s32[]{:S(2)}) async-start(), calls=%async_computation.12 | async-start | bytes 6553600 | tf_op jit(solution)/shard_map/reduce_scatter | solution.py:236
  511.2 179.1 %reduce-scatter.29.cloned.1.call-start = ((), (), s32[]{:S(2)}) async-start(), calls=%async_computation.19 | async-start | bytes 6553600
  526.4 237.9 %reduce-scatter.21.cloned.1.call-start = ((), (), s32[]{:S(2)}) async-start(), calls=%async_computation.15 | async-start | bytes 675840 | tf_op jit(solution)/shard_map/reduce_scatter | solution.py:256
  541.3 298.4 %reduce-scatter.19.cloned.1.call-start = ((), (), s32[]{:S(2)}) async-start(), calls=%async_computation.14 | async-start | bytes 675840 | tf_op jit(solution)/shard_map/reduce_scatter | solution.py:253
  577.3 344.0 %reduce-scatter.17.cloned.1.call-start = ((), (), s32[]{:S(2)}) async-start(), calls=%async_computation.13 | async-start | bytes 1351680 | tf_op jit(solution)/shard_map/reduce_scatter | solution.py:250
  632.7 369.7 %reduce-scatter.23.cloned.1.call-start = ((), (), s32[]{:S(2)}) async-start(), calls=%async_computation.16 | async-start | bytes 1351680 | tf_op jit(solution)/shard_map/reduce_scatter | solution.py:259
  (56 other events, 982.5 us)
Sparse Core Ops, SparseCore 0:
  9.7 38.1 all-gather.6
  49.5 35.2 all-gather.4
  86.5 57.0 all-gather.8
  145.0 57.3 all-gather.10
  465.2 73.8 reduce-scatter.26
  541.4 33.7 reduce-scatter.24
  577.5 55.1 reduce-scatter.14
  635.1 55.1 reduce-scatter.28
  693.8 70.4 reduce-scatter.20
  767.7 71.9 reduce-scatter.18
  843.2 77.9 reduce-scatter.16
  924.6 77.6 reduce-scatter.22
where the time goes:
time: 1020 us; the launch traced here: 1010 us
  waiting for transfers between devices  651 us (64%)
  local copies, waits for them, and re-layouts  128 us (13%)
  matrix products  93.9 us (9%)
  starting transfers between devices  80.8 us (8%)
  other arithmetic  41.9 us (4%)
  between operations  15.6 us (2%)
    ppermute x24, waiting for transfers between devices, shifted(): return lax.ppermute(block, axis, route)  135 us
    unnamed x15, waiting for transfers between devices  95.5 us
    ppermute x24, starting transfers between devices, shifted(): return lax.ppermute(block, axis, route)  80.3 us
    reduce_scatter x1, waiting for transfers between devices, per_device(): lax.psum_scatter(part_query.astype(jnp.bfloat16), 'ctx', scatter_dimensio...  80.2 us
    reduce_scatter x1, waiting for transfers between devices, per_device(): lax.psum_scatter(part_output.astype(jnp.bfloat16), 'ctx', scatter_dimensi...  79.7 us
    reduce_scatter x1, waiting for transfers between devices, per_device(): lax.psum_scatter(part_key.astype(jnp.bfloat16), 'ctx', scatter_dimension=...  74.1 us
    reduce_scatter x1, waiting for transfers between devices, per_device(): lax.psum_scatter(part_value.astype(jnp.bfloat16), 'ctx', scatter_dimensio...  63 us
    reduce_scatter x1, waiting for transfers between devices, per_device(): lax.psum_scatter(query_term.astype(jnp.bfloat16), 'fsdp', scatter_dimensi...  55.3 us
  transfers between devices with their start and end apart: 36, of which 25 were waited for; matrix products, arithmetic and copies ran while one was open for 14% of the time, Pallas kernels for 0%

commit v1 on v0

v1 whole, which is shorter than its diff:
```python
import functools

import jax
import jax.numpy as jnp
from jax import lax
from jax.experimental import pallas as pl
from jax.experimental.pallas import tpu as pltpu
from jax.sharding import PartitionSpec as P

EPS = 1e-06
ROPE_BASE = 10000.0
Q_FACTOR = 0.0625
WINDOW = 1024
F32 = jnp.float32
BF16 = jnp.bfloat16
MESH = pl.DeviceIdType.MESH
VMEM_LIMIT = 64 * 1024 * 1024 - 512 * 1024

D = 2560
ROWS = 384
NOTE_ROWS = 16
UNIT = 2 * ROWS + NOTE_ROWS


def place():
    y = lax.axis_index("fsdp")
    c = lax.axis_index("ctx")
    j = lax.rem(c, 2)
    zx = lax.div(c, 2)
    return y, lax.div(zx, 4), lax.rem(zx, 4), j


def dev(y, z, x, j):
    return (y, (z * 4 + x) * 2 + j)


def up(a, n=1):
    return lax.rem(a + n, 4)


def remote(src, dst, ss, rs, device):
    return pltpu.make_async_remote_copy(
        src_ref=src, dst_ref=dst, send_sem=ss, recv_sem=rs, device_id=device, device_id_type=MESH
    )


def meet(devices):
    barrier = pltpu.get_barrier_semaphore()
    for device in devices:
        pl.semaphore_signal(barrier, inc=1, device_id=device, device_id_type=MESH)
    pl.semaphore_wait(barrier, len(devices))


def rows_at(start, size, unit=16):
    return pl.ds(pl.multiple_of(start, unit), size)


def vmem(n):
    return [pl.BlockSpec(memory_space=pltpu.VMEM)] * n


def comm_call(kernel, name, cid, out_shape, scratch, n_in):
    return pl.pallas_call(
        kernel,
        name=name,
        out_shape=out_shape,
        in_specs=vmem(n_in),
        out_specs=jax.tree.map(lambda _: pl.BlockSpec(memory_space=pltpu.VMEM), out_shape),
        scratch_shapes=scratch,
        compiler_params=pltpu.CompilerParams(
            collective_id=cid, has_side_effects=True, vmem_limit_bytes=VMEM_LIMIT
        ),
    )


def sds(shape, dtype):
    return jax.ShapeDtypeStruct(shape, dtype)


DMA = pltpu.SemaphoreType.DMA


class RingGather:
    def __init__(self, me, plus, minus, region, half, ss, rs, index):
        self.me, self.plus, self.minus = me, plus, minus
        self.region, self.half, self.ss, self.rs, self.index = region, half, ss, rs, index

    def _copy(self, ref, k, device):
        at = self.index + (k,)
        return remote(ref, ref, self.ss.at[at], self.rs.at[at], device)

    def start(self):
        self._copy(self.region(self.me), 0, self.plus).start()
        self._copy(self.region(self.me), 1, self.minus).start()

    def forward(self):
        left, right = up(self.me, 3), up(self.me, 1)
        self._copy(self.region(left), 0, self.plus).wait_recv()
        self._copy(self.half(left, 0), 2, self.plus).start()
        self._copy(self.region(right), 1, self.minus).wait_recv()
        self._copy(self.half(right, 1), 3, self.minus).start()

    def finish(self):
        far = up(self.me, 2)
        self._copy(self.half(far, 0), 2, self.plus).wait_recv()
        self._copy(self.half(far, 1), 3, self.minus).wait_recv()

    def drain(self):
        self._copy(self.region(self.me), 0, self.plus).wait_send()
        self._copy(self.region(self.me), 1, self.minus).wait_send()
        self._copy(self.half(up(self.me, 3), 0), 2, self.plus).wait_send()
        self._copy(self.half(up(self.me, 1), 1), 3, self.minus).wait_send()


def gather_kernel(n_ref, wq, wk, wv, n2, w, lsem, nsem, ysend, yrecv, gsend, grecv):
    y, z, x, j = place()
    partner = dev(y, z, x, 1 - j)
    xp, xm = dev(y, z, up(x), j), dev(y, z, up(x, 3), j)
    zp, zm = dev(y, up(z), x, j), dev(y, up(z, 3), x, j)
    ys = [dev(up(y, r), z, x, j) for r in (1, 2, 3)]
    own = rows_at(640 * y, 640)
    local = []
    for b in range(8):
        if b < 4:
            src = wq.at[:, pl.ds(pl.multiple_of(512 * j + 128 * b, 128), 128)]
        elif b < 6:
            src = wk.at[:, pl.ds(pl.multiple_of(256 * j + 128 * (b - 4), 128), 128)]
        else:
            src = wv.at[:, pl.ds(pl.multiple_of(256 * j + 128 * (b - 6), 128), 128)]
        local.append(pltpu.make_async_copy(src, w.at[b, own], lsem.at[b]))
    local.append(pltpu.make_async_copy(n_ref, n2.at[j], lsem.at[8]))
    for cp in local:
        cp.start()
    meet([partner, xp, xm, zp, zm] + ys)
    for cp in local[:8]:
        cp.wait()

    def piece_q(yy):
        return w.at[x, rows_at(640 * yy + 160 * z, 160)]

    def piece_k(yy):
        return w.at[4 + z, rows_at(640 * yy + 160 * x, 160)]

    first = []
    for r in range(3):
        for f, piece in enumerate((piece_q, piece_k)):
            cp = remote(piece(y), piece(y), ysend.at[f, r], yrecv.at[f, r], ys[r])
            cp.start()
            first.append((cp, f, r, piece))
    swap = remote(n_ref, n2.at[j], nsem.at[0], nsem.at[1], partner)
    swap.start()

    def ring(f, stage, r):
        yy = up(y, 3 - r)
        if f == 0 and stage == 0:
            region = lambda m: w.at[m, rows_at(640 * yy + 160 * z, 160)]
            half = lambda m, h: w.at[m, rows_at(640 * yy + 160 * z + 80 * h, 80)]
        elif f == 0:
            region = lambda m: w.at[pl.ds(0, 4), rows_at(640 * yy + 160 * m, 160)]
            half = lambda m, h: w.at[pl.ds(2 * h, 2), rows_at(640 * yy + 160 * m, 160)]
        elif stage == 0:
            region = lambda m: w.at[4 + m, rows_at(640 * yy + 160 * x, 160)]
            half = lambda m, h: w.at[4 + m, rows_at(640 * yy + 160 * x + 80 * h, 80)]
        else:
            region = lambda m: w.at[pl.ds(4, 4), rows_at(640 * yy + 160 * m, 160)]
            half = lambda m, h: w.at[pl.ds(4 + 2 * h, 2), rows_at(640 * yy + 160 * m, 160)]
        on_x = (f + stage) % 2 == 0
        me, plus, minus = (x, xp, xm) if on_x else (z, zp, zm)
        return RingGather(me, plus, minus, region, half, gsend, grecv, (f, stage, r))

    rings = [[[ring(f, s, r) for r in range(3)] for s in range(2)] for f in range(2)]
    for cp, f, r, piece in first:
        yy = up(y, 3 - r)
        remote(piece(yy), piece(yy), ysend.at[f, r], yrecv.at[f, r], ys[r]).wait_recv()
        rings[f][0][r].start()
    for r in range(3):
        for f in range(2):
            rings[f][0][r].forward()
    for r in range(3):
        for f in range(2):
            rings[f][0][r].finish()
            rings[f][1][r].start()
    for r in range(3):
        for f in range(2):
            rings[f][1][r].forward()
    for r in range(3):
        for f in range(2):
            rings[f][1][r].finish()
    for r in range(3):
        for f in range(2):
            rings[f][0][r].drain()
            rings[f][1][r].drain()
    for cp, f, r, piece in first:
        cp.wait_send()
    swap.wait()
    local[8].wait()


def gather(noted, wq, wk, wv):
    return comm_call(
        gather_kernel,
        "gather_weights",
        0,
        (sds((2, ROWS + NOTE_ROWS, D), BF16), sds((8, D, 128), BF16)),
        [
            DMA((9,)),
            DMA((2,)),
            DMA((2, 3)),
            DMA((2, 3)),
            DMA((2, 2, 3, 4)),
            DMA((2, 2, 3, 4)),
        ],
        4,
    )(noted, wq, wk, wv)


def project_kernel(n2, w, cos, sin, gains, q_out, unit, raw_out):
    n = pl.program_id(0)
    rows = n2[:, :ROWS, :].reshape(2 * ROWS, D)
    weight = jnp.concatenate([w[0], w[1]], axis=-1)
    acc = jnp.dot(rows, weight, preferred_element_type=F32)

    def rotated(gain, factor):
        scale = lax.rsqrt(jnp.mean(acc * acc, axis=-1, keepdims=True) + EPS)
        normed = acc * scale * gain
        a, b = normed[:, :128], normed[:, 128:]
        c, s = cos[...], sin[...]
        return (jnp.concatenate([a * c - b * s, b * c + a * s], axis=-1) * factor).astype(BF16)

    @pl.when(n < 3)
    def _():
        raw_out[0] = acc

    @pl.when(n < 2)
    def _():
        q_out[0] = rotated(gains[0:1, :], Q_FACTOR)

    @pl.when(n == 2)
    def _():
        unit[0 : 2 * ROWS, 0:256] = rotated(gains[1:2, :], 1.0)

    @pl.when(n == 3)
    def _():
        unit[0 : 2 * ROWS, 256:512] = acc.astype(BF16)
        unit[2 * ROWS : UNIT, :] = n2[0, ROWS:, 0:512] + n2[1, ROWS:, 0:512]


def project(n2, w, cos, sin, gains):
    return pl.pallas_call(
        project_kernel,
        name="project",
        grid=(4,),
        in_specs=[
            pl.BlockSpec((2, ROWS + NOTE_ROWS, D), lambda n: (0, 0, 0)),
            pl.BlockSpec((2, D, 128), lambda n: (n, 0, 0)),
            pl.BlockSpec((2 * ROWS, 128), lambda n: (0, 0)),
            pl.BlockSpec((2 * ROWS, 128), lambda n: (0, 0)),
            pl.BlockSpec((8, 256), lambda n: (0, 0)),
        ],
        out_specs=[
            pl.BlockSpec((1, 2 * ROWS, 256), lambda n: (jnp.minimum(n, 1), 0, 0)),
            pl.BlockSpec((UNIT, 512), lambda n: (0, 0)),
            pl.BlockSpec((1, 2 * ROWS, 256), lambda n: (jnp.minimum(n, 2), 0, 0)),
        ],
        out_shape=[
            sds((2, 2 * ROWS, 256), BF16),
            sds((UNIT, 512), BF16),
            sds((3, 2 * ROWS, 256), F32),
        ],
        compiler_params=pltpu.CompilerParams(vmem_limit_bytes=VMEM_LIMIT),
    )(n2, w, cos, sin, gains)


HALO_CHUNKS = 7
HALO_ROWS = UNIT // HALO_CHUNKS


def halo_kernel(unit, wo_own, w, halo, wo, wfull, hsend, hrecv, osend, orecv, lsem, wsem):
    y, z, x, j = place()
    partner = dev(y, z, x, 1 - j)
    xp, xm = dev(y, z, up(x), j), dev(y, z, up(x, 3), j)
    zp, zm = dev(y, up(z), x, j), dev(y, up(z, 3), x, j)
    yp, ym = dev(up(y), z, x, j), dev(up(y, 3), z, x, j)
    wcopy = pltpu.make_async_copy(w, wfull.at[j], lsem.at[0])
    ocopy = pltpu.make_async_copy(wo_own, wo.at[y], lsem.at[1])
    wcopy.start()
    ocopy.start()
    meet([partner, xp, xm, zp, zm, yp, ym])

    def rows(k):
        return rows_at(k * HALO_ROWS, HALO_ROWS)

    def shift(k):
        return remote(unit.at[rows(k)], halo.at[3, rows(k)], hsend.at[0, k], hrecv.at[0, k], zp)

    def right(src, k):
        return remote(src.at[rows(k)], halo.at[0, rows(k)], hsend.at[1, k], hrecv.at[1, k], xp)

    def left(src, k):
        return remote(src.at[rows(k)], halo.at[2, rows(k)], hsend.at[2, k], hrecv.at[2, k], xm)

    def far_right(k):
        return remote(
            halo.at[0, rows(k)], halo.at[1, rows(k)], hsend.at[3, k], hrecv.at[3, k], xp
        )

    def far_left(k):
        return remote(
            halo.at[2, rows(k)], halo.at[1, rows(k)], hsend.at[4, k], hrecv.at[3, k], xm
        )

    before = halo.at[3]
    inner = jnp.logical_and(x > 0, x < 3)

    @pl.loop(0, HALO_CHUNKS)
    def _(k):
        shift(k).start()

        @pl.when(x < 3)
        def _():
            right(unit, k).start()

        @pl.when(x == 0)
        def _():
            left(unit, k).start()

    ocopy.wait()
    ring = RingGather(
        y,
        yp,
        ym,
        lambda m: wo.at[m, j],
        lambda m, h: wo.at[m, j, pl.ds(64 * h, 64)],
        osend,
        orecv,
        (0,),
    )
    ring.start()
    swap = remote(w, wfull.at[j], wsem.at[0], wsem.at[1], partner)
    swap.start()

    @pl.loop(0, HALO_CHUNKS)
    def _(k):
        shift(k).wait_recv()

        @pl.when(x == 3)
        def _():
            right(before, k).start()

        @pl.when(x > 0)
        def _():
            left(before, k).start()

        right(unit, k).wait_recv()

        @pl.when(inner)
        def _():
            far_right(k).start()

        @pl.when(k > 0)
        def _():
            left(unit, k - 1).wait_recv()

            @pl.when(inner)
            def _():
                far_left(k - 1).start()

    left(unit, HALO_CHUNKS - 1).wait_recv()

    @pl.when(inner)
    def _():
        far_left(HALO_CHUNKS - 1).start()

    ring.forward()
    share = []
    for n, m in enumerate((up(y, 3), up(y, 1), up(y, 2))):
        if n == 2:
            ring.finish()
        cp = remote(
            wo.at[m, j], wo.at[m, j], osend.at[1, n], orecv.at[1, n], partner
        )
        cp.start()
        share.append(cp)
    for n, m in enumerate((up(y, 3), up(y, 1), up(y, 2))):
        remote(
            wo.at[m, 1 - j], wo.at[m, 1 - j], osend.at[1, n], orecv.at[1, n], partner
        ).wait_recv()
    for cp in share:
        cp.wait_send()
    ring.drain()

    @pl.loop(0, HALO_CHUNKS)
    def _(k):
        far_right(k).wait_recv()
        shift(k).wait_send()
        right(unit, k).wait_send()
        left(unit, k).wait_send()

        @pl.when(inner)
        def _():
            far_right(k).wait_send()
            far_left(k).wait_send()

    swap.wait()
    wcopy.wait()


def exchange_halo(unit, wo_own, w):
    return comm_call(
        halo_kernel,
        "exchange_halo",
        1,
        (
            sds((4, UNIT, 512), BF16),
            sds((4, 2, 128, D), BF16),
            sds((2, 8, D, 128), BF16),
        ),
        [
            DMA((5, HALO_CHUNKS)),
            DMA((4, HALO_CHUNKS)),
            DMA((2, 4)),
            DMA((2, 4)),
            DMA((2,)),
            DMA((2,)),
        ],
        3,
    )(unit, wo_own, w)


KEYS = 1280


def window_of(unit, halo, s, first, last):
    parts = []
    for d in (4, 3, 2, 1, 0):
        for i in range(2):
            at = rows_at(i * ROWS + s * 128, 128)
            if d == 0:
                parts.append(unit[at, first:last])
            else:
                parts.append(halo[d - 1, at, first:last])
    return jnp.concatenate(parts, axis=0)


def forward_kernel(q, unit, halo, base, attended, soft):
    s = pl.program_id(0)
    keys = window_of(unit, halo, s, 0, 256)
    values = window_of(unit, halo, s, 256, 512)
    lanes = pl.ds(pl.multiple_of(s * 128, 128), 128)
    notes = []
    for d in (4, 3, 2, 1, 0):
        block = unit[2 * ROWS :, lanes] if d == 0 else halo[d - 1, 2 * ROWS :, lanes]
        block = block.astype(F32)
        notes.extend([block[0:1], block[8:9]])
    key_docs = jnp.concatenate(notes, axis=-1)
    query_docs = jnp.concatenate(
        [jnp.transpose(jnp.broadcast_to(note, (128, 128))) for note in notes[8:]], axis=0
    )
    query_docs = jnp.concatenate([query_docs] * (KEYS // 128), axis=-1)
    key_at = lax.broadcasted_iota(jnp.int32, (256, KEYS), 1) - WINDOW
    query_at = lax.broadcasted_iota(jnp.int32, (256, KEYS), 0)
    start = base[0]
    allowed = (
        (query_docs == key_docs)
        & (key_at <= query_at)
        & (key_at > query_at - WINDOW)
        & (key_at + start >= 0)
    )
    bias = jnp.where(allowed, 0.0, -1e30)
    for h in range(2):
        rows = q[h, :, 0].reshape(256, 256)
        scores = lax.dot_general(
            rows, keys, (((1,), (1,)), ((), ())), preferred_element_type=F32
        )
        masked = jnp.where(bias < 0.0, -1e30, scores)
        highest = jnp.max(masked, axis=-1, keepdims=True)
        raised = jnp.exp(masked - highest)
        weights = (raised / jnp.sum(raised, axis=-1, keepdims=True)).astype(BF16)
        soft[0, 256 * h : 256 * h + 256, :] = weights
        out = jnp.dot(weights, values, preferred_element_type=F32).astype(BF16)
        attended[:, 0, :, 256 * h : 256 * h + 256] = out.reshape(2, 128, 256)


def attend_forward(q, unit, halo, base):
    return pl.pallas_call(
        forward_kernel,
        name="attend_forward",
        grid=(3,),
        in_specs=[
            pl.BlockSpec((2, 2, 1, 128, 256), lambda s: (0, 0, s, 0, 0)),
            pl.BlockSpec((UNIT, 512), lambda s: (0, 0)),
            pl.BlockSpec((4, UNIT, 512), lambda s: (0, 0, 0)),
            pl.BlockSpec(memory_space=pltpu.SMEM),
        ],
        out_specs=[
            pl.BlockSpec((2, 1, 128, 512), lambda s: (0, s, 0, 0)),
            pl.BlockSpec((1, 512, KEYS), lambda s: (s, 0, 0)),
        ],
        out_shape=[sds((2, 3, 128, 512), BF16), sds((3, 512, KEYS), BF16)],
        compiler_params=pltpu.CompilerParams(vmem_limit_bytes=VMEM_LIMIT),
    )(q.reshape(2, 2, 3, 128, 256), unit, halo, base)


def backward_kernel(q, unit, halo, soft, grad, raw, cos, sin, gains, delta_out, own, parts):
    s = pl.program_id(0)
    keys = window_of(unit, halo, s, 0, 256)
    values = window_of(unit, halo, s, 256, 512)
    grads = jnp.concatenate(
        [grad[:, 0, :, 256 * h : 256 * h + 256].reshape(256, 256) for h in range(2)], axis=0
    )
    weights = soft[0]
    value_part = lax.dot_general(
        weights, grads, (((0,), (0,)), ((), ())), preferred_element_type=F32
    )

    def emit(part, first):
        for n, d in enumerate((4, 3, 2, 1, 0)):
            for i in range(2):
                piece = part[256 * n + 128 * i : 256 * n + 128 * i + 128]
                if d == 0:
                    own[i, 0, :, first : first + 256] = piece
                else:
                    parts[d - 1, i, 0, :, first : first + 256] = piece.astype(BF16)

    emit(value_part, 256)
    grad_weights = lax.dot_general(
        grads, values, (((1,), (1,)), ((), ())), preferred_element_type=F32
    )
    wide = weights.astype(F32)
    moved = wide * grad_weights
    dots = jnp.sum(moved, axis=-1, keepdims=True)
    score_grads = (moved - wide * dots).astype(BF16)
    grad_queries = jnp.dot(score_grads, keys, preferred_element_type=F32)
    queries = q[:, :, 0].reshape(512, 256)
    emit(
        lax.dot_general(
            score_grads, queries, (((0,), (0,)), ((), ())), preferred_element_type=F32
        ),
        0,
    )
    gain = gains[0:1, :]
    c = cos[:, 0].reshape(256, 128)
    sn = sin[:, 0].reshape(256, 128)
    for h in range(2):
        back = map_back(
            grad_queries[256 * h : 256 * h + 256],
            raw[h, :, 0].reshape(256, 256),
            c,
            sn,
            gain,
            Q_FACTOR,
        )
        delta_out[:, 0, :, 256 * h : 256 * h + 256] = back.astype(BF16).reshape(2, 128, 256)


def map_back(upstream, raw, c, s, gain, factor):
    a, b = upstream[:, :128] * factor, upstream[:, 128:] * factor
    turned = jnp.concatenate([a * c + b * s, b * c - a * s], axis=-1) * gain
    scale = lax.rsqrt(jnp.mean(raw * raw, axis=-1, keepdims=True) + EPS)
    inner = jnp.mean(turned * raw, axis=-1, keepdims=True)
    return scale * turned - raw * (scale * scale * scale * inner)


def attend_backward(q, unit, halo, soft, grad, raw, cos, sin, gains):
    row_block = pl.BlockSpec((2, 1, 128, 512), lambda s: (0, s, 0, 0))
    angle = pl.BlockSpec((2, 1, 128, 128), lambda s: (0, s, 0, 0))
    head_block = pl.BlockSpec((2, 2, 1, 128, 256), lambda s: (0, 0, s, 0, 0))
    return pl.pallas_call(
        backward_kernel,
        name="attend_backward",
        grid=(3,),
        in_specs=[
            head_block,
            pl.BlockSpec((UNIT, 512), lambda s: (0, 0)),
            pl.BlockSpec((4, UNIT, 512), lambda s: (0, 0, 0)),
            pl.BlockSpec((1, 512, KEYS), lambda s: (s, 0, 0)),
            row_block,
            head_block,
            angle,
            angle,
            pl.BlockSpec((8, 256), lambda s: (0, 0)),
        ],
        out_specs=[
            row_block,
            row_block,
            pl.BlockSpec((4, 2, 1, 128, 512), lambda s: (0, 0, s, 0, 0)),
        ],
        out_shape=[
            sds((2, 3, 128, 512), BF16),
            sds((2, 3, 128, 512), F32),
            sds((4, 2, 3, 128, 512), BF16),
        ],
        compiler_params=pltpu.CompilerParams(vmem_limit_bytes=VMEM_LIMIT),
    )(
        q.reshape(2, 2, 3, 128, 256),
        unit,
        halo,
        soft,
        grad.reshape(2, 3, 128, 512),
        raw.reshape(3, 2, 3, 128, 256),
        cos.reshape(2, 3, 128, 128),
        sin.reshape(2, 3, 128, 128),
        gains,
    )


def swap_kernel(count, *refs):
    halves = refs[:1]
    whole = refs[1:count]
    outs = refs[count : 2 * count]
    lsem, ssem, rsem = refs[2 * count :]
    y, z, x, j = place()
    partner = dev(y, z, x, 1 - j)
    local = []
    for n in range(count):
        src = halves[0].at[j] if n < 1 else whole[n - 1]
        cp = pltpu.make_async_copy(src, outs[n].at[j], lsem.at[n])
        cp.start()
        local.append(cp)
    meet([partner])
    sent = []
    for n in range(count):
        src = halves[0].at[1 - j] if n < 1 else whole[n - 1]
        cp = remote(src, outs[n].at[j], ssem.at[n], rsem.at[n], partner)
        cp.start()
        sent.append(cp)
    for cp in local:
        cp.wait()
    for cp in sent:
        cp.wait()


def swap(name, cid, halves, *whole):
    count = 1 + len(whole)
    shapes = [sds(halves.shape, halves.dtype)] + [sds((2,) + w.shape, w.dtype) for w in whole]
    return comm_call(
        functools.partial(swap_kernel, count),
        name,
        cid,
        shapes,
        [DMA((count,)), DMA((count,)), DMA((count,))],
        count,
    )(halves, *whole)


def output_kernel(att, wo, tok, cot, gain, layer_out, gp, ga, proj, up_buf):
    left, right = att[0], att[1]
    for n in range(5):
        cols = slice(512 * n, 512 * n + 512)
        proj[:, cols] = jnp.dot(left, wo[0:512, cols], preferred_element_type=F32) + jnp.dot(
            right, wo[512:1024, cols], preferred_element_type=F32
        )

    @pl.loop(0, ROWS // 16)
    def _(k):
        at = rows_at(k * 16, 16)
        p = proj[at, :]
        g = gain[...]
        scale = lax.rsqrt(jnp.mean(p * p, axis=-1, keepdims=True) + EPS)
        layer_out[at, :] = (tok[at, :].astype(F32) + p * scale * g).astype(BF16)
        h = cot[at, :].astype(F32) * g
        inner = jnp.mean(h * p, axis=-1, keepdims=True)
        gp[at, :] = (scale * h - p * (scale * scale * scale * inner)).astype(BF16)

    upstream = gp[...]
    for half in range(2):
        ga[half] = lax.dot_general(
            upstream,
            wo[512 * half : 512 * half + 512, :],
            (((1,), (1,)), ((), ())),
            preferred_element_type=F32,
        ).astype(BF16)


def output_stage(att, wo, tok, cot, gain):
    return pl.pallas_call(
        output_kernel,
        name="output_stage",
        in_specs=vmem(5),
        out_specs=vmem(3),
        out_shape=[sds((ROWS, D), BF16), sds((ROWS, D), BF16), sds((2, ROWS, 512), BF16)],
        scratch_shapes=[pltpu.VMEM((ROWS, D), F32), pltpu.VMEM((8, 128), F32)],
        compiler_params=pltpu.CompilerParams(vmem_limit_bytes=VMEM_LIMIT),
    )(att, wo, tok, cot, gain)


CHUNKS = 6


def return_kernel(parts, own, total, relay, near, after, relayed, summed, bsum, ssem, rsem):
    y, z, x, j = place()
    xp, xm = dev(y, z, up(x), j), dev(y, z, up(x, 3), j)
    zp, zm = dev(y, up(z), x, j), dev(y, up(z, 3), x, j)
    meet([xp, xm, zp, zm])
    inner = jnp.logical_and(x > 0, x < 3)
    low = x < 2

    def relay_left(k):
        return remote(parts.at[1, k], relay.at[0, k], ssem.at[0, k], rsem.at[0, k], xm)

    def relay_right(k):
        return remote(parts.at[1, k], relay.at[1, k], ssem.at[1, k], rsem.at[1, k], xp)

    def to_left(src, k):
        return remote(src.at[k], near.at[0, k], ssem.at[2, k], rsem.at[2, k], xm)

    def to_right(src, k):
        return remote(src.at[k], near.at[1, k], ssem.at[3, k], rsem.at[3, k], xp)

    def back(k):
        return remote(bsum.at[k], after.at[k], ssem.at[4, k], rsem.at[4, k], zm)

    @pl.loop(0, CHUNKS)
    def _(k):
        @pl.when(low)
        def _():
            relay_right(k).start()

        @pl.when(jnp.logical_not(low))
        def _():
            relay_left(k).start()

        @pl.when(jnp.logical_not(inner))
        def _():
            to_left(parts.at[0], k).start()
            to_right(parts.at[2], k).start()

    @pl.when(inner)
    def _():
        @pl.loop(0, CHUNKS)
        def _(k):
            relay_left(k).wait_recv()
            relayed[0, k] = (parts[0, k].astype(F32) + relay[0, k].astype(F32)).astype(BF16)
            to_left(relayed.at[0], k).start()
            relay_right(k).wait_recv()
            relayed[1, k] = (parts[2, k].astype(F32) + relay[1, k].astype(F32)).astype(BF16)
            to_right(relayed.at[1], k).start()

    @pl.loop(0, CHUNKS)
    def _(k):
        to_left(parts.at[0], k).wait_recv()
        to_right(parts.at[2], k).wait_recv()
        from_right = near[0, k].astype(F32)
        from_left = near[1, k].astype(F32)
        zero = jnp.zeros_like(from_left)
        near_a = jnp.where(x < 3, from_right, zero) + jnp.where(x == 0, from_left, zero)
        near_b = jnp.where(x == 3, from_right, zero) + jnp.where(x > 0, from_left, zero)
        summed[k] = near_a
        bsum[k] = (parts[3, k].astype(F32) + near_b).astype(BF16)
        back(k).start()

    @pl.loop(0, CHUNKS)
    def _(k):
        back(k).wait_recv()
        total[k] = own[k] + summed[k] + after[k].astype(F32)

    @pl.loop(0, CHUNKS)
    def _(k):
        @pl.when(low)
        def _():
            relay_right(k).wait_send()

        @pl.when(jnp.logical_not(low))
        def _():
            relay_left(k).wait_send()

        to_left(parts.at[0], k).wait_send()
        to_right(parts.at[2], k).wait_send()
        back(k).wait_send()


def return_grads(parts, own):
    block = (CHUNKS, 128, 512)
    return comm_call(
        return_kernel,
        "return_grads",
        2,
        sds(block, F32),
        [
            pltpu.VMEM((2,) + block, BF16),
            pltpu.VMEM((2,) + block, BF16),
            pltpu.VMEM(block, BF16),
            pltpu.VMEM((2,) + block, BF16),
            pltpu.VMEM(block, F32),
            pltpu.VMEM(block, BF16),
            DMA((5, CHUNKS)),
            DMA((5, CHUNKS)),
        ],
        2,
    )(parts.reshape((4,) + block), own.reshape(block))


def in_grads_kernel(n2, total, raw, cos, sin, gains, qd, gq, gkv, kvd):
    @pl.when(pl.program_id(0) == 0)
    def _():
        kd = map_back(total[:, :256], raw[0], cos[...], sin[...], gains[1:2, :], 1.0)
        kvd[:, :256] = kd.astype(BF16)
        kvd[:, 256:] = total[:, 256:].astype(BF16)

    rows = n2[:, :ROWS, :].reshape(2 * ROWS, 640)
    for half in range(2):
        rhs_q = qd[:, 256 * half : 256 * half + 256]
        rhs_kv = jnp.concatenate(
            [kvd[:, 128 * half : 128 * half + 128], kvd[:, 256 + 128 * half : 384 + 128 * half]],
            axis=-1,
        )
        for rhs, out in ((rhs_q, gq), (rhs_kv, gkv)):
            term = lax.dot_general(
                rows, rhs, (((0,), (0,)), ((), ())), preferred_element_type=F32
            )
            out[half, 0] = term.astype(BF16).reshape(4, 160, 256)


def in_grads(n2, total, raw, cos, sin, gains, qd):
    grads = pl.BlockSpec((2, 1, 4, 160, 256), lambda n: (0, n, 0, 0, 0))
    return pl.pallas_call(
        in_grads_kernel,
        name="in_grads",
        grid=(4,),
        in_specs=[
            pl.BlockSpec((2, ROWS + NOTE_ROWS, 640), lambda n: (0, 0, n)),
            pl.BlockSpec((2 * ROWS, 512), lambda n: (0, 0)),
            pl.BlockSpec((1, 2 * ROWS, 256), lambda n: (2, 0, 0)),
            pl.BlockSpec((2 * ROWS, 128), lambda n: (0, 0)),
            pl.BlockSpec((2 * ROWS, 128), lambda n: (0, 0)),
            pl.BlockSpec((8, 256), lambda n: (0, 0)),
            pl.BlockSpec((2 * ROWS, 512), lambda n: (0, 0)),
        ],
        out_specs=[grads, grads, pl.BlockSpec((2 * ROWS, 512), lambda n: (0, 0))],
        out_shape=[
            sds((2, 4, 4, 160, 256), BF16),
            sds((2, 4, 4, 160, 256), BF16),
            sds((2 * ROWS, 512), BF16),
        ],
        compiler_params=pltpu.CompilerParams(vmem_limit_bytes=VMEM_LIMIT),
    )(n2, total, raw, cos, sin, gains, qd)


def out_grads_kernel(att, gp2, out):
    term = lax.dot_general(
        att[...],
        gp2[...].reshape(2 * ROWS, 640),
        (((0,), (0,)), ((), ())),
        preferred_element_type=F32,
    )
    out[0] = term.astype(BF16).reshape(2, 4, 64, 640)


def out_grads(att, gp2):
    return pl.pallas_call(
        out_grads_kernel,
        name="out_grads",
        grid=(4,),
        in_specs=[
            pl.BlockSpec((2 * ROWS, 512), lambda n: (0, 0)),
            pl.BlockSpec((2, ROWS, 640), lambda n: (0, 0, n)),
        ],
        out_specs=pl.BlockSpec((1, 2, 4, 64, 640), lambda n: (n, 0, 0, 0, 0)),
        out_shape=sds((4, 2, 4, 64, 640), BF16),
        compiler_params=pltpu.CompilerParams(vmem_limit_bytes=VMEM_LIMIT),
    )(att, gp2)


def input_kernel(dq, dkv, w, tok, cot, gain, out, acc):
    n = pl.program_id(0)
    total = None
    for half in range(2):
        lhs = jnp.concatenate([dq[half], dkv[half]], axis=-1)
        rhs = jnp.concatenate([w[half, b] for b in range(8)], axis=-1)
        term = lax.dot_general(lhs, rhs, (((1,), (1,)), ((), ())), preferred_element_type=F32)
        total = term if total is None else total + term
    acc[n] = total

    @pl.when(n == pl.num_programs(0) - 1)
    def _():
        @pl.loop(0, ROWS // 16)
        def _(k):
            at = rows_at(k * 16, 16)
            t = tok[at, :].astype(F32)
            grad = jnp.concatenate([acc[m, at, :] for m in range(5)], axis=-1)
            h = grad * gain[...]
            scale = lax.rsqrt(jnp.mean(t * t, axis=-1, keepdims=True) + EPS)
            inner = jnp.mean(h * t, axis=-1, keepdims=True)
            back = scale * h - t * (scale * scale * scale * inner)
            out[at, :] = (cot[at, :].astype(F32) + back).astype(BF16)


def input_stage(dq, dkv, wfull, tok, cot, gain):
    return pl.pallas_call(
        input_kernel,
        name="input_stage",
        grid=(5,),
        in_specs=[
            pl.BlockSpec((2, ROWS, 512), lambda n: (0, 0, 0)),
            pl.BlockSpec((2, ROWS, 512), lambda n: (0, 0, 0)),
            pl.BlockSpec((2, 8, 512, 128), lambda n: (0, 0, n, 0)),
            pl.BlockSpec((ROWS, D), lambda n: (0, 0)),
            pl.BlockSpec((ROWS, D), lambda n: (0, 0)),
            pl.BlockSpec((1, D), lambda n: (0, 0)),
        ],
        out_specs=pl.BlockSpec((ROWS, D), lambda n: (0, 0)),
        out_shape=sds((ROWS, D), BF16),
        scratch_shapes=[pltpu.VMEM((5, ROWS, 512), F32)],
        compiler_params=pltpu.CompilerParams(vmem_limit_bytes=VMEM_LIMIT),
    )(dq, dkv, wfull, tok, cot, gain)


def add_into(ref, at, other):
    ref[at] = (ref[at].astype(F32) + other.astype(F32)).astype(BF16)


class RingReduce:
    def __init__(self, me, plus, minus, data, pick, half, relay, recv, ss, rs, index):
        self.me, self.plus, self.minus = me, plus, minus
        self.data, self.pick, self.half = data, pick, half
        self.relay, self.recv, self.ss, self.rs, self.index = relay, recv, ss, rs, index

    def _copy(self, src, dst, k, device):
        at = self.index + (k,)
        return remote(src, dst, self.ss.at[at], self.rs.at[at], device)

    def _first(self):
        far = up(self.me, 2)
        return (
            self._copy(self.data.at[self.half(far, 0)], self.relay.at[0], 0, self.plus),
            self._copy(self.data.at[self.half(far, 1)], self.relay.at[1], 1, self.minus),
        )

    def _second(self):
        right, left = up(self.me, 1), up(self.me, 3)
        return (
            self._copy(self.data.at[self.pick(right)], self.recv.at[0], 2, self.plus),
            self._copy(self.data.at[self.pick(left)], self.recv.at[1], 3, self.minus),
        )

    def start(self):
        for cp in self._first():
            cp.start()

    def forward(self):
        a, b = self._first()
        c, d = self._second()
        a.wait_recv()
        add_into(self.data, self.half(up(self.me, 1), 0), self.relay[0])
        c.start()
        b.wait_recv()
        add_into(self.data, self.half(up(self.me, 3), 1), self.relay[1])
        d.start()

    def finish(self):
        c, d = self._second()
        c.wait_recv()
        d.wait_recv()
        return (
            self.data[self.pick(self.me)].astype(F32)
            + self.recv[0].astype(F32)
            + self.recv[1].astype(F32)
        )

    def drain(self):
        for cp in self._first() + self._second():
            cp.wait_send()


def reduce_kernel(
    gq, gkv, go, oq, okv, oo,
    q_relay, q_recv, q_mid, q_relay2, q_recv2, q_end, q_land,
    k_relay, k_recv, k_mid, k_relay2, k_recv2, k_end, k_land,
    o_relay, o_recv, o_mid, o_relay2, o_recv2, o_end, o_land,
    ss, rs, ls, lr, lc,
):
    y, z, x, j = place()
    partner = dev(y, z, x, 1 - j)
    xp, xm = dev(y, z, up(x), j), dev(y, z, up(x, 3), j)
    zp, zm = dev(y, up(z), x, j), dev(y, up(z, 3), x, j)
    yp, ym = dev(up(y), z, x, j), dev(up(y, 3), z, x, j)
    yfar = [dev(up(y, r), z, x, i) for r in (1, 2, 3) for i in (0, 1)]
    zfar = [dev(y, up(z, r), x, i) for r in (1, 2, 3) for i in (0, 1)]
    meet([partner, xp, xm] + yfar + zfar)
    every = slice(None)
    q1 = RingReduce(
        x, xp, xm, gq, lambda m: (every, every, m), lambda m, h: (h, every, m),
        q_relay, q_recv, ss, rs, (0, 0),
    )
    k1 = RingReduce(
        z, zp, zm, gkv, lambda m: (every, m), lambda m, h: (h, m),
        k_relay, k_recv, ss, rs, (1, 0),
    )
    o1 = RingReduce(
        y, yp, ym, go, lambda m: (m,), lambda m, h: (m, h),
        o_relay, o_recv, ss, rs, (2, 0),
    )
    q2 = RingReduce(
        z, zp, zm, q_mid, lambda m: (every, m), lambda m, h: (h, m),
        q_relay2, q_recv2, ss, rs, (0, 1),
    )
    k2 = RingReduce(
        x, xp, xm, k_mid, lambda m: (every, m), lambda m, h: (h, m),
        k_relay2, k_recv2, ss, rs, (1, 1),
    )
    o2 = RingReduce(
        x, xp, xm, o_mid, lambda m: (every, m), lambda m, h: (h, m),
        o_relay2, o_recv2, ss, rs, (2, 1),
    )
    firsts, seconds = (o1, k1, q1), (o2, k2, q2)
    mids, ends = (o_mid, k_mid, q_mid), (o_end, k_end, q_end)
    for ring in firsts:
        ring.start()
    for ring in firsts:
        ring.forward()
    for ring, mid, after in zip(firsts, mids, seconds):
        mid[...] = ring.finish().astype(BF16)
        after.start()
    for ring in seconds:
        ring.forward()
    for ring, end in zip(seconds, ends):
        end[...] = ring.finish().astype(BF16)

    def last(f, end, land, rows, at_y, send):
        me = y if at_y else z
        for h in range(2):
            goal = 2 * j + h
            for i in range(2):
                here = jnp.logical_and(goal == me, i == j)
                device = dev(goal, z, x, i) if at_y else dev(y, goal, x, i)
                src = end.at[h, pl.ds(rows * i, rows)]
                n = 2 * h + i

                @pl.when(here)
                def _():
                    cp = pltpu.make_async_copy(src, land.at[me], lc.at[f])
                    if send == 0:
                        cp.start()
                    else:
                        cp.wait()

                @pl.when(jnp.logical_not(here))
                def _():
                    cp = remote(src, land.at[me], ls.at[f, n], lr.at[f, me], device)
                    if send == 0:
                        cp.start()
                    else:
                        cp.wait_send()

    def landed(f, end, land, rows, at_y, out):
        me = y if at_y else z
        mine = lax.div(me, 2) == j
        for m in range(4):
            here = jnp.logical_and(m == me, mine)

            @pl.when(jnp.logical_not(here))
            def _():
                remote(
                    end.at[0, pl.ds(0, rows)], land.at[m], ls.at[f, 0], lr.at[f, m], partner
                ).wait_recv()

        out[...] = (land[0].astype(F32) + land[1].astype(F32)) + (
            land[2].astype(F32) + land[3].astype(F32)
        )

    flows = (
        (0, q_end, q_land, 80, True, oq),
        (1, k_end, k_land, 80, True, okv),
        (2, o_end, o_land, 32, False, oo),
    )
    for f, end, land, rows, at_y, out in flows:
        last(f, end, land, rows, at_y, 0)
    for f, end, land, rows, at_y, out in flows:
        last(f, end, land, rows, at_y, 1)
    for flow in flows:
        landed(*flow)
    for ring in firsts + seconds:
        ring.drain()


def reduce_grads(gq, gkv, go):
    def buffers(half1, whole1, mid, half2, whole2, end, land):
        return [
            pltpu.VMEM((2,) + half1, BF16),
            pltpu.VMEM((2,) + whole1, BF16),
            pltpu.VMEM(mid, BF16),
            pltpu.VMEM((2,) + half2, BF16),
            pltpu.VMEM((2,) + whole2, BF16),
            pltpu.VMEM(end, BF16),
            pltpu.VMEM((4,) + land, BF16),
        ]

    wide = buffers(
        (4, 160, 256), (2, 4, 160, 256), (2, 4, 160, 256),
        (160, 256), (2, 160, 256), (2, 160, 256), (80, 256),
    )
    tall = buffers(
        (4, 64, 640), (2, 4, 64, 640), (2, 4, 64, 640),
        (64, 640), (2, 64, 640), (2, 64, 640), (32, 640),
    )
    return comm_call(
        reduce_kernel,
        "reduce_grads",
        3,
        (sds((80, 256), F32), sds((80, 256), F32), sds((32, 640), F32)),
        wide
        + wide
        + tall
        + [DMA((3, 2, 4)), DMA((3, 2, 4)), DMA((3, 4)), DMA((3, 4)), DMA((3,))],
        3,
    )(gq, gkv, go)


def per_device(
    tokens,
    doc_ids,
    cotangent,
    input_gain,
    query_weight,
    key_weight,
    value_weight,
    output_weight,
    query_gain,
    key_gain,
    post_gain,
):
    seq_count, shard_size, width = tokens.shape
    c = lax.axis_index("ctx")
    core = lax.rem(c, 2)
    tok = tokens.reshape(ROWS, D)
    cot = cotangent.reshape(ROWS, D)
    wide = tok.astype(F32)
    scale = lax.rsqrt(jnp.mean(wide * wide, axis=-1, keepdims=True) + EPS)
    normed = (wide * scale * input_gain).astype(BF16)
    line = jnp.pad(doc_ids.reshape(1, ROWS).astype(BF16), ((0, 0), (0, D - ROWS)))
    at = lax.broadcasted_iota(jnp.int32, (NOTE_ROWS, 1), 0)
    notes = jnp.where(at == 8 * core, line, jnp.zeros((), BF16))
    noted = jnp.concatenate([normed, notes], axis=0)

    start = lax.div(c, 2) * 256
    positions = (start + jnp.arange(256, dtype=jnp.int32)).astype(F32)
    exponents = jnp.arange(128, dtype=jnp.int32).astype(F32) * (2.0 / 256)
    angles = positions[:, None] * ROPE_BASE ** (-exponents)

    def table(values):
        values = values.reshape(2, 1, 128, 128)
        return jnp.broadcast_to(values, (2, 3, 128, 128)).reshape(2 * ROWS, 128)

    cos, sin = table(jnp.cos(angles)), table(jnp.sin(angles))
    gains = jnp.pad(jnp.stack([query_gain, key_gain]), ((0, 6), (0, 0)))
    base = start.reshape(1).astype(jnp.int32)

    n2, w = gather(noted, query_weight, key_weight, value_weight)
    q, unit, raw = project(n2, w, cos, sin, gains)
    halo, wo, wfull = exchange_halo(
        unit, output_weight.reshape(2, 128, D), w
    )
    attended, soft = attend_forward(q, unit, halo, base)
    attended = attended.reshape(2, ROWS, 512)
    (att,) = swap("swap_attended", 4, attended)
    layer_out, gp, ga = output_stage(
        att, wo.reshape(1024, D), tok, cot, post_gain.reshape(1, D)
    )
    grad, gp2 = swap("swap_grads", 5, ga, gp)
    qd, own, parts = attend_backward(q, unit, halo, soft, grad, raw, cos, sin, gains)
    total = return_grads(parts, own)
    go = out_grads(attended.reshape(2 * ROWS, 512), gp2)
    gq, gkv, kvd = in_grads(
        n2, total.reshape(2 * ROWS, 512), raw, cos, sin, gains, qd.reshape(2 * ROWS, 512)
    )
    (dq,) = swap("swap_query_deltas", 6, qd.reshape(2, ROWS, 512))
    (dkv,) = swap("swap_key_deltas", 7, kvd.reshape(2, ROWS, 512))
    tokens_grad = input_stage(dq, dkv, wfull, tok, cot, input_gain.reshape(1, D))
    oq, okv, oo = reduce_grads(gq, gkv, go)
    shape = (seq_count, shard_size, width)
    return (
        layer_out.reshape(shape),
        tokens_grad.reshape(shape),
        oq,
        okv[:, :128],
        okv[:, 128:],
        oo,
    )


def solution(mesh):
    placed = (
        P("fsdp", "ctx", None),
        P("fsdp", "ctx"),
        P("fsdp", "ctx", None),
        P(),
        P("fsdp", None),
        P("fsdp", None),
        P("fsdp", None),
        P("fsdp", None),
        P(),
        P(),
        P(),
    )
    return jax.shard_map(
        per_device,
        mesh=mesh,
        in_specs=placed,
        out_specs=(
            P("fsdp", "ctx", None),
            P("fsdp", "ctx", None),
            P("ctx", "fsdp"),
            P("ctx", "fsdp"),
            P("ctx", "fsdp"),
            P("ctx", "fsdp"),
        ),
        check_vma=False,
    )
```

time: 1020 us -> 316 us (0.31)
  waiting for transfers between devices: 651 us -> 0 us
  Pallas kernels: 0 us -> 303 us
  local copies, waits for them, and re-layouts: 128 us -> 5.56 us
  matrix products: 93.9 us -> 0 us
  starting transfers between devices: 80.8 us -> 0 us
  other arithmetic: 41.9 us -> 5.86 us
  between operations: 15.6 us -> 0.8 us
    reduce_scatter x5 -> x0, waiting for transfers between devices: 352 us -> none  [the longest x1 80.2 us: per_device(): lax.psum_scatter(part_query.astype(jnp.bfloat16), 'ctx', scatter_dimensio...]
    pallas_call x0 -> x15, Pallas kernels: none -> 303 us  [the longest x1 69.2 us: reduce_grads(): comm_call(reduce_kernel, 'reduce_grads', 3, (sds((80, 256), F32), sds((80...]
    ppermute x24 -> x0, waiting for transfers between devices: 135 us -> none  [shifted(): return lax.ppermute(block, axis, route)]
    unnamed x15 -> x0, waiting for transfers between devices: 95.5 us -> none
    dot_general x17 -> x0, matrix products: 84.7 us -> none  [the longest x1 7.06 us: attend_back(): jnp.einsum('bgrsk,bsgrd->bkgd', soft_weights, grad_heads, preferred_eleme...]
    ppermute x24 -> x0, starting transfers between devices: 80.3 us -> none  [shifted(): return lax.ppermute(block, axis, route)]
    all_gather x4 -> x0, waiting for transfers between devices: 68.1 us -> none  [the longest x1 34.9 us: per_device(): lax.all_gather(value_weight, 'fsdp', axis=0, tiled=True)]
    another operation x7 -> x0, local copies, waits for them, and re-layouts: 49.9 us -> none  [the longest x4 43.4 us: per_device(): jnp.stack([grad_keys, grad_values])]
  transfers between devices with their start and end apart: 36 -> 0, of which waited for: 25 -> 0; matrix products, arithmetic and copies ran while one was open for 14% -> 0% of each run, Pallas kernels for 0% -> 0%
where the time goes in v1:
time: 316 us; the launch traced here: 315 us
  Pallas kernels  303 us (96%)
  other arithmetic  5.86 us (2%)
  local copies, waits for them, and re-layouts  5.56 us (2%)
    pallas_call x1, Pallas kernels, reduce_grads(): comm_call(reduce_kernel, 'reduce_grads', 3, (sds((80, 256), F32), sds((80...  69.2 us
    pallas_call x1, Pallas kernels, exchange_halo(): comm_call(halo_kernel, 'exchange_halo', 1, (sds((4, UNIT, 512), BF16), sd...  62.7 us
    pallas_call x1, Pallas kernels, gather(): comm_call(gather_kernel, 'gather_weights', 0, (sds((2, ROWS + NOTE_ROWS,...  39.2 us
    pallas_call x1, Pallas kernels, return_grads(): comm_call(return_kernel, 'return_grads', 2, sds(block, F32), [pltpu.VMEM(...  38.6 us
    pallas_call x4, Pallas kernels, swap(): comm_call(functools.partial(swap_kernel, count), name, cid, shapes, [DMA(...  20.9 us
    pallas_call x1, Pallas kernels, input_stage(): pl.pallas_call(input_kernel, name='input_stage', grid=(5,), in_specs=[pl....  14.3 us
    pallas_call x1, Pallas kernels, output_stage(): pl.pallas_call(output_kernel, name='output_stage', in_specs=vmem(5), out_...  13 us
    pallas_call x1, Pallas kernels, attend_backward(): pl.pallas_call(backward_kernel, name='attend_backward', grid=(3,), in_spe...  10.4 us

profile of v1, /device:TPU:1, one launch (start us, length us, event | category | flops | bytes accessed | tf_op | source)
XLA Modules:
  0.0 315.4 jit_solution(4226800862703106296)
XLA Ops:
  1.2 0.8 broadcast_in_dim.42.cos
  2.0 0.8 broadcast_in_dim.43.sin
  2.8 0.7 convert_bitcast_fusion
  3.6 2.0 multiply_reduce_fusion
  6.2 1.4 pad_maximum_fusion.n_ref
  7.6 39.2 %gather_weights.1 = (bf16[2,400,2560]{2,1,0:T(8,128)(2,1)}, bf16[8,2560,128]{2,1,0:T(8,128)(2,1)}) custom-call(bf16[400,2560]{1,0:T(8,128)(2,1)} %pad_maximum_fusion.n_ref, bf16[640,1024]{1,0:T(8,128)(2,1)} %wq.1, bf16[640,512]{1,0:T(8,128)(2,1)} %wk.1, bf16[640,512]{1,0:T(8,128)(2,1)} %wv.1), custom_call_target="tpu_custom_call" | custom-call | tf_op jit(solution)/shard_map/gather_weights/pallas_call | solution.py:200
  47.4 10.1 %project.1 = (bf16[2,768,256]{2,1,0:T(8,128)(2,1)}, bf16[784,512]{1,0:T(8,128)(2,1)}, f32[3,768,256]{2,1,0:T(8,128)}) custom-call(bf16[2,400,2560]{2,1,0:T(8,128)(2,1)} %get-tuple-element.30.n2, bf16[8,2560,128]{2,1,0:T(8,128)(2,1)} %get-tuple-element.31.w, f32[768,128]{1,0:T(8,128)} %bitcast.36, f32[768,128]{1,0:T(8,128)} %bitcast.38, ...), custom_call_target="tpu_custom_call" | custom-call | tf_op jit(solution)/shard_map/project/pallas_call | solution.py:249
  57.4 62.7 %exchange_halo.1 = (bf16[4,784,512]{2,1,0:T(8,128)(2,1)}, bf16[4,2,128,2560]{3,2,1,0:T(8,128)(2,1)}, bf16[2,8,2560,128]{3,2,1,0:T(8,128)(2,1)}) custom-call(bf16[784,512]{1,0:T(8,128)(2,1)} %get-tuple-element.33.unit, bf16[2,128,2560]{2,1,0:T(8,128)(2,1)} %bitcast.51, bf16[8,2560,128]{2,1,0:T(8,128)(2,1)} %get-tuple-element.31.w), custom_call_target="tpu_custom_call" | custom-call | tf_op jit(solution)/shard_map/exchange_halo/pallas_call | solution.py:409
  120.1 9.1 %attend_forward.1 = (bf16[2,3,128,512]{3,2,1,0:T(8,128)(2,1)}, bf16[3,512,1280]{2,1,0:T(8,128)(2,1)}) custom-call(bf16[2,2,3,128,256]{4,3,2,1,0:T(8,128)(2,1)} %bitcast.45, bf16[784,512]{1,0:T(8,128)(2,1)} %get-tuple-element.33.unit, bf16[4,784,512]{2,1,0:T(8,128)(2,1)} %get-tuple-element.34.halo, s32[1]{0:T(128)} %bitcast.8.base), custom_call_target="tpu_custom_call" | custom-call | tf_op jit(solution)/shard_map/attend_forward/pallas_call | solution.py:485
  129.2 4.0 %swap_attended.1.att = bf16[2,384,512]{2,1,0:T(8,128)(2,1)} custom-call(bf16[2,384,512]{2,1,0:T(8,128)(2,1)} %bitcast.42), custom_call_target="tpu_custom_call" | custom-call | tf_op jit(solution)/shard_map/swap_attended/pallas_call | solution.py:636
  133.8 13.0 %output_stage.1 = (bf16[384,2560]{1,0:T(8,128)(2,1)}, bf16[384,2560]{1,0:T(8,128)(2,1)}, bf16[2,384,512]{2,1,0:T(8,128)(2,1)}) custom-call(bf16[2,384,512]{2,1,0:T(8,128)(2,1)} %swap_attended.1.att, bf16[1024,2560]{1,0:T(8,128)(2,1)} %bitcast.41, bf16[384,2560]{1,0:T(8,128)(2,1)} %bitcast.31, bf16[384,2560]{1,0:T(8,128)(2,1)} %bitcast.34, ...), custom_call_target="tpu_custom_call" | custom-call | tf_op jit(solution)/shard_map/output_stage/pallas_call | solution.py:676
  146.8 9.0 %swap_grads.1 = (bf16[2,384,512]{2,1,0:T(8,128)(2,1)}, bf16[2,384,2560]{2,1,0:T(8,128)(2,1)}) custom-call(bf16[2,384,512]{2,1,0:T(8,128)(2,1)} %get-tuple-element.39.refs_0_, bf16[384,2560]{1,0:T(8,128)(2,1)} %get-tuple-element.40.refs_1_), custom_call_target="tpu_custom_call" | custom-call | tf_op jit(solution)/shard_map/swap_grads/pallas_call | solution.py:636
  155.8 6.3 %out_grads.1.go = bf16[4,2,4,64,640]{4,3,2,1,0:T(8,128)(2,1)} custom-call(bf16[768,512]{1,0:T(8,128)(2,1)} %bitcast.43, bf16[2,384,2560]{2,1,0:T(8,128)(2,1)} %get-tuple-element.50.gp2), custom_call_target="tpu_custom_call" | custom-call | tf_op jit(solution)/shard_map/out_grads/pallas_call | solution.py:850
  162.1 10.4 %attend_backward.1 = (bf16[2,3,128,512]{3,2,1,0:T(8,128)(2,1)}, f32[2,3,128,512]{3,2,1,0:T(8,128)}, bf16[4,2,3,128,512]{4,3,2,1,0:T(8,128)(2,1)}) custom-call(bf16[2,2,3,128,256]{4,3,2,1,0:T(8,128)(2,1)} %bitcast.46, bf16[784,512]{1,0:T(8,128)(2,1)} %get-tuple-element.33.unit, bf16[4,784,512]{2,1,0:T(8,128)(2,1)} %get-tuple-element.34.halo, ...), custom_call_target="tpu_custom_call" | custom-call | tf_op jit(solution)/shard_map/attend_backward/pallas_call | solution.py:568
  172.5 38.6 %return_grads.1 = f32[6,128,512]{2,1,0:T(8,128)} custom-call(bf16[4,6,128,512]{3,2,1,0:T(8,128)(2,1)} %bitcast.44, f32[6,128,512]{2,1,0:T(8,128)} %bitcast.50), custom_call_target="tpu_custom_call" | custom-call | tf_op jit(solution)/shard_map/return_grads/pallas_call | solution.py:774
  211.0 9.6 %in_grads.1 = (bf16[2,4,4,160,256]{4,3,2,1,0:T(8,128)(2,1)}, bf16[2,4,4,160,256]{4,3,2,1,0:T(8,128)(2,1)}, bf16[768,512]{1,0:T(8,128)(2,1)}) custom-call(bf16[2,400,2560]{2,1,0:T(8,128)(2,1)} %get-tuple-element.30.n2, f32[768,512]{1,0:T(8,128)} %bitcast.40, f32[3,768,256]{2,1,0:T(8,128)} %get-tuple-element.42.raw, f32[768,128]{1,0:T(8,128)} %bitcast.37, ...), custom_call_target="tpu_custom_call" | custom-call | tf_op jit(solution)/shard_map/in_grads/pallas_call | solution.py:816
  220.7 69.2 %reduce_grads.1 = (f32[80,256]{1,0:T(8,128)}, f32[80,256]{1,0:T(8,128)}, f32[32,640]{1,0:T(8,128)}) custom-call(bf16[2,4,4,160,256]{4,3,2,1,0:T(8,128)(2,1)} %get-tuple-element.48.gq, bf16[2,4,4,160,256]{4,3,2,1,0:T(8,128)(2,1)} %get-tuple-element.49.gkv, bf16[4,2,4,64,640]{4,3,2,1,0:T(8,128)(2,1)} %out_grads.1.go), custom_call_target="tpu_custom_call" | custom-call | tf_op jit(solution)/shard_map/reduce_grads/pallas_call | solution.py:1096
  289.9 1.4 fusion
  291.3 3.9 %swap_key_deltas.1.dkv = bf16[2,384,512]{2,1,0:T(8,128)(2,1)} custom-call(bf16[2,384,512]{2,1,0:T(8,128)(2,1)} %bitcast.52), custom_call_target="tpu_custom_call" | custom-call | tf_op jit(solution)/shard_map/swap_key_deltas/pallas_call | solution.py:636
  295.3 4.0 %swap_query_deltas.1.dq = bf16[2,384,512]{2,1,0:T(8,128)(2,1)} custom-call(bf16[2,384,512]{2,1,0:T(8,128)(2,1)} %bitcast.48), custom_call_target="tpu_custom_call" | custom-call | tf_op jit(solution)/shard_map/swap_query_deltas/pallas_call | solution.py:636
  299.3 0.6 broadcast_in_dim.44.gain
  299.9 14.3 %input_stage.1 = bf16[384,2560]{1,0:T(8,128)(2,1)} custom-call(bf16[2,384,512]{2,1,0:T(8,128)(2,1)} %swap_query_deltas.1.dq, bf16[2,384,512]{2,1,0:T(8,128)(2,1)} %swap_key_deltas.1.dkv, bf16[2,8,2560,128]{3,2,1,0:T(8,128)(2,1)} %get-tuple-element.47.w, bf16[384,2560]{1,0:T(8,128)(2,1)} %bitcast.32, bf16[384,2560]{1,0:T(8,128)(2,1)} %bitcast.35, ...), custom_call_target="tpu_custom_call" | custom-call | tf_op jit(solution)/shard_map/input_stage/pallas_call | solution.py:889
  314.2 0.6 copy.22
  314.8 0.6 copy.23
  (25 shorter events, 2.4 us)
Async XLA Ops:
  0.6 5.0 %copy-start = (bf16[3,128,2560]{2,1,0:T(8,128)(2,1)S(1)}, bf16[3,128,2560]{2,1,0:T(8,128)(2,1)}, u32[]{:S(2)}) copy-start(bf16[3,128,2560]{2,1,0:T(8,128)(2,1)} %param.11) | copy-start | bytes 5898244
  0.6 5.0 %copy-start.3 = (f32[2560]{0:T(1024)S(1)}, f32[2560]{0:T(1024)}, u32[]{:S(2)}) copy-start(f32[2560]{0:T(1024)} %param.14) | copy-start | bytes 30724
  7.6 39.2 %copy-start.5 = (f32[256]{0:T(256)S(1)}, f32[256]{0:T(256)}, u32[]{:S(2)}) copy-start(f32[256]{0:T(256)} %param.20) | copy-start | bytes 3076
  7.6 39.2 %copy-start.6 = (f32[256]{0:T(256)S(1)}, f32[256]{0:T(256)}, u32[]{:S(2)}) copy-start(f32[256]{0:T(256)} %param.19) | copy-start | bytes 3076
  120.1 13.1 %copy-start.4 = (f32[2560]{0:T(1024)S(1)}, f32[2560]{0:T(1024)}, u32[]{:S(2)}) copy-start(f32[2560]{0:T(1024)} %param.21) | copy-start | bytes 30724
  299.9 14.3 %copy-start.2 = (f32[80,256]{1,0:T(8,128)S(1)}, f32[80,256]{1,0:T(8,128)}, u32[]{:S(2)}) copy-start(f32[80,256]{1,0:T(8,128)} %get-tuple-element.66) | copy-start | bytes 245764
  299.9 14.9 %copy-start.1 = (f32[32,640]{1,0:T(8,128)S(1)}, f32[32,640]{1,0:T(8,128)}, u32[]{:S(2)}) copy-start(f32[32,640]{1,0:T(8,128)} %get-tuple-element.69) | copy-start | bytes 245764

commit v2 on v1

v2 whole, which is shorter than its diff:
```python
import functools

import jax
import jax.numpy as jnp
from jax import lax
from jax.experimental import pallas as pl
from jax.experimental.pallas import tpu as pltpu
from jax.sharding import PartitionSpec as P

EPS = 1e-06
ROPE_BASE = 10000.0
Q_FACTOR = 0.0625
WINDOW = 1024
F32 = jnp.float32
BF16 = jnp.bfloat16
MESH = pl.DeviceIdType.MESH
VMEM_LIMIT = 64 * 1024 * 1024 - 512 * 1024

D = 2560
ROWS = 384
NOTE_ROWS = 16
UNIT = 2 * ROWS + NOTE_ROWS


def place():
    y = lax.axis_index("fsdp")
    c = lax.axis_index("ctx")
    j = lax.rem(c, 2)
    zx = lax.div(c, 2)
    return y, lax.div(zx, 4), lax.rem(zx, 4), j


def dev(y, z, x, j):
    return (y, (z * 4 + x) * 2 + j)


def up(a, n=1):
    return lax.rem(a + n, 4)


def remote(src, dst, ss, rs, device):
    return pltpu.make_async_remote_copy(
        src_ref=src, dst_ref=dst, send_sem=ss, recv_sem=rs, device_id=device, device_id_type=MESH
    )


def meet(devices):
    barrier = pltpu.get_barrier_semaphore()
    for device in devices:
        pl.semaphore_signal(barrier, inc=1, device_id=device, device_id_type=MESH)
    pl.semaphore_wait(barrier, len(devices))


def rows_at(start, size, unit=16):
    return pl.ds(pl.multiple_of(start, unit), size)


def vmem(n):
    return [pl.BlockSpec(memory_space=pltpu.VMEM)] * n


def spaces(kinds):
    where = {"v": pltpu.VMEM, "h": pl.ANY}
    return [pl.BlockSpec(memory_space=where[kind]) for kind in kinds]


def comm_call(kernel, name, cid, out_shape, scratch, ins, outs):
    return pl.pallas_call(
        kernel,
        name=name,
        out_shape=list(out_shape),
        in_specs=spaces(ins),
        out_specs=spaces(outs),
        scratch_shapes=scratch,
        compiler_params=pltpu.CompilerParams(
            collective_id=cid, has_side_effects=True, vmem_limit_bytes=VMEM_LIMIT
        ),
    )


def sds(shape, dtype):
    return jax.ShapeDtypeStruct(shape, dtype)


DMA = pltpu.SemaphoreType.DMA


class RingGather:
    def __init__(self, me, plus, minus, region, half, ss, rs, index):
        self.me, self.plus, self.minus = me, plus, minus
        self.region, self.half, self.ss, self.rs, self.index = region, half, ss, rs, index

    def _copy(self, ref, k, device):
        at = self.index + (k,)
        return remote(ref, ref, self.ss.at[at], self.rs.at[at], device)

    def start(self):
        self._copy(self.region(self.me), 0, self.plus).start()
        self._copy(self.region(self.me), 1, self.minus).start()

    def forward(self):
        left, right = up(self.me, 3), up(self.me, 1)
        self._copy(self.region(left), 0, self.plus).wait_recv()
        self._copy(self.half(left, 0), 2, self.plus).start()
        self._copy(self.region(right), 1, self.minus).wait_recv()
        self._copy(self.half(right, 1), 3, self.minus).start()

    def finish(self):
        far = up(self.me, 2)
        self._copy(self.half(far, 0), 2, self.plus).wait_recv()
        self._copy(self.half(far, 1), 3, self.minus).wait_recv()

    def drain(self):
        self._copy(self.region(self.me), 0, self.plus).wait_send()
        self._copy(self.region(self.me), 1, self.minus).wait_send()
        self._copy(self.half(up(self.me, 3), 0), 2, self.plus).wait_send()
        self._copy(self.half(up(self.me, 1), 1), 3, self.minus).wait_send()


PLANE = 96


def gather_kernel(n_ref, wq, wk, wv, n2, w, lsem, nsem, ysend, yrecv, gsend, grecv, rsend, rrecv):
    y, z, x, j = place()
    partner = dev(y, z, x, 1 - j)
    xp, xm = dev(y, z, up(x), j), dev(y, z, up(x, 3), j)
    zp, zm = dev(y, up(z), x, j), dev(y, up(z, 3), x, j)
    ys = [dev(up(y, r), z, x, j) for r in (1, 2, 3)]
    own = rows_at(640 * y, 640)
    local = []
    for b in range(8):
        if b < 4:
            src = wq.at[:, pl.ds(pl.multiple_of(512 * j + 128 * b, 128), 128)]
        elif b < 6:
            src = wk.at[:, pl.ds(pl.multiple_of(256 * j + 128 * (b - 4), 128), 128)]
        else:
            src = wv.at[:, pl.ds(pl.multiple_of(256 * j + 128 * (b - 6), 128), 128)]
        local.append(pltpu.make_async_copy(src, w.at[b, own], lsem.at[b]))
    local.append(pltpu.make_async_copy(n_ref, n2.at[j], lsem.at[8]))
    for cp in local:
        cp.start()
    meet([partner, xp, xm, zp, zm] + ys)
    for cp in local[:8]:
        cp.wait()

    def piece_q(yy):
        return w.at[x, rows_at(640 * yy + PLANE * z, PLANE)]

    def piece_k(yy):
        return w.at[4 + z, rows_at(640 * yy + PLANE * x, PLANE)]

    straight = RingGather(
        y,
        ys[0],
        ys[2],
        lambda m: w.at[:, rows_at(640 * m + 4 * PLANE, 640 - 4 * PLANE)],
        lambda m, h: w.at[pl.ds(4 * h, 4), rows_at(640 * m + 4 * PLANE, 640 - 4 * PLANE)],
        rsend,
        rrecv,
        (),
    )

    first = []
    for r in range(3):
        for f, piece in enumerate((piece_q, piece_k)):
            cp = remote(piece(y), piece(y), ysend.at[f, r], yrecv.at[f, r], ys[r])
            cp.start()
            first.append((cp, f, r, piece))
    straight.start()
    swap = remote(n_ref, n2.at[j], nsem.at[0], nsem.at[1], partner)
    swap.start()

    def ring(f, stage, r):
        yy = up(y, 3 - r)
        first, count = 4 * f, PLANE // 2
        if stage == 0:
            inner = z if f == 0 else x
            region = lambda m: w.at[first + m, rows_at(640 * yy + PLANE * inner, PLANE)]
            half = lambda m, h: w.at[
                first + m, rows_at(640 * yy + PLANE * inner + count * h, count)
            ]
        else:
            region = lambda m: w.at[pl.ds(first, 4), rows_at(640 * yy + PLANE * m, PLANE)]
            half = lambda m, h: w.at[
                pl.ds(first + 2 * h, 2), rows_at(640 * yy + PLANE * m, PLANE)
            ]
        on_x = (f + stage) % 2 == 0
        me, plus, minus = (x, xp, xm) if on_x else (z, zp, zm)
        return RingGather(me, plus, minus, region, half, gsend, grecv, (f, stage, r))

    rings = [[[ring(f, s, r) for r in range(3)] for s in range(2)] for f in range(2)]
    for cp, f, r, piece in first:
        yy = up(y, 3 - r)
        remote(piece(yy), piece(yy), ysend.at[f, r], yrecv.at[f, r], ys[r]).wait_recv()
        rings[f][0][r].start()
    for r in range(3):
        for f in range(2):
            rings[f][0][r].forward()
    for r in range(3):
        for f in range(2):
            rings[f][0][r].finish()
            rings[f][1][r].start()
    straight.forward()
    for r in range(3):
        for f in range(2):
            rings[f][1][r].forward()
    for r in range(3):
        for f in range(2):
            rings[f][1][r].finish()
    for r in range(3):
        for f in range(2):
            rings[f][0][r].drain()
            rings[f][1][r].drain()
    straight.finish()
    straight.drain()
    for cp, f, r, piece in first:
        cp.wait_send()
    swap.wait()
    local[8].wait()


def gather(noted, wq, wk, wv):
    return comm_call(
        gather_kernel,
        "gather_weights",
        0,
        (sds((2, ROWS + NOTE_ROWS, D), BF16), sds((8, D, 128), BF16)),
        [
            DMA((9,)),
            DMA((2,)),
            DMA((2, 3)),
            DMA((2, 3)),
            DMA((2, 2, 3, 4)),
            DMA((2, 2, 3, 4)),
            DMA((4,)),
            DMA((4,)),
        ],
        "vvvv",
        "hh",
    )(noted, wq, wk, wv)


def project_kernel(n2, w, cos, sin, gains, q_out, unit, raw_out):
    n = pl.program_id(0)
    rows = n2[:, :ROWS, :].reshape(2 * ROWS, D)
    weight = jnp.concatenate([w[0], w[1]], axis=-1)
    acc = jnp.dot(rows, weight, preferred_element_type=F32)

    def rotated(gain, factor):
        scale = lax.rsqrt(jnp.mean(acc * acc, axis=-1, keepdims=True) + EPS)
        normed = acc * scale * gain
        a, b = normed[:, :128], normed[:, 128:]
        c, s = cos[...], sin[...]
        return (jnp.concatenate([a * c - b * s, b * c + a * s], axis=-1) * factor).astype(BF16)

    @pl.when(n < 3)
    def _():
        raw_out[0] = acc

    @pl.when(n < 2)
    def _():
        q_out[0] = rotated(gains[0:1, :], Q_FACTOR)

    @pl.when(n == 2)
    def _():
        unit[0 : 2 * ROWS, 0:256] = rotated(gains[1:2, :], 1.0)

    @pl.when(n == 3)
    def _():
        unit[0 : 2 * ROWS, 256:512] = acc.astype(BF16)
        unit[2 * ROWS : UNIT, :] = n2[0, ROWS:, 0:512] + n2[1, ROWS:, 0:512]


def project(n2, w, cos, sin, gains):
    return pl.pallas_call(
        project_kernel,
        name="project",
        grid=(4,),
        in_specs=[
            pl.BlockSpec((2, ROWS + NOTE_ROWS, D), lambda n: (0, 0, 0)),
            pl.BlockSpec((2, D, 128), lambda n: (n, 0, 0)),
            pl.BlockSpec((2 * ROWS, 128), lambda n: (0, 0)),
            pl.BlockSpec((2 * ROWS, 128), lambda n: (0, 0)),
            pl.BlockSpec((8, 256), lambda n: (0, 0)),
        ],
        out_specs=[
            pl.BlockSpec((1, 2 * ROWS, 256), lambda n: (jnp.minimum(n, 1), 0, 0)),
            pl.BlockSpec((UNIT, 512), lambda n: (0, 0)),
            pl.BlockSpec((1, 2 * ROWS, 256), lambda n: (jnp.minimum(n, 2), 0, 0)),
        ],
        out_shape=[
            sds((2, 2 * ROWS, 256), BF16),
            sds((UNIT, 512), BF16),
            sds((3, 2 * ROWS, 256), F32),
        ],
        compiler_params=pltpu.CompilerParams(vmem_limit_bytes=VMEM_LIMIT),
    )(n2, w, cos, sin, gains)


HALO_CHUNKS = 7
HALO_ROWS = UNIT // HALO_CHUNKS


def halo_kernel(unit, wo_own, w, halo, wo, wother, hsend, hrecv, osend, orecv, lsem, wsem):
    y, z, x, j = place()
    partner = dev(y, z, x, 1 - j)
    xp, xm = dev(y, z, up(x), j), dev(y, z, up(x, 3), j)
    zp, zm = dev(y, up(z), x, j), dev(y, up(z, 3), x, j)
    yp, ym = dev(up(y), z, x, j), dev(up(y, 3), z, x, j)
    ocopy = pltpu.make_async_copy(wo_own, wo.at[y], lsem.at[1])
    ocopy.start()
    meet([partner, xp, xm, zp, zm, yp, ym])

    def rows(k):
        return rows_at(k * HALO_ROWS, HALO_ROWS)

    def shift(k):
        return remote(unit.at[rows(k)], halo.at[3, rows(k)], hsend.at[0, k], hrecv.at[0, k], zp)

    def right(src, k):
        return remote(src.at[rows(k)], halo.at[0, rows(k)], hsend.at[1, k], hrecv.at[1, k], xp)

    def left(src, k):
        return remote(src.at[rows(k)], halo.at[2, rows(k)], hsend.at[2, k], hrecv.at[2, k], xm)

    def far_right(k):
        return remote(
            halo.at[0, rows(k)], halo.at[1, rows(k)], hsend.at[3, k], hrecv.at[3, k], xp
        )

    def far_left(k):
        return remote(
            halo.at[2, rows(k)], halo.at[1, rows(k)], hsend.at[4, k], hrecv.at[3, k], xm
        )

    before = halo.at[3]
    inner = jnp.logical_and(x > 0, x < 3)

    @pl.loop(0, HALO_CHUNKS)
    def _(k):
        shift(k).start()

        @pl.when(x < 3)
        def _():
            right(unit, k).start()

        @pl.when(x == 0)
        def _():
            left(unit, k).start()

    ocopy.wait()
    ring = RingGather(
        y,
        yp,
        ym,
        lambda m: wo.at[m, j],
        lambda m, h: wo.at[m, j, pl.ds(64 * h, 64)],
        osend,
        orecv,
        (0,),
    )
    ring.start()
    swap = remote(w, wother, wsem.at[0], wsem.at[1], partner)
    swap.start()

    def step(k):
        shift(k).wait_recv()

        @pl.when(x == 3)
        def _():
            right(before, k).start()

        @pl.when(x > 0)
        def _():
            left(before, k).start()

        right(unit, k).wait_recv()

        @pl.when(inner)
        def _():
            far_right(k).start()

        @pl.when(k > 0)
        def _():
            left(unit, k - 1).wait_recv()

            @pl.when(inner)
            def _():
                far_left(k - 1).start()

    pl.loop(0, 4)(step)
    ring.forward()
    share = []

    def give(n, m):
        cp = remote(wo.at[m, j], wo.at[m, j], osend.at[1, n], orecv.at[1, n], partner)
        cp.start()
        share.append(cp)

    give(0, up(y, 3))
    give(1, up(y, 1))
    pl.loop(4, HALO_CHUNKS)(step)
    left(unit, HALO_CHUNKS - 1).wait_recv()

    @pl.when(inner)
    def _():
        far_left(HALO_CHUNKS - 1).start()

    ring.finish()
    give(2, up(y, 2))
    for n, m in enumerate((up(y, 3), up(y, 1), up(y, 2))):
        remote(
            wo.at[m, 1 - j], wo.at[m, 1 - j], osend.at[1, n], orecv.at[1, n], partner
        ).wait_recv()
    for cp in share:
        cp.wait_send()
    ring.drain()

    @pl.loop(0, HALO_CHUNKS)
    def _(k):
        far_right(k).wait_recv()
        shift(k).wait_send()
        right(unit, k).wait_send()
        left(unit, k).wait_send()

        @pl.when(inner)
        def _():
            far_right(k).wait_send()
            far_left(k).wait_send()

    swap.wait()


def exchange_halo(unit, wo_own, w):
    return comm_call(
        halo_kernel,
        "exchange_halo",
        1,
        (
            sds((4, UNIT, 512), BF16),
            sds((4, 2, 128, D), BF16),
            sds((8, D, 128), BF16),
        ),
        [
            DMA((5, HALO_CHUNKS)),
            DMA((4, HALO_CHUNKS)),
            DMA((2, 4)),
            DMA((2, 4)),
            DMA((2,)),
            DMA((2,)),
        ],
        "vvh",
        "hhh",
    )(unit, wo_own, w)


KEYS = 1280


def window_of(unit, halo, s, first, last):
    parts = []
    for d in (4, 3, 2, 1, 0):
        for i in range(2):
            at = rows_at(i * ROWS + s * 128, 128)
            if d == 0:
                parts.append(unit[at, first:last])
            else:
                parts.append(halo[d - 1, at, first:last])
    return jnp.concatenate(parts, axis=0)


def map_back(upstream, raw, c, s, gain, factor):
    a, b = upstream[:, :128] * factor, upstream[:, 128:] * factor
    turned = jnp.concatenate([a * c + b * s, b * c - a * s], axis=-1) * gain
    scale = lax.rsqrt(jnp.mean(raw * raw, axis=-1, keepdims=True) + EPS)
    inner = jnp.mean(turned * raw, axis=-1, keepdims=True)
    return scale * turned - raw * (scale * scale * scale * inner)


def add_into(ref, at, other):
    ref[at] = (ref[at].astype(F32) + other.astype(F32)).astype(BF16)


class RingReduce:
    def __init__(self, me, plus, minus, data, pick, half, relay, recv, ss, rs, index):
        self.me, self.plus, self.minus = me, plus, minus
        self.data, self.pick, self.half = data, pick, half
        self.relay, self.recv, self.ss, self.rs, self.index = relay, recv, ss, rs, index

    def _copy(self, src, dst, k, device):
        at = self.index + (k,)
        return remote(src, dst, self.ss.at[at], self.rs.at[at], device)

    def _first(self):
        far = up(self.me, 2)
        return (
            self._copy(self.data.at[self.half(far, 0)], self.relay.at[0], 0, self.plus),
            self._copy(self.data.at[self.half(far, 1)], self.relay.at[1], 1, self.minus),
        )

    def _second(self):
        right, left = up(self.me, 1), up(self.me, 3)
        return (
            self._copy(self.data.at[self.pick(right)], self.recv.at[0], 2, self.plus),
            self._copy(self.data.at[self.pick(left)], self.recv.at[1], 3, self.minus),
        )

    def start(self):
        for cp in self._first():
            cp.start()

    def forward(self):
        a, b = self._first()
        c, d = self._second()
        a.wait_recv()
        add_into(self.data, self.half(up(self.me, 1), 0), self.relay[0])
        c.start()
        b.wait_recv()
        add_into(self.data, self.half(up(self.me, 3), 1), self.relay[1])
        d.start()

    def finish(self):
        c, d = self._second()
        c.wait_recv()
        d.wait_recv()
        return (
            self.data[self.pick(self.me)].astype(F32)
            + self.recv[0].astype(F32)
            + self.recv[1].astype(F32)
        )

    def drain(self):
        for cp in self._first() + self._second():
            cp.wait_send()


def middle_kernel(
    q, unit, halo, base, wo_h, tok_h, cot_h, gain, raw_h, cos, sin, gains, n2_h,
    layer_out, own, parts, qd, o_mid, gq,
    wo, tok, cot, raw, n2, soft, att, attx, proj, gp2, grad, grad_send, go, o_relay, o_recv,
    loadsem, asend, arecv, gsend, grecv, dsem, ss, rs,
):
    y, z, x, j = place()
    partner = dev(y, z, x, 1 - j)
    yp, ym = dev(up(y), z, x, j), dev(up(y, 3), z, x, j)
    loads = [
        pltpu.make_async_copy(src, dst, loadsem.at[n])
        for n, (src, dst) in enumerate(
            ((wo_h, wo), (tok_h, tok), (cot_h, cot), (raw_h.at[pl.ds(0, 2)], raw), (n2_h, n2))
        )
    ]
    for cp in loads:
        cp.start()
    meet([partner, yp, ym])

    def give_attended(s):
        return remote(att.at[1 - j, s], attx.at[s], asend.at[s], arecv.at[s], partner)

    key_at = lax.broadcasted_iota(jnp.int32, (256, KEYS), 1) - WINDOW
    query_at = lax.broadcasted_iota(jnp.int32, (256, KEYS), 0)

    @pl.loop(0, 3)
    def _(s):
        keys = window_of(unit, halo, s, 0, 256)
        values = window_of(unit, halo, s, 256, 512)
        lanes = pl.ds(pl.multiple_of(s * 128, 128), 128)
        notes = []
        for d in (4, 3, 2, 1, 0):
            block = unit[2 * ROWS :, lanes] if d == 0 else halo[d - 1, 2 * ROWS :, lanes]
            block = block.astype(F32)
            notes.extend([block[0:1], block[8:9]])
        key_docs = jnp.concatenate(notes, axis=-1)
        query_docs = jnp.concatenate(
            [jnp.transpose(jnp.broadcast_to(note, (128, 128))) for note in notes[8:]], axis=0
        )
        query_docs = jnp.concatenate([query_docs] * (KEYS // 128), axis=-1)
        allowed = (
            (query_docs == key_docs)
            & (key_at <= query_at)
            & (key_at > query_at - WINDOW)
            & (key_at + base[0:1, 0:1] >= 0)
        )
        for h in range(2):
            rows = q[h, :, s].reshape(256, 256)
            scores = lax.dot_general(
                rows, keys, (((1,), (1,)), ((), ())), preferred_element_type=F32
            )
            masked = jnp.where(allowed, scores, -1e30)
            highest = jnp.max(masked, axis=-1, keepdims=True)
            raised = jnp.exp(masked - highest)
            weights = (raised / jnp.sum(raised, axis=-1, keepdims=True)).astype(BF16)
            soft[s, 256 * h : 256 * h + 256, :] = weights
            out = jnp.dot(weights, values, preferred_element_type=F32).astype(BF16)
            att[:, s, :, 256 * h : 256 * h + 256] = out.reshape(2, 128, 256)
        give_attended(s).start()

    for cp in loads[:3]:
        cp.wait()
    for s in range(3):
        give_attended(s).wait_recv()
    mine, others = att[j].reshape(ROWS, 512), attx[...].reshape(ROWS, 512)
    own_heads, other_heads = rows_at(512 * j, 512), rows_at(512 * (1 - j), 512)

    @pl.loop(0, 5)
    def _(n):
        cols = pl.ds(pl.multiple_of(512 * n, 512), 512)
        proj[:, cols] = jnp.dot(
            mine, wo[own_heads, cols], preferred_element_type=F32
        ) + jnp.dot(others, wo[other_heads, cols], preferred_element_type=F32)

    def give_projected(t):
        at = pl.ds(128 * t, 128)
        return remote(gp2.at[0, at], gp2.at[1, at], gsend.at[t], grecv.at[t], partner)

    for t in range(3):

        @pl.loop(8 * t, 8 * t + 8)
        def _(k):
            at = rows_at(k * 16, 16)
            p = proj[at, :]
            g = gain[...]
            scale = lax.rsqrt(jnp.mean(p * p, axis=-1, keepdims=True) + EPS)
            layer_out[at, :] = (tok[at, :].astype(F32) + p * scale * g).astype(BF16)
            h = cot[at, :].astype(F32) * g
            inner = jnp.mean(h * p, axis=-1, keepdims=True)
            gp2[0, at, :] = (scale * h - p * (scale * scale * scale * inner)).astype(BF16)

        give_projected(t).start()

    upstream = gp2[0]

    def attended_grad(heads):
        part = lax.dot_general(
            upstream, wo[heads, :], (((1,), (1,)), ((), ())), preferred_element_type=F32
        )
        return part.astype(BF16).reshape(3, 128, 512)

    grad_send[...] = attended_grad(other_heads)
    give_grad = remote(grad_send, grad.at[j], dsem.at[0], dsem.at[1], partner)
    give_grad.start()
    grad[j] = attended_grad(own_heads)
    for t in range(3):
        give_projected(t).wait_recv()
    across = (((0,), (0,)), ((), ()))
    other_rows = att[1 - j].reshape(ROWS, 512)
    for n in range(4):
        cols = slice(640 * n, 640 * n + 640)
        term = lax.dot_general(
            mine, gp2[0, :, cols], across, preferred_element_type=F32
        ) + lax.dot_general(other_rows, gp2[1, :, cols], across, preferred_element_type=F32)
        go[n] = term.astype(BF16).reshape(2, 4, 64, 640)
    o1 = RingReduce(
        y, yp, ym, go, lambda m: (m,), lambda m, h: (m, h), o_relay, o_recv, ss, rs, ()
    )
    o1.start()
    loads[3].wait()
    give_grad.wait_recv()

    def backward(first, last):
        @pl.loop(first, last)
        def _(s):
            keys = window_of(unit, halo, s, 0, 256)
            values = window_of(unit, halo, s, 256, 512)
            grads = jnp.concatenate(
                [grad[:, s, :, 256 * h : 256 * h + 256].reshape(256, 256) for h in range(2)],
                axis=0,
            )
            weights = soft[s]

            def emit(part, first_col):
                for n, d in enumerate((4, 3, 2, 1, 0)):
                    for i in range(2):
                        piece = part[256 * n + 128 * i : 256 * n + 128 * i + 128]
                        if d == 0:
                            own[i, s, :, first_col : first_col + 256] = piece
                        else:
                            parts[d - 1, i, s, :, first_col : first_col + 256] = piece.astype(BF16)

            emit(lax.dot_general(weights, grads, across, preferred_element_type=F32), 256)
            grad_weights = lax.dot_general(
                grads, values, (((1,), (1,)), ((), ())), preferred_element_type=F32
            )
            wide = weights.astype(F32)
            moved = wide * grad_weights
            dots = jnp.sum(moved, axis=-1, keepdims=True)
            score_grads = (moved - wide * dots).astype(BF16)
            grad_queries = jnp.dot(score_grads, keys, preferred_element_type=F32)
            queries = jnp.concatenate(
                [q[h, :, s].reshape(256, 256) for h in range(2)], axis=0
            )
            emit(lax.dot_general(score_grads, queries, across, preferred_element_type=F32), 0)
            c, sn = cos[:, s].reshape(256, 128), sin[:, s].reshape(256, 128)
            for h in range(2):
                back = map_back(
                    grad_queries[256 * h : 256 * h + 256],
                    raw[h, :, s].reshape(256, 256),
                    c,
                    sn,
                    gains[0:1, :],
                    Q_FACTOR,
                )
                qd[:, s, :, 256 * h : 256 * h + 256] = back.astype(BF16).reshape(2, 128, 256)

    backward(0, 2)
    o1.forward()
    backward(2, 3)
    loads[4].wait()

    @pl.loop(0, 4)
    def _(n):
        rows = n2[:, :ROWS, pl.ds(pl.multiple_of(640 * n, 128), 640)].reshape(2 * ROWS, 640)
        for h in range(2):
            deltas = qd[:, :, :, 256 * h : 256 * h + 256].reshape(2 * ROWS, 256)
            term = lax.dot_general(rows, deltas, across, preferred_element_type=F32)
            gq[h, n] = term.astype(BF16).reshape(4, 160, 256)

    o_mid[...] = o1.finish().astype(BF16)
    o1.drain()
    for s in range(3):
        give_attended(s).wait_send()
        give_projected(s).wait_send()
    give_grad.wait_send()


def middle(q, unit, halo, base, wo, tok, cot, gain, raw, cos, sin, gains, n2):
    return comm_call(
        middle_kernel,
        "middle",
        4,
        (
            sds((ROWS, D), BF16),
            sds((2, 3, 128, 512), F32),
            sds((4, 2, 3, 128, 512), BF16),
            sds((2, 3, 128, 512), BF16),
            sds((2, 4, 64, 640), BF16),
            sds((2, 4, 4, 160, 256), BF16),
        ),
        [
            pltpu.VMEM((1024, D), BF16),
            pltpu.VMEM((ROWS, D), BF16),
            pltpu.VMEM((ROWS, D), BF16),
            pltpu.VMEM((2, 2, 3, 128, 256), F32),
            pltpu.VMEM((2, ROWS + NOTE_ROWS, D), BF16),
            pltpu.VMEM((3, 512, KEYS), BF16),
            pltpu.VMEM((2, 3, 128, 512), BF16),
            pltpu.VMEM((3, 128, 512), BF16),
            pltpu.VMEM((ROWS, D), F32),
            pltpu.VMEM((2, ROWS, D), BF16),
            pltpu.VMEM((2, 3, 128, 512), BF16),
            pltpu.VMEM((3, 128, 512), BF16),
            pltpu.VMEM((4, 2, 4, 64, 640), BF16),
            pltpu.VMEM((2, 4, 64, 640), BF16),
            pltpu.VMEM((2, 2, 4, 64, 640), BF16),
            DMA((5,)),
            DMA((3,)),
            DMA((3,)),
            DMA((3,)),
            DMA((3,)),
            DMA((2,)),
            DMA((4,)),
            DMA((4,)),
        ],
        "vvvvhhhvhvvvh",
        "vvvvvv",
    )(
        q.reshape(2, 2, 3, 128, 256),
        unit,
        halo,
        base,
        wo,
        tok,
        cot,
        gain,
        raw.reshape(3, 2, 3, 128, 256),
        cos.reshape(2, 3, 128, 128),
        sin.reshape(2, 3, 128, 128),
        gains,
        n2,
    )


def key_grads_kernel(n2, total, raw, cos, sin, gains, gkv, kvd):
    @pl.when(pl.program_id(0) == 0)
    def _():
        kd = map_back(total[:, :256], raw[0], cos[...], sin[...], gains[1:2, :], 1.0)
        kvd[:, :256] = kd.astype(BF16)
        kvd[:, 256:] = total[:, 256:].astype(BF16)

    rows = n2[:, :ROWS, :].reshape(2 * ROWS, 640)
    for half in range(2):
        rhs = jnp.concatenate(
            [kvd[:, 128 * half : 128 * half + 128], kvd[:, 256 + 128 * half : 384 + 128 * half]],
            axis=-1,
        )
        term = lax.dot_general(rows, rhs, (((0,), (0,)), ((), ())), preferred_element_type=F32)
        term = term.astype(BF16).reshape(4, 2, 80, 256)
        for i in range(2):
            gkv[i, half, 0] = term[:, i]


def key_grads(n2, total, raw, cos, sin, gains):
    return pl.pallas_call(
        key_grads_kernel,
        name="key_grads",
        grid=(4,),
        in_specs=[
            pl.BlockSpec((2, ROWS + NOTE_ROWS, 640), lambda n: (0, 0, n)),
            pl.BlockSpec((2 * ROWS, 512), lambda n: (0, 0)),
            pl.BlockSpec((1, 2 * ROWS, 256), lambda n: (2, 0, 0)),
            pl.BlockSpec((2 * ROWS, 128), lambda n: (0, 0)),
            pl.BlockSpec((2 * ROWS, 128), lambda n: (0, 0)),
            pl.BlockSpec((8, 256), lambda n: (0, 0)),
        ],
        out_specs=[
            pl.BlockSpec((2, 2, 1, 4, 80, 256), lambda n: (0, 0, n, 0, 0, 0)),
            pl.BlockSpec((2 * ROWS, 512), lambda n: (0, 0)),
        ],
        out_shape=[
            sds((2, 2, 4, 4, 80, 256), BF16),
            sds((2 * ROWS, 512), BF16),
        ],
        compiler_params=pltpu.CompilerParams(vmem_limit_bytes=VMEM_LIMIT),
    )(n2, total, raw, cos, sin, gains)


CHUNKS = 6
EVERY = slice(None)


def send_last(end, land, sends, ls, lr, lc, start):
    for n, (src, slot, device, here) in enumerate(sends):

        @pl.when(here)
        def _():
            cp = pltpu.make_async_copy(src, land.at[slot], lc)
            if start:
                cp.start()
            else:
                cp.wait()

        @pl.when(jnp.logical_not(here))
        def _():
            cp = remote(src, land.at[slot], ls.at[n], lr.at[slot], device)
            if start:
                cp.start()
            else:
                cp.wait_send()


def sum_last(like, land, ls, lr, me, mine, partner, out):
    for m in range(4):

        @pl.when(jnp.logical_not(jnp.logical_and(m == me, mine)))
        def _():
            remote(like, land.at[m], ls.at[0], lr.at[m], partner).wait_recv()

    out[...] = (land[0].astype(F32) + land[1].astype(F32)) + (
        land[2].astype(F32) + land[3].astype(F32)
    )


def return_kernel(
    parts, own, o_mid, gq, qd,
    total, oo, q_mid, dq,
    relay, near, after, relayed, summed, bsum,
    o_relay2, o_recv2, o_end, o_land, q_relay, q_recv,
    ssem, rsem, ss, rs, ls, lr, lc, dsem,
):
    y, z, x, j = place()
    partner = dev(y, z, x, 1 - j)
    xp, xm = dev(y, z, up(x), j), dev(y, z, up(x, 3), j)
    zp, zm = dev(y, up(z), x, j), dev(y, up(z, 3), x, j)
    zfar = [dev(y, up(z, r), x, i) for r in (1, 2, 3) for i in (0, 1)]
    keep = pltpu.make_async_copy(qd.at[j], dq.at[0], dsem.at[0])
    keep.start()
    meet([partner, xp, xm] + zfar)
    inner = jnp.logical_and(x > 0, x < 3)
    low = x < 2

    def relay_left(k):
        return remote(parts.at[1, k], relay.at[0, k], ssem.at[0, k], rsem.at[0, k], xm)

    def relay_right(k):
        return remote(parts.at[1, k], relay.at[1, k], ssem.at[1, k], rsem.at[1, k], xp)

    def to_left(src, k):
        return remote(src.at[k], near.at[0, k], ssem.at[2, k], rsem.at[2, k], xm)

    def to_right(src, k):
        return remote(src.at[k], near.at[1, k], ssem.at[3, k], rsem.at[3, k], xp)

    def back(k):
        return remote(bsum.at[k], after.at[k], ssem.at[4, k], rsem.at[4, k], zm)

    q1 = RingReduce(
        z, zp, zm, gq, lambda m: (EVERY, m), lambda m, h: (h, m), q_relay, q_recv, ss, rs, (0,)
    )
    o2 = RingReduce(
        x, xp, xm, o_mid, lambda m: (EVERY, m), lambda m, h: (h, m),
        o_relay2, o_recv2, ss, rs, (1,),
    )

    q1.start()
    o2.start()

    @pl.loop(0, CHUNKS)
    def _(k):
        @pl.when(low)
        def _():
            relay_right(k).start()

        @pl.when(jnp.logical_not(low))
        def _():
            relay_left(k).start()

        @pl.when(jnp.logical_not(inner))
        def _():
            to_left(parts.at[0], k).start()
            to_right(parts.at[2], k).start()

    give = remote(qd.at[1 - j], dq.at[1], dsem.at[1], dsem.at[2], partner)
    give.start()

    def relay_step(first, last):
        @pl.when(inner)
        def _():
            @pl.loop(first, last)
            def _(k):
                relay_left(k).wait_recv()
                relayed[0, k] = (parts[0, k].astype(F32) + relay[0, k].astype(F32)).astype(BF16)
                to_left(relayed.at[0], k).start()
                relay_right(k).wait_recv()
                relayed[1, k] = (parts[2, k].astype(F32) + relay[1, k].astype(F32)).astype(BF16)
                to_right(relayed.at[1], k).start()

    def near_step(first, last):
        @pl.loop(first, last)
        def _(k):
            to_left(parts.at[0], k).wait_recv()
            to_right(parts.at[2], k).wait_recv()
            from_right = near[0, k].astype(F32)
            from_left = near[1, k].astype(F32)
            zero = jnp.zeros_like(from_left)
            near_a = jnp.where(x < 3, from_right, zero) + jnp.where(x == 0, from_left, zero)
            near_b = jnp.where(x == 3, from_right, zero) + jnp.where(x > 0, from_left, zero)
            summed[k] = near_a
            bsum[k] = (parts[3, k].astype(F32) + near_b).astype(BF16)
            back(k).start()

    relay_step(0, 2)
    q1.forward()
    relay_step(2, 4)
    o2.forward()
    relay_step(4, CHUNKS)
    near_step(0, 3)
    q_mid[...] = q1.finish().astype(BF16)
    near_step(3, CHUNKS)

    o_end[...] = o2.finish().astype(BF16)
    o_sends = []
    for h in range(2):
        for i in range(2):
            goal = 2 * j + h
            o_sends.append(
                (
                    o_end.at[h, pl.ds(32 * i, 32)],
                    z,
                    dev(y, goal, x, i),
                    jnp.logical_and(goal == z, i == j),
                )
            )
    send_last(o_end, o_land, o_sends, ls, lr, lc, True)

    @pl.loop(0, CHUNKS)
    def _(k):
        back(k).wait_recv()
        total[k] = own[k] + summed[k] + after[k].astype(F32)

    send_last(o_end, o_land, o_sends, ls, lr, lc, False)
    sum_last(o_end.at[0, pl.ds(0, 32)], o_land, ls, lr, z, lax.div(z, 2) == j, partner, oo)

    @pl.loop(0, CHUNKS)
    def _(k):
        @pl.when(low)
        def _():
            relay_right(k).wait_send()

        @pl.when(jnp.logical_not(low))
        def _():
            relay_left(k).wait_send()

        to_left(parts.at[0], k).wait_send()
        to_right(parts.at[2], k).wait_send()
        back(k).wait_send()

    for ring in (q1, o2):
        ring.drain()
    keep.wait()
    give.wait()


def return_grads(parts, own, o_mid, gq, qd):
    block = (CHUNKS, 128, 512)
    return comm_call(
        return_kernel,
        "return_grads",
        2,
        (
            sds(block, F32),
            sds((32, 640), F32),
            sds((2, 4, 160, 256), BF16),
            sds((2, ROWS, 512), BF16),
        ),
        [
            pltpu.VMEM((2,) + block, BF16),
            pltpu.VMEM((2,) + block, BF16),
            pltpu.VMEM(block, BF16),
            pltpu.VMEM((2,) + block, BF16),
            pltpu.VMEM(block, F32),
            pltpu.VMEM(block, BF16),
            pltpu.VMEM((2, 64, 640), BF16),
            pltpu.VMEM((2, 2, 64, 640), BF16),
            pltpu.VMEM((2, 64, 640), BF16),
            pltpu.VMEM((4, 32, 640), BF16),
            pltpu.VMEM((2, 4, 160, 256), BF16),
            pltpu.VMEM((2, 2, 4, 160, 256), BF16),
            DMA((5, CHUNKS)),
            DMA((5, CHUNKS)),
            DMA((2, 4)),
            DMA((2, 4)),
            DMA((4,)),
            DMA((4,)),
            DMA(()),
            DMA((3,)),
        ],
        "vvvvv",
        "vvvv",
    )(parts.reshape((4,) + block), own.reshape(block), o_mid, gq, qd)


def finish_kernel(
    gkv, kvd, dq, q_mid, w, wother, tok, cot, gain,
    okv, oq, out,
    dkv, w_buf, tok_buf, cot_buf, acc,
    relay, recv, mid, relay2, recv2, end, land, q_relay, q_recv, q_end, q_land,
    ss, rs, ls, lr, lc, dsem, msem,
):
    y, z, x, j = place()
    partner = dev(y, z, x, 1 - j)
    xp, xm = dev(y, z, up(x), j), dev(y, z, up(x, 3), j)
    zp, zm = dev(y, up(z), x, j), dev(y, up(z, 3), x, j)
    yfar = [dev(up(y, r), z, x, i) for r in (1, 2, 3) for i in (0, 1)]
    loads = [
        pltpu.make_async_copy(kvd.at[j], dkv.at[0], msem.at[0]),
        pltpu.make_async_copy(w, w_buf.at[0], msem.at[1]),
        pltpu.make_async_copy(wother, w_buf.at[1], msem.at[2]),
        pltpu.make_async_copy(tok, tok_buf, msem.at[3]),
        pltpu.make_async_copy(cot, cot_buf, msem.at[4]),
    ]
    for cp in loads:
        cp.start()
    meet([partner, xp, xm, zp, zm] + yfar)
    firsts, seconds = [], []
    for f in range(2):
        on_z, on_x = (z, zp, zm), (x, xp, xm)
        a, b = (on_z, on_x) if f == 0 else (on_x, on_z)
        if f == 0:
            pick, half = lambda m: (EVERY, m), lambda m, h: (h, m)
        else:
            pick, half = lambda m: (EVERY, EVERY, m), lambda m, h: (h, EVERY, m)
        firsts.append(
            RingReduce(*a, gkv.at[f], pick, half, relay.at[f], recv.at[f], ss, rs, (f, 0))
        )
        seconds.append(
            RingReduce(
                *b, mid.at[f], lambda m: (EVERY, m), lambda m, h: (h, m),
                relay2.at[f], recv2.at[f], ss, rs, (f, 1),
            )
        )
    q2 = RingReduce(
        x, xp, xm, q_mid, lambda m: (EVERY, m), lambda m, h: (h, m), q_relay, q_recv, ss, rs, (2, 0)
    )
    give = remote(kvd.at[1 - j], dkv.at[1], dsem.at[0], dsem.at[1], partner)
    give.start()
    q2.start()
    for ring in firsts:
        ring.start()
    for cp in loads:
        cp.wait()
    give.wait_recv()

    def tiles(first, last):
        @pl.loop(first, last)
        def _(n):
            total = None
            for half in range(2):
                lhs = jnp.concatenate([dq[half], dkv[half]], axis=-1)
                rhs = jnp.concatenate(
                    [w_buf[half, b, rows_at(512 * n, 512), :] for b in range(8)], axis=-1
                )
                term = lax.dot_general(
                    lhs, rhs, (((1,), (1,)), ((), ())), preferred_element_type=F32
                )
                total = term if total is None else total + term
            acc[n] = total

    def norm_rows(first, last):
        @pl.loop(first, last)
        def _(k):
            at = rows_at(k * 16, 16)
            t = tok_buf[at, :].astype(F32)
            grad = jnp.concatenate([acc[m, at, :] for m in range(5)], axis=-1)
            h = grad * gain[...]
            scale = lax.rsqrt(jnp.mean(t * t, axis=-1, keepdims=True) + EPS)
            inner = jnp.mean(h * t, axis=-1, keepdims=True)
            back = scale * h - t * (scale * scale * scale * inner)
            out[at, :] = (cot_buf[at, :].astype(F32) + back).astype(BF16)

    tiles(0, 1)
    q2.forward()
    tiles(1, 2)
    for ring in firsts:
        ring.forward()
    tiles(2, 4)
    q_end[...] = q2.finish().astype(BF16)
    q_sends = []
    for h in range(2):
        for i in range(2):
            goal = 2 * j + h
            q_sends.append(
                (
                    q_end.at[h, pl.ds(80 * i, 80)],
                    y,
                    dev(goal, z, x, i),
                    jnp.logical_and(goal == y, i == j),
                )
            )
    send_last(q_end, q_land, q_sends, ls.at[1], lr.at[1], lc.at[1], True)
    tiles(4, 5)
    for f in range(2):
        mid[f] = firsts[f].finish().astype(BF16)
        seconds[f].start()
    norm_rows(0, 12)
    for ring in seconds:
        ring.forward()
    norm_rows(12, 24)
    sends = []
    for f in range(2):
        end[f] = seconds[f].finish().astype(BF16)
        for h in range(2):
            goal = 2 * j + h
            sends.append(
                (end.at[f, h], y, dev(goal, z, x, f), jnp.logical_and(goal == y, f == j))
            )
    send_last(end, land, sends, ls.at[0], lr.at[0], lc.at[0], True)
    mine = lax.div(y, 2) == j
    send_last(q_end, q_land, q_sends, ls.at[1], lr.at[1], lc.at[1], False)
    sum_last(q_end.at[0, pl.ds(0, 80)], q_land, ls.at[1], lr.at[1], y, mine, partner, oq)
    send_last(end, land, sends, ls.at[0], lr.at[0], lc.at[0], False)
    sum_last(end.at[0, 0], land, ls.at[0], lr.at[0], y, mine, partner, okv)
    for ring in firsts + seconds + [q2]:
        ring.drain()
    give.wait_send()


def finish(gkv, kvd, dq, q_mid, w, wother, tok, cot, gain):
    return comm_call(
        finish_kernel,
        "finish",
        3,
        (sds((80, 256), F32), sds((80, 256), F32), sds((ROWS, D), BF16)),
        [
            pltpu.VMEM((2, ROWS, 512), BF16),
            pltpu.VMEM((2, 8, D, 128), BF16),
            pltpu.VMEM((ROWS, D), BF16),
            pltpu.VMEM((ROWS, D), BF16),
            pltpu.VMEM((5, ROWS, 512), F32),
            pltpu.VMEM((2, 2, 4, 80, 256), BF16),
            pltpu.VMEM((2, 2, 2, 4, 80, 256), BF16),
            pltpu.VMEM((2, 2, 4, 80, 256), BF16),
            pltpu.VMEM((2, 2, 80, 256), BF16),
            pltpu.VMEM((2, 2, 2, 80, 256), BF16),
            pltpu.VMEM((2, 2, 80, 256), BF16),
            pltpu.VMEM((4, 80, 256), BF16),
            pltpu.VMEM((2, 160, 256), BF16),
            pltpu.VMEM((2, 2, 160, 256), BF16),
            pltpu.VMEM((2, 160, 256), BF16),
            pltpu.VMEM((4, 80, 256), BF16),
            DMA((3, 2, 4)),
            DMA((3, 2, 4)),
            DMA((2, 4)),
            DMA((2, 4)),
            DMA((2,)),
            DMA((2,)),
            DMA((5,)),
        ],
        "vvvvhhhhv",
        "vvv",
    )(gkv, kvd, dq, q_mid, w, wother, tok, cot, gain)


def per_device(
    tokens,
    doc_ids,
    cotangent,
    input_gain,
    query_weight,
    key_weight,
    value_weight,
    output_weight,
    query_gain,
    key_gain,
    post_gain,
):
    seq_count, shard_size, width = tokens.shape
    c = lax.axis_index("ctx")
    core = lax.rem(c, 2)
    tok = tokens.reshape(ROWS, D)
    cot = cotangent.reshape(ROWS, D)
    wide = tok.astype(F32)
    scale = lax.rsqrt(jnp.mean(wide * wide, axis=-1, keepdims=True) + EPS)
    normed = (wide * scale * input_gain).astype(BF16)
    line = jnp.pad(doc_ids.reshape(1, ROWS).astype(BF16), ((0, 0), (0, D - ROWS)))
    at = lax.broadcasted_iota(jnp.int32, (NOTE_ROWS, 1), 0)
    notes = jnp.where(at == 8 * core, line, jnp.zeros((), BF16))
    noted = jnp.concatenate([normed, notes], axis=0)

    start = lax.div(c, 2) * 256
    positions = (start + jnp.arange(256, dtype=jnp.int32)).astype(F32)
    exponents = jnp.arange(128, dtype=jnp.int32).astype(F32) * (2.0 / 256)
    angles = positions[:, None] * ROPE_BASE ** (-exponents)

    def table(values):
        values = values.reshape(2, 1, 128, 128)
        return jnp.broadcast_to(values, (2, 3, 128, 128)).reshape(2 * ROWS, 128)

    cos, sin = table(jnp.cos(angles)), table(jnp.sin(angles))
    gains = jnp.pad(jnp.stack([query_gain, key_gain]), ((0, 6), (0, 0)))
    base = jnp.full((8, 128), start, jnp.int32)

    n2, w = gather(noted, query_weight, key_weight, value_weight)
    q, unit, raw = project(n2, w, cos, sin, gains)
    halo, wo, wother = exchange_halo(unit, output_weight.reshape(2, 128, D), w)
    layer_out, own, parts, qd, o_mid, gq = middle(
        q, unit, halo, base, wo.reshape(1024, D), tok, cot, post_gain.reshape(1, D),
        raw, cos, sin, gains, n2,
    )
    total, oo, q_mid, dq = return_grads(parts, own, o_mid, gq, qd.reshape(2, ROWS, 512))
    gkv, kvd = key_grads(n2, total.reshape(2 * ROWS, 512), raw, cos, sin, gains)
    okv, oq, tokens_grad = finish(
        gkv, kvd.reshape(2, ROWS, 512), dq, q_mid, w, wother, tok, cot, input_gain.reshape(1, D)
    )
    shape = (seq_count, shard_size, width)
    return (
        layer_out.reshape(shape),
        tokens_grad.reshape(shape),
        oq,
        okv[:, :128],
        okv[:, 128:],
        oo,
    )


def solution(mesh):
    placed = (
        P("fsdp", "ctx", None),
        P("fsdp", "ctx"),
        P("fsdp", "ctx", None),
        P(),
        P("fsdp", None),
        P("fsdp", None),
        P("fsdp", None),
        P("fsdp", None),
        P(),
        P(),
        P(),
    )
    return jax.shard_map(
        per_device,
        mesh=mesh,
        in_specs=placed,
        out_specs=(
            P("fsdp", "ctx", None),
            P("fsdp", "ctx", None),
            P("ctx", "fsdp"),
            P("ctx", "fsdp"),
            P("ctx", "fsdp"),
            P("ctx", "fsdp"),
        ),
        check_vma=False,
    )
```

time: 316 us -> 267 us (0.84)
  Pallas kernels: 303 us -> 250 us
  local copies, waits for them, and re-layouts: 5.56 us -> 10.5 us
    pallas_call x12 -> x4, Pallas kernels: 191 us -> 162 us  [the longest x1 54 us: middle(): comm_call(middle_kernel, 'middle', 4, (sds((ROWS, D), BF16), sds((2, 3, 1...]
    pallas_call x1, Pallas kernels: 62.7 us -> 46.3 us  [exchange_halo(): comm_call(halo_kernel, 'exchange_halo', 1, (sds((4, UNIT, 512), BF16), sd...]
    pallas_call x1, Pallas kernels: 39.2 us -> 31.9 us  [gather(): comm_call(gather_kernel, 'gather_weights', 0, (sds((2, ROWS + NOTE_ROWS,...]
    unnamed x17 -> x21, local copies, waits for them, and re-layouts: 1.31 us -> 5.52 us
where the time goes in v2:
time: 267 us
  Pallas kernels  250 us (94%)
  local copies, waits for them, and re-layouts  10.5 us (4%)
  other arithmetic  5.92 us (2%)
    pallas_call x1, Pallas kernels, middle(): comm_call(middle_kernel, 'middle', 4, (sds((ROWS, D), BF16), sds((2, 3, 1...  54 us
    pallas_call x1, Pallas kernels, return_grads(): comm_call(return_kernel, 'return_grads', 2, (sds(block, F32), sds((32, 64...  51.2 us
    pallas_call x1, Pallas kernels, finish(): comm_call(finish_kernel, 'finish', 3, (sds((80, 256), F32), sds((80, 256)...  49 us
    pallas_call x1, Pallas kernels, exchange_halo(): comm_call(halo_kernel, 'exchange_halo', 1, (sds((4, UNIT, 512), BF16), sd...  46.3 us
    pallas_call x1, Pallas kernels, gather(): comm_call(gather_kernel, 'gather_weights', 0, (sds((2, ROWS + NOTE_ROWS,...  31.9 us
    pallas_call x1, Pallas kernels, project(): pl.pallas_call(project_kernel, name='project', grid=(4,), in_specs=[pl.Bl...  10 us
    pallas_call x1, Pallas kernels, key_grads(): pl.pallas_call(key_grads_kernel, name='key_grads', grid=(4,), in_specs=[p...  7.46 us
    unnamed x21, local copies, waits for them, and re-layouts  5.52 us

profile of v2, /device:TPU:1, one launch (start us, length us, event | category | flops | bytes accessed | tf_op | source)
XLA Modules:
  0.0 267.1 jit_solution(17605891325610335962)
XLA Ops:
  0.7 0.5 multiply_sine_fusion
  1.2 0.8 broadcast_in_dim.45.cos
  2.0 0.8 broadcast_in_dim.46.sin
  2.8 0.7 convert_bitcast_fusion
  3.5 0.1 broadcast_select_fusion
  3.6 2.0 multiply_reduce_fusion
  5.6 0.5 multiply_convert_fusion
  6.1 1.5 pad_maximum_fusion.n_ref
  7.6 31.9 %gather_weights.1 = (bf16[2,400,2560]{2,1,0:T(8,128)(2,1)}, bf16[8,2560,128]{2,1,0:T(8,128)(2,1)}) custom-call(bf16[400,2560]{1,0:T(8,128)(2,1)} %pad_maximum_fusion.n_ref, bf16[640,1024]{1,0:T(8,128)(2,1)} %wq.1, bf16[640,512]{1,0:T(8,128)(2,1)} %wk.1, bf16[640,512]{1,0:T(8,128)(2,1)} %wv.1), custom_call_target="tpu_custom_call" | custom-call | tf_op jit(solution)/shard_map/gather_weights/pallas_call | solution.py:223
  39.6 0.6 select_maximum_fusion.gains
  40.2 10.0 %project.1 = (bf16[2,768,256]{2,1,0:T(8,128)(2,1)}, bf16[784,512]{1,0:T(8,128)(2,1)}, f32[3,768,256]{2,1,0:T(8,128)}) custom-call(bf16[2,400,2560]{2,1,0:T(8,128)(2,1)} %get-tuple-element.29.n2.n2_h, bf16[8,2560,128]{2,1,0:T(8,128)(2,1)} %get-tuple-element.30.w, f32[768,128]{1,0:T(8,128)} %bitcast.31, f32[768,128]{1,0:T(8,128)} %bitcast.33, ...), custom_call_target="tpu_custom_call" | custom-call | tf_op jit(solution)/shard_map/project/pallas_call | solution.py:275
  50.2 46.3 %exchange_halo.1 = (bf16[4,784,512]{2,1,0:T(8,128)(2,1)}, bf16[4,2,128,2560]{3,2,1,0:T(8,128)(2,1)}, bf16[8,2560,128]{2,1,0:T(8,128)(2,1)}) custom-call(bf16[784,512]{1,0:T(8,128)(2,1)} %get-tuple-element.32.unit, bf16[2,128,2560]{2,1,0:T(8,128)(2,1)} %bitcast.41, bf16[8,2560,128]{2,1,0:T(8,128)(2,1)} %get-tuple-element.30.w), custom_call_target="tpu_custom_call" | custom-call | tf_op jit(solution)/shard_map/exchange_halo/pallas_call | solution.py:435
  96.5 0.6 broadcast_in_dim.47.base
  97.1 0.6 reshape.146.gain
  97.7 54.0 %middle.1 = (bf16[384,2560]{1,0:T(8,128)(2,1)}, f32[2,3,128,512]{3,2,1,0:T(8,128)}, bf16[4,2,3,128,512]{4,3,2,1,0:T(8,128)(2,1)}, bf16[2,3,128,512]{3,2,1,0:T(8,...) custom-call(bf16[2,2,3,128,256]{4,3,2,1,0:T(8,128)(2,1)} %bitcast.43, ...), custom_call_target="tpu_custom_call" | custom-call | tf_op jit(solution)/shard_map/middle/pallas_call | solution.py:726
  151.7 51.2 %return_grads.1 = (f32[6,128,512]{2,1,0:T(8,128)}, f32[32,640]{1,0:T(8,128)}, bf16[2,4,160,256]{3,2,1,0:T(8,128)(2,1)}, bf16[2,384,512]{2,1,0:T(8,128)(2,1)}) custom-call(bf16[4,6,128,512]{3,2,1,0:T(8,128)(2,1)} %bitcast.36, f32[6,128,512]{2,1,0:T(8,128)} %bitcast.40, bf16[2,4,64,640]{3,2,1,0:T(8,128)(2,1)} %get-tuple-element.39.o_mid, ...), custom_call_target="tpu_custom_call" | custom-call | tf_op jit(solution)/shard_map/return_grads/pallas_call | solution.py:1004
  203.0 7.5 %key_grads.1 = (bf16[2,2,4,4,80,256]{5,4,3,2,1,0:T(8,128)(2,1)}, bf16[768,512]{1,0:T(8,128)(2,1)}) custom-call(bf16[2,400,2560]{2,1,0:T(8,128)(2,1)} %get-tuple-element.29.n2.n2_h, f32[768,512]{1,0:T(8,128)} %bitcast.39, f32[3,768,256]{2,1,0:T(8,128)} %get-tuple-element.35.raw, f32[768,128]{1,0:T(8,128)} %bitcast.32, f32[768,128]{1,0:T(8,128)} %bitcast.34, ...), custom_call_target="tpu_custom_call" | custom-call | tf_op jit(solution)/shard_map/key_grads/pallas_call | solution.py:802
  210.4 0.6 broadcast_in_dim.48.gain
  211.0 49.0 %finish.1 = (f32[80,256]{1,0:T(8,128)}, f32[80,256]{1,0:T(8,128)}, bf16[384,2560]{1,0:T(8,128)(2,1)}) custom-call(bf16[2,2,4,4,80,256]{5,4,3,2,1,0:T(8,128)(2,1)} %get-tuple-element.43.gkv, bf16[2,384,512]{2,1,0:T(8,128)(2,1)} %bitcast.42, bf16[2,384,512]{2,1,0:T(8,128)(2,1)} %get-tuple-element.45.dq, bf16[2,4,160,256]{3,2,1,0:T(8,128)(2,1)} %get-tuple-element.46.q_mid, ...), custom_call_target="tpu_custom_call" | custom-call | tf_op jit(solution)/shard_map/finish/pallas_call | solution.py:1167
  260.0 1.6 fusion
  261.6 2.9 %copy.24 = bf16[3,128,2560]{2,1,0:T(8,128)(2,1)} copy(bf16[3,128,2560]{2,1,0:T(8,128)(2,1)} %bitcast.37) | data formatting | bytes 3932160
  264.5 1.3 copy.25
  265.8 0.6 copy.26
  266.4 0.6 copy.27
  (22 shorter events, 0.1 us)
Async XLA Ops:
  0.6 5.0 %copy-start = (bf16[3,128,2560]{2,1,0:T(8,128)(2,1)S(1)}, bf16[3,128,2560]{2,1,0:T(8,128)(2,1)}, u32[]{:S(2)}) copy-start(bf16[3,128,2560]{2,1,0:T(8,128)(2,1)} %param.11) | copy-start | bytes 5898244
  0.6 5.0 %copy-start.4 = (f32[2560]{0:T(1024)S(1)}, f32[2560]{0:T(1024)}, u32[]{:S(2)}) copy-start(f32[2560]{0:T(1024)} %param.14) | copy-start | bytes 30724
  7.6 31.9 %copy-start.6 = (f32[256]{0:T(256)S(1)}, f32[256]{0:T(256)}, u32[]{:S(2)}) copy-start(f32[256]{0:T(256)} %param.20) | copy-start | bytes 3076
  7.6 31.9 %copy-start.7 = (f32[256]{0:T(256)S(1)}, f32[256]{0:T(256)}, u32[]{:S(2)}) copy-start(f32[256]{0:T(256)} %param.19) | copy-start | bytes 3076
  50.2 46.9 %copy-start.5 = (f32[2560]{0:T(1024)S(1)}, f32[2560]{0:T(1024)}, u32[]{:S(2)}) copy-start(f32[2560]{0:T(1024)} %param.21) | copy-start | bytes 30724
  260.0 4.5 %copy-start.1 = (bf16[384,2560]{1,0:T(8,128)(2,1)S(1)}, bf16[384,2560]{1,0:T(8,128)(2,1)}, u32[]{:S(2)}) copy-start(bf16[384,2560]{1,0:T(8,128)(2,1)} %get-tuple-element.48) | copy-start | bytes 5898244
  264.5 1.3 copy-start.3
  264.5 1.9 copy-start.2

commit v3 on v2

--- a/solution.py
+++ b/solution.py
@@ -535,23 +535,25 @@
 
 
 def middle_kernel(
-    q, unit, halo, base, wo_h, tok_h, cot_h, gain, raw_h, cos, sin, gains, n2_h,
-    layer_out, own, parts, qd, o_mid, gq,
-    wo, tok, cot, raw, n2, soft, att, attx, proj, gp2, grad, grad_send, go, o_relay, o_recv,
-    loadsem, asend, arecv, gsend, grecv, dsem, ss, rs,
+    q, unit, halo, base, wo_h, tok_h, cot_h, gain,
+    layer_out, grad, go, soft_h,
+    wo, tok, cot, soft, att, attx, proj, gp2, grad_send,
+    loadsem, keepsem, asend, arecv, gsend, grecv, dsem,
 ):
     y, z, x, j = place()
     partner = dev(y, z, x, 1 - j)
-    yp, ym = dev(up(y), z, x, j), dev(up(y, 3), z, x, j)
     loads = [
         pltpu.make_async_copy(src, dst, loadsem.at[n])
         for n, (src, dst) in enumerate(
-            ((wo_h, wo), (tok_h, tok), (cot_h, cot), (raw_h.at[pl.ds(0, 2)], raw), (n2_h, n2))
+            ((wo_h, wo), (tok_h, tok), (cot_h, cot))
         )
     ]
     for cp in loads:
         cp.start()
-    meet([partner, yp, ym])
+    meet([partner])
+
+    def keep_soft(s):
+        return pltpu.make_async_copy(soft.at[s], soft_h.at[s], keepsem.at[s])
 
     def give_attended(s):
         return remote(att.at[1 - j, s], attx.at[s], asend.at[s], arecv.at[s], partner)
@@ -593,8 +595,9 @@
             out = jnp.dot(weights, values, preferred_element_type=F32).astype(BF16)
             att[:, s, :, 256 * h : 256 * h + 256] = out.reshape(2, 128, 256)
         give_attended(s).start()
-
-    for cp in loads[:3]:
+        keep_soft(s).start()
+
+    for cp in loads:
         cp.wait()
     for s in range(3):
         give_attended(s).wait_recv()
@@ -649,181 +652,48 @@
             mine, gp2[0, :, cols], across, preferred_element_type=F32
         ) + lax.dot_general(other_rows, gp2[1, :, cols], across, preferred_element_type=F32)
         go[n] = term.astype(BF16).reshape(2, 4, 64, 640)
-    o1 = RingReduce(
-        y, yp, ym, go, lambda m: (m,), lambda m, h: (m, h), o_relay, o_recv, ss, rs, ()
-    )
-    o1.start()
-    loads[3].wait()
     give_grad.wait_recv()
-
-    def backward(first, last):
-        @pl.loop(first, last)
-        def _(s):
-            keys = window_of(unit, halo, s, 0, 256)
-            values = window_of(unit, halo, s, 256, 512)
-            grads = jnp.concatenate(
-                [grad[:, s, :, 256 * h : 256 * h + 256].reshape(256, 256) for h in range(2)],
-                axis=0,
-            )
-            weights = soft[s]
-
-            def emit(part, first_col):
-                for n, d in enumerate((4, 3, 2, 1, 0)):
-                    for i in range(2):
-                        piece = part[256 * n + 128 * i : 256 * n + 128 * i + 128]
-                        if d == 0:
-                            own[i, s, :, first_col : first_col + 256] = piece
-                        else:
-                            parts[d - 1, i, s, :, first_col : first_col + 256] = piece.astype(BF16)
-
-            emit(lax.dot_general(weights, grads, across, preferred_element_type=F32), 256)
-            grad_weights = lax.dot_general(
-                grads, values, (((1,), (1,)), ((), ())), preferred_element_type=F32
-            )
-            wide = weights.astype(F32)
-            moved = wide * grad_weights
-            dots = jnp.sum(moved, axis=-1, keepdims=True)
-            score_grads = (moved - wide * dots).astype(BF16)
-            grad_queries = jnp.dot(score_grads, keys, preferred_element_type=F32)
-            queries = jnp.concatenate(
-                [q[h, :, s].reshape(256, 256) for h in range(2)], axis=0
-            )
-            emit(lax.dot_general(score_grads, queries, across, preferred_element_type=F32), 0)
-            c, sn = cos[:, s].reshape(256, 128), sin[:, s].reshape(256, 128)
-            for h in range(2):
-                back = map_back(
-                    grad_queries[256 * h : 256 * h + 256],
-                    raw[h, :, s].reshape(256, 256),
-                    c,
-                    sn,
-                    gains[0:1, :],
-                    Q_FACTOR,
-                )
-                qd[:, s, :, 256 * h : 256 * h + 256] = back.astype(BF16).reshape(2, 128, 256)
-
-    backward(0, 2)
-    o1.forward()
-    backward(2, 3)
-    loads[4].wait()
-
-    @pl.loop(0, 4)
-    def _(n):
-        rows = n2[:, :ROWS, pl.ds(pl.multiple_of(640 * n, 128), 640)].reshape(2 * ROWS, 640)
-        for h in range(2):
-            deltas = qd[:, :, :, 256 * h : 256 * h + 256].reshape(2 * ROWS, 256)
-            term = lax.dot_general(rows, deltas, across, preferred_element_type=F32)
-            gq[h, n] = term.astype(BF16).reshape(4, 160, 256)
-
-    o_mid[...] = o1.finish().astype(BF16)
-    o1.drain()
     for s in range(3):
         give_attended(s).wait_send()
         give_projected(s).wait_send()
+        keep_soft(s).wait()
     give_grad.wait_send()
 
 
-def middle(q, unit, halo, base, wo, tok, cot, gain, raw, cos, sin, gains, n2):
+def middle(q, unit, halo, base, wo, tok, cot, gain):
     return comm_call(
         middle_kernel,
         "middle",
         4,
         (
             sds((ROWS, D), BF16),
-            sds((2, 3, 128, 512), F32),
-            sds((4, 2, 3, 128, 512), BF16),
             sds((2, 3, 128, 512), BF16),
-            sds((2, 4, 64, 640), BF16),
-            sds((2, 4, 4, 160, 256), BF16),
+            sds((4, 2, 4, 64, 640), BF16),
+            sds((3, 512, KEYS), BF16),
         ),
         [
             pltpu.VMEM((1024, D), BF16),
             pltpu.VMEM((ROWS, D), BF16),
             pltpu.VMEM((ROWS, D), BF16),
-            pltpu.VMEM((2, 2, 3, 128, 256), F32),
-            pltpu.VMEM((2, ROWS + NOTE_ROWS, D), BF16),
             pltpu.VMEM((3, 512, KEYS), BF16),
             pltpu.VMEM((2, 3, 128, 512), BF16),
             pltpu.VMEM((3, 128, 512), BF16),
             pltpu.VMEM((ROWS, D), F32),
             pltpu.VMEM((2, ROWS, D), BF16),
-            pltpu.VMEM((2, 3, 128, 512), BF16),
             pltpu.VMEM((3, 128, 512), BF16),
-            pltpu.VMEM((4, 2, 4, 64, 640), BF16),
-            pltpu.VMEM((2, 4, 64, 640), BF16),
-            pltpu.VMEM((2, 2, 4, 64, 640), BF16),
-            DMA((5,)),
+            DMA((3,)),
+            DMA((3,)),
             DMA((3,)),
             DMA((3,)),
             DMA((3,)),
             DMA((3,)),
             DMA((2,)),
-            DMA((4,)),
-            DMA((4,)),
         ],
-        "vvvvhhhvhvvvh",
-        "vvvvvv",
-    )(
-        q.reshape(2, 2, 3, 128, 256),
-        unit,
-        halo,
-        base,
-        wo,
-        tok,
-        cot,
-        gain,
-        raw.reshape(3, 2, 3, 128, 256),
-        cos.reshape(2, 3, 128, 128),
-        sin.reshape(2, 3, 128, 128),
-        gains,
-        n2,
-    )
-
-
-def key_grads_kernel(n2, total, raw, cos, sin, gains, gkv, kvd):
-    @pl.when(pl.program_id(0) == 0)
-    def _():
-        kd = map_back(total[:, :256], raw[0], cos[...], sin[...], gains[1:2, :], 1.0)
-        kvd[:, :256] = kd.astype(BF16)
-        kvd[:, 256:] = total[:, 256:].astype(BF16)
-
-    rows = n2[:, :ROWS, :].reshape(2 * ROWS, 640)
-    for half in range(2):
-        rhs = jnp.concatenate(
-            [kvd[:, 128 * half : 128 * half + 128], kvd[:, 256 + 128 * half : 384 + 128 * half]],
-            axis=-1,
-        )
-        term = lax.dot_general(rows, rhs, (((0,), (0,)), ((), ())), preferred_element_type=F32)
-        term = term.astype(BF16).reshape(4, 2, 80, 256)
-        for i in range(2):
-            gkv[i, half, 0] = term[:, i]
-
-
-def key_grads(n2, total, raw, cos, sin, gains):
-    return pl.pallas_call(
-        key_grads_kernel,
-        name="key_grads",
-        grid=(4,),
-        in_specs=[
-            pl.BlockSpec((2, ROWS + NOTE_ROWS, 640), lambda n: (0, 0, n)),
-            pl.BlockSpec((2 * ROWS, 512), lambda n: (0, 0)),
-            pl.BlockSpec((1, 2 * ROWS, 256), lambda n: (2, 0, 0)),
-            pl.BlockSpec((2 * ROWS, 128), lambda n: (0, 0)),
-            pl.BlockSpec((2 * ROWS, 128), lambda n: (0, 0)),
-            pl.BlockSpec((8, 256), lambda n: (0, 0)),
-        ],
-        out_specs=[
-            pl.BlockSpec((2, 2, 1, 4, 80, 256), lambda n: (0, 0, n, 0, 0, 0)),
-            pl.BlockSpec((2 * ROWS, 512), lambda n: (0, 0)),
-        ],
-        out_shape=[
-            sds((2, 2, 4, 4, 80, 256), BF16),
-            sds((2 * ROWS, 512), BF16),
-        ],
-        compiler_params=pltpu.CompilerParams(vmem_limit_bytes=VMEM_LIMIT),
-    )(n2, total, raw, cos, sin, gains)
-
-
-CHUNKS = 6
+        "vvvvhhhv",
+        "vvvh",
+    )(q.reshape(2, 2, 3, 128, 256), unit, halo, base, wo, tok, cot, gain)
+
+
 EVERY = slice(None)
 
 
@@ -859,344 +729,491 @@
     )
 
 
-def return_kernel(
-    parts, own, o_mid, gq, qd,
-    total, oo, q_mid, dq,
-    relay, near, after, relayed, summed, bsum,
-    o_relay2, o_recv2, o_end, o_land, q_relay, q_recv,
-    ssem, rsem, ss, rs, ls, lr, lc, dsem,
+TAIL = dict(
+    own=((2, 3, 128, 512), F32),
+    parts=((4, 2, 3, 128, 512), BF16),
+    qd=((2, 3, 128, 512), BF16),
+    dq=((3, 128, 512), BF16),
+    kvd=((2, 3, 128, 512), BF16),
+    dkv=((3, 128, 512), BF16),
+    n2=((2, ROWS + NOTE_ROWS, D), BF16),
+    raw_k=((2, 3, 128, 256), F32),
+    gq=((2, 4, 4, 160, 256), BF16),
+    gkv=((2, 2, 4, 4, 80, 256), BF16),
+    relay=((2, 2, 3, 128, 512), BF16),
+    near=((2, 2, 3, 128, 512), BF16),
+    after=((2, 3, 128, 512), BF16),
+    go=((4, 2, 4, 64, 640), BF16),
+    o_relay=((2, 4, 64, 640), BF16),
+    o_recv=((2, 2, 4, 64, 640), BF16),
+    o_mid=((2, 4, 64, 640), BF16),
+    o_relay2=((2, 64, 640), BF16),
+    o_recv2=((2, 2, 64, 640), BF16),
+    o_end=((2, 64, 640), BF16),
+    o_land=((4, 32, 640), BF16),
+    q_relay=((2, 4, 160, 256), BF16),
+    q_recv=((2, 2, 4, 160, 256), BF16),
+    q_mid=((2, 4, 160, 256), BF16),
+    q_relay2=((2, 160, 256), BF16),
+    q_recv2=((2, 2, 160, 256), BF16),
+    q_end=((2, 160, 256), BF16),
+    q_land=((4, 80, 256), BF16),
+    k_relay=((2, 2, 4, 80, 256), BF16),
+    k_recv=((2, 2, 2, 4, 80, 256), BF16),
+    k_mid=((2, 2, 4, 80, 256), BF16),
+    k_relay2=((2, 2, 80, 256), BF16),
+    k_recv2=((2, 2, 2, 80, 256), BF16),
+    k_end=((2, 2, 80, 256), BF16),
+    k_land=((4, 80, 256), BF16),
+)
+TAIL_SEMS = dict(
+    ssem=(5, 2, 3),
+    rsem=(5, 2, 3),
+    dsend=(2, 3),
+    drecv=(2, 3),
+    ss=(4, 2, 4),
+    rs=(4, 2, 4),
+    ls=(3, 4),
+    lr=(3, 4),
+    lc=(3,),
+    load=(16,),
+    keep=(3,),
+    put=(2,),
+)
+
+
+def tail_kernel(
+    q_h, unit_h, halo_h, soft_h, grad_h, raw_h, cos, sin, gains, go_h, n2_h,
+    w_h, wother_h, tok_h, cot_h, gain,
+    oo, oq, okv, out_h,
+    *scratch,
 ):
+    names = list(TAIL) + list(TAIL_SEMS)
+    b = dict(zip(names, scratch))
+    own, parts, qd, kvd = b["own"], b["parts"], b["qd"], b["kvd"]
+    relay, near, after = b["relay"], b["near"], b["after"]
+    ssem, rsem, ss, rs, load = b["ssem"], b["rsem"], b["ss"], b["rs"], b["load"]
     y, z, x, j = place()
     partner = dev(y, z, x, 1 - j)
     xp, xm = dev(y, z, up(x), j), dev(y, z, up(x, 3), j)
     zp, zm = dev(y, up(z), x, j), dev(y, up(z, 3), x, j)
+    yp, ym = dev(up(y), z, x, j), dev(up(y, 3), z, x, j)
+    yfar = [dev(up(y, r), z, x, i) for r in (1, 2, 3) for i in (0, 1)]
     zfar = [dev(y, up(z, r), x, i) for r in (1, 2, 3) for i in (0, 1)]
-    keep = pltpu.make_async_copy(qd.at[j], dq.at[0], dsem.at[0])
-    keep.start()
-    meet([partner, xp, xm] + zfar)
     inner = jnp.logical_and(x > 0, x < 3)
     low = x < 2
-
-    def relay_left(k):
-        return remote(parts.at[1, k], relay.at[0, k], ssem.at[0, k], rsem.at[0, k], xm)
-
-    def relay_right(k):
-        return remote(parts.at[1, k], relay.at[1, k], ssem.at[1, k], rsem.at[1, k], xp)
-
-    def to_left(src, k):
-        return remote(src.at[k], near.at[0, k], ssem.at[2, k], rsem.at[2, k], xm)
-
-    def to_right(src, k):
-        return remote(src.at[k], near.at[1, k], ssem.at[3, k], rsem.at[3, k], xp)
-
-    def back(k):
-        return remote(bsum.at[k], after.at[k], ssem.at[4, k], rsem.at[4, k], zm)
-
+    across = (((0,), (0,)), ((), ()))
+    apart = (((1,), (1,)), ((), ()))
+
+    def get(src, dst, n):
+        return pltpu.make_async_copy(src, dst, load.at[n])
+
+    def relay_left(i, s):
+        return remote(parts.at[1, i, s], relay.at[0, i, s], ssem.at[0, i, s], rsem.at[0, i, s], xm)
+
+    def relay_right(i, s):
+        return remote(parts.at[1, i, s], relay.at[1, i, s], ssem.at[1, i, s], rsem.at[1, i, s], xp)
+
+    def to_left(i, s):
+        return remote(parts.at[0, i, s], near.at[0, i, s], ssem.at[2, i, s], rsem.at[2, i, s], xm)
+
+    def to_right(i, s):
+        return remote(parts.at[2, i, s], near.at[1, i, s], ssem.at[3, i, s], rsem.at[3, i, s], xp)
+
+    def back(i, s):
+        return remote(parts.at[3, i, s], after.at[i, s], ssem.at[4, i, s], rsem.at[4, i, s], zm)
+
+    def give_delta(f, s):
+        src, dst = ((qd, b["dq"]), (kvd, b["dkv"]))[f]
+        return remote(
+            src.at[1 - j, s], dst.at[s], b["dsend"].at[f, s], b["drecv"].at[f, s], partner
+        )
+
+    rows_whole, rows_half = lambda m: (EVERY, m), lambda m, h: (h, m)
+    o1 = RingReduce(
+        y, yp, ym, b["go"], lambda m: (m,), lambda m, h: (m, h),
+        b["o_relay"], b["o_recv"], ss, rs, (0, 0),
+    )
+    o2 = RingReduce(
+        x, xp, xm, b["o_mid"], rows_whole, rows_half, b["o_relay2"], b["o_recv2"], ss, rs, (0, 1)
+    )
     q1 = RingReduce(
-        z, zp, zm, gq, lambda m: (EVERY, m), lambda m, h: (h, m), q_relay, q_recv, ss, rs, (0,)
-    )
-    o2 = RingReduce(
-        x, xp, xm, o_mid, lambda m: (EVERY, m), lambda m, h: (h, m),
-        o_relay2, o_recv2, ss, rs, (1,),
-    )
-
-    q1.start()
-    o2.start()
-
-    @pl.loop(0, CHUNKS)
-    def _(k):
-        @pl.when(low)
-        def _():
-            relay_right(k).start()
-
-        @pl.when(jnp.logical_not(low))
-        def _():
-            relay_left(k).start()
-
-        @pl.when(jnp.logical_not(inner))
-        def _():
-            to_left(parts.at[0], k).start()
-            to_right(parts.at[2], k).start()
-
-    give = remote(qd.at[1 - j], dq.at[1], dsem.at[1], dsem.at[2], partner)
-    give.start()
-
-    def relay_step(first, last):
+        z, zp, zm, b["gq"], rows_whole, rows_half, b["q_relay"], b["q_recv"], ss, rs, (1, 0)
+    )
+    q2 = RingReduce(
+        x, xp, xm, b["q_mid"], rows_whole, rows_half, b["q_relay2"], b["q_recv2"], ss, rs, (1, 1)
+    )
+    k1, k2 = [], []
+    for f in range(2):
+        first, second = ((z, zp, zm), (x, xp, xm))[:: 1 - 2 * f]
+        if f == 0:
+            pick, half = rows_whole, rows_half
+        else:
+            pick, half = lambda m: (EVERY, EVERY, m), lambda m, h: (h, EVERY, m)
+        k1.append(
+            RingReduce(
+                *first, b["gkv"].at[f], pick, half,
+                b["k_relay"].at[f], b["k_recv"].at[f], ss, rs, (2 + f, 0),
+            )
+        )
+        k2.append(
+            RingReduce(
+                *second, b["k_mid"].at[f], rows_whole, rows_half,
+                b["k_relay2"].at[f], b["k_recv2"].at[f], ss, rs, (2 + f, 1),
+            )
+        )
+
+    def attention(q, unit, halo, soft, grad, raw):
+        loads = [
+            get(go_h, b["go"], 0),
+            get(unit_h, unit, 1),
+            get(halo_h, halo, 2),
+            get(q_h, q, 3),
+            get(grad_h, grad, 4),
+            get(raw_h.at[pl.ds(0, 2)], raw, 5),
+        ]
+
+        def get_soft(s):
+            return pltpu.make_async_copy(soft_h.at[s], soft.at[s], b["keep"].at[s])
+
+        for cp in loads:
+            cp.start()
+        for s in range(3):
+            get_soft(s).start()
+        get(n2_h, b["n2"], 6).start()
+        get(raw_h.at[2], b["raw_k"], 7).start()
+        meet([partner, xp, xm] + yfar + zfar)
+        loads[0].wait()
+        o1.start()
+        for cp in loads[1:]:
+            cp.wait()
+
+        def backward(first, last):
+            @pl.loop(first, last)
+            def _(s):
+                get_soft(s).wait()
+                keys = window_of(unit, halo, s, 0, 256)
+                values = window_of(unit, halo, s, 256, 512)
+                grads = jnp.concatenate(
+                    [grad[:, s, :, 256 * h : 256 * h + 256].reshape(256, 256) for h in range(2)],
+                    axis=0,
+                )
+                weights = soft[s]
+
+                def emit(part, first_col):
+                    for n, d in enumerate((4, 3, 2, 1, 0)):
+                        for i in range(2):
+                            piece = part[256 * n + 128 * i : 256 * n + 128 * i + 128]
+                            cols = slice(first_col, first_col + 256)
+                            if d == 0:
+                                own[i, s, :, cols] = piece
+                            else:
+                                parts[d - 1, i, s, :, cols] = piece.astype(BF16)
+
+                emit(lax.dot_general(weights, grads, across, preferred_element_type=F32), 256)
+                grad_weights = lax.dot_general(
+                    grads, values, apart, preferred_element_type=F32
+                )
+                wide = weights.astype(F32)
+                moved = wide * grad_weights
+                dots = jnp.sum(moved, axis=-1, keepdims=True)
+                score_grads = (moved - wide * dots).astype(BF16)
+                queries = jnp.concatenate(
+                    [q[h, :, s].reshape(256, 256) for h in range(2)], axis=0
+                )
+                emit(
+                    lax.dot_general(score_grads, queries, across, preferred_element_type=F32), 0
+                )
+                for i in range(2):
+
+                    @pl.when(low)
+                    def _():
+                        relay_right(i, s).start()
+
+                    @pl.when(jnp.logical_not(low))
+                    def _():
+                        relay_left(i, s).start()
+
+                    @pl.when(jnp.logical_not(inner))
+                    def _():
+                        to_left(i, s).start()
+                        to_right(i, s).start()
+
+                grad_queries = jnp.dot(score_grads, keys, preferred_element_type=F32)
+                c, sn = cos[:, s].reshape(256, 128), sin[:, s].reshape(256, 128)
+                for h in range(2):
+                    turned = map_back(
+                        grad_queries[256 * h : 256 * h + 256],
+                        raw[h, :, s].reshape(256, 256),
+                        c,
+                        sn,
+                        gains[0:1, :],
+                        Q_FACTOR,
+                    )
+                    qd[:, s, :, 256 * h : 256 * h + 256] = turned.astype(BF16).reshape(2, 128, 256)
+                give_delta(0, s).start()
+
+        backward(0, 2)
+        o1.forward()
+        backward(2, 3)
+
+    pl.run_scoped(
+        attention,
+        pltpu.VMEM((2, 2, 3, 128, 256), BF16),
+        pltpu.VMEM((UNIT, 512), BF16),
+        pltpu.VMEM((4, UNIT, 512), BF16),
+        pltpu.VMEM((3, 512, KEYS), BF16),
+        pltpu.VMEM((2, 3, 128, 512), BF16),
+        pltpu.VMEM((2, 2, 3, 128, 256), F32),
+    )
+
+    def relay_step(s):
         @pl.when(inner)
         def _():
-            @pl.loop(first, last)
-            def _(k):
-                relay_left(k).wait_recv()
-                relayed[0, k] = (parts[0, k].astype(F32) + relay[0, k].astype(F32)).astype(BF16)
-                to_left(relayed.at[0], k).start()
-                relay_right(k).wait_recv()
-                relayed[1, k] = (parts[2, k].astype(F32) + relay[1, k].astype(F32)).astype(BF16)
-                to_right(relayed.at[1], k).start()
-
-    def near_step(first, last):
-        @pl.loop(first, last)
-        def _(k):
-            to_left(parts.at[0], k).wait_recv()
-            to_right(parts.at[2], k).wait_recv()
-            from_right = near[0, k].astype(F32)
-            from_left = near[1, k].astype(F32)
+            for i in range(2):
+                relay_left(i, s).wait_recv()
+                add_into(parts, (0, i, s), relay[0, i, s])
+                to_left(i, s).start()
+                relay_right(i, s).wait_recv()
+                add_into(parts, (2, i, s), relay[1, i, s])
+                to_right(i, s).start()
+
+    def near_step(s):
+        for i in range(2):
+            to_left(i, s).wait_recv()
+            to_right(i, s).wait_recv()
+            from_right = near[0, i, s].astype(F32)
+            from_left = near[1, i, s].astype(F32)
             zero = jnp.zeros_like(from_left)
             near_a = jnp.where(x < 3, from_right, zero) + jnp.where(x == 0, from_left, zero)
             near_b = jnp.where(x == 3, from_right, zero) + jnp.where(x > 0, from_left, zero)
-            summed[k] = near_a
-            bsum[k] = (parts[3, k].astype(F32) + near_b).astype(BF16)
-            back(k).start()
-
-    relay_step(0, 2)
-    q1.forward()
-    relay_step(2, 4)
-    o2.forward()
-    relay_step(4, CHUNKS)
-    near_step(0, 3)
-    q_mid[...] = q1.finish().astype(BF16)
-    near_step(3, CHUNKS)
-
-    o_end[...] = o2.finish().astype(BF16)
-    o_sends = []
-    for h in range(2):
+            add_into(parts, (3, i, s), near_b)
+            back(i, s).start()
+            own[i, s] = own[i, s] + near_a
+
+    def total_step(s):
         for i in range(2):
-            goal = 2 * j + h
-            o_sends.append(
-                (
-                    o_end.at[h, pl.ds(32 * i, 32)],
-                    z,
-                    dev(y, goal, x, i),
-                    jnp.logical_and(goal == z, i == j),
-                )
+            back(i, s).wait_recv()
+            total = own[i, s] + after[i, s].astype(F32)
+            kd = map_back(
+                total[:, :256], b["raw_k"][i, s], cos[i, s], sin[i, s], gains[1:2, :], 1.0
             )
-    send_last(o_end, o_land, o_sends, ls, lr, lc, True)
-
-    @pl.loop(0, CHUNKS)
-    def _(k):
-        back(k).wait_recv()
-        total[k] = own[k] + summed[k] + after[k].astype(F32)
-
-    send_last(o_end, o_land, o_sends, ls, lr, lc, False)
-    sum_last(o_end.at[0, pl.ds(0, 32)], o_land, ls, lr, z, lax.div(z, 2) == j, partner, oo)
-
-    @pl.loop(0, CHUNKS)
-    def _(k):
-        @pl.when(low)
-        def _():
-            relay_right(k).wait_send()
-
-        @pl.when(jnp.logical_not(low))
-        def _():
-            relay_left(k).wait_send()
-
-        to_left(parts.at[0], k).wait_send()
-        to_right(parts.at[2], k).wait_send()
-        back(k).wait_send()
-
-    for ring in (q1, o2):
+            kvd[i, s, :, 0:256] = kd.astype(BF16)
+            kvd[i, s, :, 256:512] = total[:, 256:].astype(BF16)
+        give_delta(1, s).start()
+
+    def rows_of(zz):
+        cols = pl.ds(pl.multiple_of(640 * zz, 128), 640)
+        return b["n2"][:, :ROWS, cols].reshape(2 * ROWS, 640)
+
+    def query_terms(zz):
+        rows = rows_of(zz)
+        for h in range(2):
+            deltas = qd[:, :, :, 256 * h : 256 * h + 256].reshape(2 * ROWS, 256)
+            term = lax.dot_general(rows, deltas, across, preferred_element_type=F32)
+            b["gq"][h, zz] = term.astype(BF16).reshape(4, 160, 256)
+
+    def key_terms(zz):
+        rows = rows_of(zz)
+        for h in range(2):
+            deltas = jnp.concatenate(
+                [
+                    kvd[:, :, :, 128 * h : 128 * h + 128],
+                    kvd[:, :, :, 256 + 128 * h : 384 + 128 * h],
+                ],
+                axis=-1,
+            ).reshape(2 * ROWS, 256)
+            term = lax.dot_general(rows, deltas, across, preferred_element_type=F32)
+            term = term.astype(BF16).reshape(4, 2, 80, 256)
+            for i in range(2):
+                b["gkv"][i, h, zz] = term[:, i]
+
+    def owners(end, rows, at_y):
+        sends = []
+        for h in range(2):
+            for i in range(2):
+                goal = 2 * j + h
+                here = jnp.logical_and(goal == (y if at_y else z), i == j)
+                device = dev(goal, z, x, i) if at_y else dev(y, goal, x, i)
+                sends.append((end.at[h, pl.ds(rows * i, rows)], y if at_y else z, device, here))
+        return sends
+
+    def rest(w_buf, tok, cot, acc):
+        def get_weights(first):
+            return [
+                get(w_h.at[pl.ds(first, 4)], w_buf.at[0], 8),
+                get(wother_h.at[pl.ds(first, 4)], w_buf.at[1], 9),
+            ]
+
+        side = get_weights(0) + [get(tok_h, tok, 10), get(cot_h, cot, 11)]
+        for cp in side:
+            cp.start()
+
+        def tiles(first, last, mine, other, fresh):
+            @pl.loop(first, last)
+            def _(n):
+                total = None
+                for half, lhs in enumerate((mine, other)):
+                    rhs = jnp.concatenate(
+                        [w_buf[half, m, rows_at(512 * n, 512), :] for m in range(4)], axis=-1
+                    )
+                    term = lax.dot_general(lhs, rhs, apart, preferred_element_type=F32)
+                    total = term if total is None else total + term
+                acc[n] = total if fresh else acc[n] + total
+
+        def norm_rows(part):
+            @pl.loop(12 * part, 12 * part + 12)
+            def _(k):
+                at = rows_at(k * 16, 16)
+                t = tok[at, :].astype(F32)
+                grad = jnp.concatenate([acc[m, at, :] for m in range(5)], axis=-1)
+                h = grad * gain[...]
+                scale = lax.rsqrt(jnp.mean(t * t, axis=-1, keepdims=True) + EPS)
+                middle = jnp.mean(h * t, axis=-1, keepdims=True)
+                turned = scale * h - t * (scale * scale * scale * middle)
+                cot[at, :] = (cot[at, :].astype(F32) + turned).astype(BF16)
+
+            at = pl.ds(192 * part, 192)
+            cp = pltpu.make_async_copy(cot.at[at], out_h.at[at], b["put"].at[part])
+            cp.start()
+            return cp
+
+        relay_step(0)
+        get(n2_h, b["n2"], 6).wait()
+        query_terms(up(z, 2))
+        q1.start()
+        relay_step(1)
+        query_terms(up(z, 1))
+        query_terms(up(z, 3))
+        relay_step(2)
+        query_terms(z)
+        for cp in side[:2]:
+            cp.wait()
+        for s in range(3):
+            give_delta(0, s).wait_recv()
+        tiles(0, 5, qd[j].reshape(ROWS, 512), b["dq"][...].reshape(ROWS, 512), True)
+        later = get_weights(4)
+        for cp in later:
+            cp.start()
+        q1.forward()
+        b["o_mid"][...] = o1.finish().astype(BF16)
+        o2.start()
+        near_step(0)
+        near_step(1)
+        near_step(2)
+        o2.forward()
+        get(raw_h.at[2], b["raw_k"], 7).wait()
+        total_step(0)
+        total_step(1)
+        b["q_mid"][...] = q1.finish().astype(BF16)
+        q2.start()
+        total_step(2)
+        key_terms(up(z, 2))
+        k1[0].start()
+        key_terms(up(z, 1))
+        key_terms(up(z, 3))
+        q2.forward()
+        key_terms(z)
+        k1[1].start()
+        b["o_end"][...] = o2.finish().astype(BF16)
+        o_sends = owners(b["o_end"], 32, False)
+        send_last(b["o_end"], b["o_land"], o_sends, b["ls"].at[0], b["lr"].at[0], b["lc"].at[0], True)
+        k1[0].forward()
+        for cp in later:
+            cp.wait()
+        for s in range(3):
+            give_delta(1, s).wait_recv()
+        kv_mine, kv_other = kvd[j].reshape(ROWS, 512), b["dkv"][...].reshape(ROWS, 512)
+        tiles(0, 3, kv_mine, kv_other, False)
+        k1[1].forward()
+        b["q_end"][...] = q2.finish().astype(BF16)
+        q_sends = owners(b["q_end"], 80, True)
+        send_last(b["q_end"], b["q_land"], q_sends, b["ls"].at[1], b["lr"].at[1], b["lc"].at[1], True)
+        tiles(3, 5, kv_mine, kv_other, False)
+        for cp in side[2:]:
+            cp.wait()
+        b["k_mid"][0] = k1[0].finish().astype(BF16)
+        k2[0].start()
+        puts = [norm_rows(0)]
+        b["k_mid"][1] = k1[1].finish().astype(BF16)
+        k2[1].start()
+        k2[0].forward()
+        puts.append(norm_rows(1))
+        k2[1].forward()
+        k_sends = []
+        for f in range(2):
+            b["k_end"][f] = k2[f].finish().astype(BF16)
+            for h in range(2):
+                goal = 2 * j + h
+                here = jnp.logical_and(goal == y, f == j)
+                k_sends.append((b["k_end"].at[f, h], y, dev(goal, z, x, f), here))
+        send_last(b["k_end"], b["k_land"], k_sends, b["ls"].at[2], b["lr"].at[2], b["lc"].at[2], True)
+        flows = (
+            (o_sends, b["o_end"].at[0, pl.ds(0, 32)], b["o_end"], b["o_land"], z, oo),
+            (q_sends, b["q_end"].at[0, pl.ds(0, 80)], b["q_end"], b["q_land"], y, oq),
+            (k_sends, b["k_end"].at[0, 0], b["k_end"], b["k_land"], y, okv),
+        )
+        for n, (sends, like, end, land, me, out) in enumerate(flows):
+            ls, lr, lc = b["ls"].at[n], b["lr"].at[n], b["lc"].at[n]
+            send_last(end, land, sends, ls, lr, lc, False)
+            sum_last(like, land, ls, lr, me, lax.div(me, 2) == j, partner, out)
+        for cp in puts:
+            cp.wait()
+
+    pl.run_scoped(
+        rest,
+        pltpu.VMEM((2, 4, D, 128), BF16),
+        pltpu.VMEM((ROWS, D), BF16),
+        pltpu.VMEM((ROWS, D), BF16),
+        pltpu.VMEM((5, ROWS, 512), F32),
+    )
+    for s in range(3):
+        for i in range(2):
+
+            @pl.when(low)
+            def _():
+                relay_right(i, s).wait_send()
+
+            @pl.when(jnp.logical_not(low))
+            def _():
+                relay_left(i, s).wait_send()
+
+            to_left(i, s).wait_send()
+            to_right(i, s).wait_send()
+            back(i, s).wait_send()
+        for f in range(2):
+            give_delta(f, s).wait_send()
+    for ring in [o1, o2, q1, q2] + k1 + k2:
         ring.drain()
-    keep.wait()
-    give.wait()
-
-
-def return_grads(parts, own, o_mid, gq, qd):
-    block = (CHUNKS, 128, 512)
+
+
+def tail(q, unit, halo, soft, grad, raw, cos, sin, gains, go, n2, w, wother, tok, cot, gain):
     return comm_call(
-        return_kernel,
-        "return_grads",
+        tail_kernel,
+        "tail",
         2,
-        (
-            sds(block, F32),
-            sds((32, 640), F32),
-            sds((2, 4, 160, 256), BF16),
-            sds((2, ROWS, 512), BF16),
-        ),
-        [
-            pltpu.VMEM((2,) + block, BF16),
-            pltpu.VMEM((2,) + block, BF16),
-            pltpu.VMEM(block, BF16),
-            pltpu.VMEM((2,) + block, BF16),
-            pltpu.VMEM(block, F32),
-            pltpu.VMEM(block, BF16),
-            pltpu.VMEM((2, 64, 640), BF16),
-            pltpu.VMEM((2, 2, 64, 640), BF16),
-            pltpu.VMEM((2, 64, 640), BF16),
-            pltpu.VMEM((4, 32, 640), BF16),
-            pltpu.VMEM((2, 4, 160, 256), BF16),
-            pltpu.VMEM((2, 2, 4, 160, 256), BF16),
-            DMA((5, CHUNKS)),
-            DMA((5, CHUNKS)),
-            DMA((2, 4)),
-            DMA((2, 4)),
-            DMA((4,)),
-            DMA((4,)),
-            DMA(()),
-            DMA((3,)),
-        ],
-        "vvvvv",
-        "vvvv",
-    )(parts.reshape((4,) + block), own.reshape(block), o_mid, gq, qd)
-
-
-def finish_kernel(
-    gkv, kvd, dq, q_mid, w, wother, tok, cot, gain,
-    okv, oq, out,
-    dkv, w_buf, tok_buf, cot_buf, acc,
-    relay, recv, mid, relay2, recv2, end, land, q_relay, q_recv, q_end, q_land,
-    ss, rs, ls, lr, lc, dsem, msem,
-):
-    y, z, x, j = place()
-    partner = dev(y, z, x, 1 - j)
-    xp, xm = dev(y, z, up(x), j), dev(y, z, up(x, 3), j)
-    zp, zm = dev(y, up(z), x, j), dev(y, up(z, 3), x, j)
-    yfar = [dev(up(y, r), z, x, i) for r in (1, 2, 3) for i in (0, 1)]
-    loads = [
-        pltpu.make_async_copy(kvd.at[j], dkv.at[0], msem.at[0]),
-        pltpu.make_async_copy(w, w_buf.at[0], msem.at[1]),
-        pltpu.make_async_copy(wother, w_buf.at[1], msem.at[2]),
-        pltpu.make_async_copy(tok, tok_buf, msem.at[3]),
-        pltpu.make_async_copy(cot, cot_buf, msem.at[4]),
-    ]
-    for cp in loads:
-        cp.start()
-    meet([partner, xp, xm, zp, zm] + yfar)
-    firsts, seconds = [], []
-    for f in range(2):
-        on_z, on_x = (z, zp, zm), (x, xp, xm)
-        a, b = (on_z, on_x) if f == 0 else (on_x, on_z)
-        if f == 0:
-            pick, half = lambda m: (EVERY, m), lambda m, h: (h, m)
-        else:
-            pick, half = lambda m: (EVERY, EVERY, m), lambda m, h: (h, EVERY, m)
-        firsts.append(
-            RingReduce(*a, gkv.at[f], pick, half, relay.at[f], recv.at[f], ss, rs, (f, 0))
-        )
-        seconds.append(
-            RingReduce(
-                *b, mid.at[f], lambda m: (EVERY, m), lambda m, h: (h, m),
-                relay2.at[f], recv2.at[f], ss, rs, (f, 1),
-            )
-        )
-    q2 = RingReduce(
-        x, xp, xm, q_mid, lambda m: (EVERY, m), lambda m, h: (h, m), q_relay, q_recv, ss, rs, (2, 0)
-    )
-    give = remote(kvd.at[1 - j], dkv.at[1], dsem.at[0], dsem.at[1], partner)
-    give.start()
-    q2.start()
-    for ring in firsts:
-        ring.start()
-    for cp in loads:
-        cp.wait()
-    give.wait_recv()
-
-    def tiles(first, last):
-        @pl.loop(first, last)
-        def _(n):
-            total = None
-            for half in range(2):
-                lhs = jnp.concatenate([dq[half], dkv[half]], axis=-1)
-                rhs = jnp.concatenate(
-                    [w_buf[half, b, rows_at(512 * n, 512), :] for b in range(8)], axis=-1
-                )
-                term = lax.dot_general(
-                    lhs, rhs, (((1,), (1,)), ((), ())), preferred_element_type=F32
-                )
-                total = term if total is None else total + term
-            acc[n] = total
-
-    def norm_rows(first, last):
-        @pl.loop(first, last)
-        def _(k):
-            at = rows_at(k * 16, 16)
-            t = tok_buf[at, :].astype(F32)
-            grad = jnp.concatenate([acc[m, at, :] for m in range(5)], axis=-1)
-            h = grad * gain[...]
-            scale = lax.rsqrt(jnp.mean(t * t, axis=-1, keepdims=True) + EPS)
-            inner = jnp.mean(h * t, axis=-1, keepdims=True)
-            back = scale * h - t * (scale * scale * scale * inner)
-            out[at, :] = (cot_buf[at, :].astype(F32) + back).astype(BF16)
-
-    tiles(0, 1)
-    q2.forward()
-    tiles(1, 2)
-    for ring in firsts:
-        ring.forward()
-    tiles(2, 4)
-    q_end[...] = q2.finish().astype(BF16)
-    q_sends = []
-    for h in range(2):
-        for i in range(2):
-            goal = 2 * j + h
-            q_sends.append(
-                (
-                    q_end.at[h, pl.ds(80 * i, 80)],
-                    y,
-                    dev(goal, z, x, i),
-                    jnp.logical_and(goal == y, i == j),
-                )
-            )
-    send_last(q_end, q_land, q_sends, ls.at[1], lr.at[1], lc.at[1], True)
-    tiles(4, 5)
-    for f in range(2):
-        mid[f] = firsts[f].finish().astype(BF16)
-        seconds[f].start()
-    norm_rows(0, 12)
-    for ring in seconds:
-        ring.forward()
-    norm_rows(12, 24)
-    sends = []
-    for f in range(2):
-        end[f] = seconds[f].finish().astype(BF16)
-        for h in range(2):
-            goal = 2 * j + h
-            sends.append(
-                (end.at[f, h], y, dev(goal, z, x, f), jnp.logical_and(goal == y, f == j))
-            )
-    send_last(end, land, sends, ls.at[0], lr.at[0], lc.at[0], True)
-    mine = lax.div(y, 2) == j
-    send_last(q_end, q_land, q_sends, ls.at[1], lr.at[1], lc.at[1], False)
-    sum_last(q_end.at[0, pl.ds(0, 80)], q_land, ls.at[1], lr.at[1], y, mine, partner, oq)
-    send_last(end, land, sends, ls.at[0], lr.at[0], lc.at[0], False)
-    sum_last(end.at[0, 0], land, ls.at[0], lr.at[0], y, mine, partner, okv)
-    for ring in firsts + seconds + [q2]:
-        ring.drain()
-    give.wait_send()
-
-
-def finish(gkv, kvd, dq, q_mid, w, wother, tok, cot, gain):
-    return comm_call(
-        finish_kernel,
-        "finish",
-        3,
-        (sds((80, 256), F32), sds((80, 256), F32), sds((ROWS, D), BF16)),
-        [
-            pltpu.VMEM((2, ROWS, 512), BF16),
-            pltpu.VMEM((2, 8, D, 128), BF16),
-            pltpu.VMEM((ROWS, D), BF16),
-            pltpu.VMEM((ROWS, D), BF16),
-            pltpu.VMEM((5, ROWS, 512), F32),
-            pltpu.VMEM((2, 2, 4, 80, 256), BF16),
-            pltpu.VMEM((2, 2, 2, 4, 80, 256), BF16),
-            pltpu.VMEM((2, 2, 4, 80, 256), BF16),
-            pltpu.VMEM((2, 2, 80, 256), BF16),
-            pltpu.VMEM((2, 2, 2, 80, 256), BF16),
-            pltpu.VMEM((2, 2, 80, 256), BF16),
-            pltpu.VMEM((4, 80, 256), BF16),
-            pltpu.VMEM((2, 160, 256), BF16),
-            pltpu.VMEM((2, 2, 160, 256), BF16),
-            pltpu.VMEM((2, 160, 256), BF16),
-            pltpu.VMEM((4, 80, 256), BF16),
-            DMA((3, 2, 4)),
-            DMA((3, 2, 4)),
-            DMA((2, 4)),
-            DMA((2, 4)),
-            DMA((2,)),
-            DMA((2,)),
-            DMA((5,)),
-        ],
-        "vvvvhhhhv",
-        "vvv",
-    )(gkv, kvd, dq, q_mid, w, wother, tok, cot, gain)
+        (sds((32, 640), F32), sds((80, 256), F32), sds((80, 256), F32), sds((ROWS, D), BF16)),
+        [pltpu.VMEM(*spec) for spec in TAIL.values()] + [DMA(n) for n in TAIL_SEMS.values()],
+        "hhhhhhvvvhhhhhhv",
+        "vvvh",
+    )(
+        q.reshape(2, 2, 3, 128, 256),
+        unit,
+        halo,
+        soft,
+        grad,
+        raw.reshape(3, 2, 3, 128, 256),
+        cos.reshape(2, 3, 128, 128),
+        sin.reshape(2, 3, 128, 128),
+        gains,
+        go,
+        n2,
+        w,
+        wother,
+        tok,
+        cot,
+        gain,
+    )
 
 
 def per_device(
@@ -1241,14 +1258,12 @@
     n2, w = gather(noted, query_weight, key_weight, value_weight)
     q, unit, raw = project(n2, w, cos, sin, gains)
     halo, wo, wother = exchange_halo(unit, output_weight.reshape(2, 128, D), w)
-    layer_out, own, parts, qd, o_mid, gq = middle(
-        q, unit, halo, base, wo.reshape(1024, D), tok, cot, post_gain.reshape(1, D),
-        raw, cos, sin, gains, n2,
-    )
-    total, oo, q_mid, dq = return_grads(parts, own, o_mid, gq, qd.reshape(2, ROWS, 512))
-    gkv, kvd = key_grads(n2, total.reshape(2 * ROWS, 512), raw, cos, sin, gains)
-    okv, oq, tokens_grad = finish(
-        gkv, kvd.reshape(2, ROWS, 512), dq, q_mid, w, wother, tok, cot, input_gain.reshape(1, D)
+    layer_out, grad, go, soft = middle(
+        q, unit, halo, base, wo.reshape(1024, D), tok, cot, post_gain.reshape(1, D)
+    )
+    oo, oq, okv, tokens_grad = tail(
+        q, unit, halo, soft, grad, raw, cos, sin, gains, go, n2, w, wother, tok, cot,
+        input_gain.reshape(1, D),
     )
     shape = (seq_count, shard_size, width)
     return (

time: 267 us -> 242 us (0.906)
  Pallas kernels: 250 us -> 224 us
    pallas_call x1, Pallas kernels: 54 us -> 26.6 us  [middle(): comm_call(middle_kernel, 'middle', 4, (sds((ROWS, D), BF16), sds((2, 3, 1...]
    pallas_call x3 -> x1, Pallas kernels: 108 us -> 109 us  [tail(): comm_call(tail_kernel, 'tail', 2, (sds((32, 640), F32), sds((80, 256), F3...]
where the time goes in v3:
time: 242 us
  Pallas kernels  224 us (93%)
  local copies, waits for them, and re-layouts  10.5 us (4%)
  other arithmetic  6.78 us (3%)
    pallas_call x1, Pallas kernels, tail(): comm_call(tail_kernel, 'tail', 2, (sds((32, 640), F32), sds((80, 256), F3...  109 us
    pallas_call x1, Pallas kernels, exchange_halo(): comm_call(halo_kernel, 'exchange_halo', 1, (sds((4, UNIT, 512), BF16), sd...  45.9 us
    pallas_call x1, Pallas kernels, gather(): comm_call(gather_kernel, 'gather_weights', 0, (sds((2, ROWS + NOTE_ROWS,...  31.9 us
    pallas_call x1, Pallas kernels, middle(): comm_call(middle_kernel, 'middle', 4, (sds((ROWS, D), BF16), sds((2, 3, 1...  26.6 us
    pallas_call x1, Pallas kernels, project(): pl.pallas_call(project_kernel, name='project', grid=(4,), in_specs=[pl.Bl...  10 us
    unnamed x21, local copies, waits for them, and re-layouts  5.52 us

profile of v3, /device:TPU:1, one launch (start us, length us, event | category | flops | bytes accessed | tf_op | source)
XLA Modules:
  0.0 241.6 jit_solution(17480304161835967029)
XLA Ops:
  0.6 0.0 copy-start
  0.7 0.8 convert_bitcast_fusion
  1.5 0.1 broadcast_select_fusion
  1.6 2.0 multiply_reduce_fusion
  3.6 1.2 multiply_convert_fusion
  4.8 1.5 pad_maximum_fusion.n_ref
  6.3 31.9 %gather_weights.1 = (bf16[2,400,2560]{2,1,0:T(8,128)(2,1)}, bf16[8,2560,128]{2,1,0:T(8,128)(2,1)}) custom-call(bf16[400,2560]{1,0:T(8,128)(2,1)} %pad_maximum_fusion.n_ref, bf16[640,1024]{1,0:T(8,128)(2,1)} %wq.1, bf16[640,512]{1,0:T(8,128)(2,1)} %wk.1, bf16[640,512]{1,0:T(8,128)(2,1)} %wv.1), custom_call_target="tpu_custom_call" | custom-call | tf_op jit(solution)/shard_map/gather_weights/pallas_call | solution.py:223
  38.3 0.5 multiply_sine_fusion
  38.8 0.8 broadcast_in_dim.45.cos
  39.6 0.8 broadcast_in_dim.46.sin
  40.4 0.0 copy-done.7
  40.4 0.6 select_maximum_fusion.gains
  41.0 10.0 %project.1 = (bf16[2,768,256]{2,1,0:T(8,128)(2,1)}, bf16[784,512]{1,0:T(8,128)(2,1)}, f32[3,768,256]{2,1,0:T(8,128)}) custom-call(bf16[2,400,2560]{2,1,0:T(8,128)(2,1)} %get-tuple-element.22.n2.n2_h, bf16[8,2560,128]{2,1,0:T(8,128)(2,1)} %get-tuple-element.23.w.w_h, f32[768,128]{1,0:T(8,128)} %bitcast.26, f32[768,128]{1,0:T(8,128)} %bitcast.27, ...), custom_call_target="tpu_custom_call" | custom-call | tf_op jit(solution)/shard_map/project/pallas_call | solution.py:275
  51.1 45.9 %exchange_halo.1 = (bf16[4,784,512]{2,1,0:T(8,128)(2,1)}, bf16[4,2,128,2560]{3,2,1,0:T(8,128)(2,1)}, bf16[8,2560,128]{2,1,0:T(8,128)(2,1)}) custom-call(bf16[784,512]{1,0:T(8,128)(2,1)} %get-tuple-element.25.unit.unit_h, bf16[2,128,2560]{2,1,0:T(8,128)(2,1)} %bitcast.33, bf16[8,2560,128]{2,1,0:T(8,128)(2,1)} %get-tuple-element.23.w.w_h), custom_call_target="tpu_custom_call" | custom-call | tf_op jit(solution)/shard_map/exchange_halo/pallas_call | solution.py:435
  96.9 0.6 broadcast_in_dim.47.base
  97.5 0.6 reshape.132.gain
  98.1 26.6 %middle.1 = (bf16[384,2560]{1,0:T(8,128)(2,1)}, bf16[2,3,128,512]{3,2,1,0:T(8,128)(2,1)}, bf16[4,2,4,64,640]{4,3,2,1,0:T(8,128)(2,1)}, bf16[3,512,1280]{2,1,0:T(8,128)(2,1)}) custom-call(bf16[2,2,3,128,256]{4,3,2,1,0:T(8,128)(2,1)} %bitcast.28, bf16[784,512]{1,0:T(8,128)(2,1)} %get-tuple-element.25.unit.unit_h, ...), custom_call_target="tpu_custom_call" | custom-call | tf_op jit(solution)/shard_map/middle/pallas_call | solution.py:664
  124.8 0.6 broadcast_in_dim.48.gain
  125.4 109.1 %tail.1 = (f32[32,640]{1,0:T(8,128)}, f32[80,256]{1,0:T(8,128)}, f32[80,256]{1,0:T(8,128)}, bf16[384,2560]{1,0:T(8,128)(2,1)}) custom-call(bf16[2,2,3,128,256]{4,3,2,1,0:T(8,128)(2,1)} %bitcast.29, bf16[784,512]{1,0:T(8,128)(2,1)} %get-tuple-element.25.unit.unit_h, bf16[4,784,512]{2,1,0:T(8,128)(2,1)} %get-tuple-element.26.halo.halo_h, ...), custom_call_target="tpu_custom_call" | custom-call | tf_op jit(solution)/shard_map/tail/pallas_call | solution.py:1191
  234.5 1.6 fusion
  236.1 2.9 %copy.24 = bf16[3,128,2560]{2,1,0:T(8,128)(2,1)} copy(bf16[3,128,2560]{2,1,0:T(8,128)(2,1)} %bitcast.31) | data formatting | bytes 3932160
  239.0 1.3 copy.25
  240.3 0.6 copy.26
  240.9 0.6 copy.27
  (20 shorter events, 0.1 us)
Async XLA Ops:
  0.6 3.0 %copy-start = (bf16[3,128,2560]{2,1,0:T(8,128)(2,1)S(1)}, bf16[3,128,2560]{2,1,0:T(8,128)(2,1)}, u32[]{:S(2)}) copy-start(bf16[3,128,2560]{2,1,0:T(8,128)(2,1)} %param.11) | copy-start | bytes 5898244
  6.3 34.1 %copy-start.6 = (f32[256]{0:T(256)S(1)}, f32[256]{0:T(256)}, u32[]{:S(2)}) copy-start(f32[256]{0:T(256)} %param.20) | copy-start | bytes 3076
  6.3 34.1 %copy-start.7 = (f32[256]{0:T(256)S(1)}, f32[256]{0:T(256)}, u32[]{:S(2)}) copy-start(f32[256]{0:T(256)} %param.19) | copy-start | bytes 3076
  51.1 46.5 %copy-start.5 = (f32[2560]{0:T(1024)S(1)}, f32[2560]{0:T(1024)}, u32[]{:S(2)}) copy-start(f32[2560]{0:T(1024)} %param.21) | copy-start | bytes 30724
  98.1 26.6 %copy-start.4 = (f32[2560]{0:T(1024)S(1)}, f32[2560]{0:T(1024)}, u32[]{:S(2)}) copy-start(f32[2560]{0:T(1024)} %param.14) | copy-start | bytes 30724
  234.5 4.5 %copy-start.1 = (bf16[384,2560]{1,0:T(8,128)(2,1)S(1)}, bf16[384,2560]{1,0:T(8,128)(2,1)}, u32[]{:S(2)}) copy-start(bf16[384,2560]{1,0:T(8,128)(2,1)} %get-tuple-element.34) | copy-start | bytes 5898244
  239.0 1.3 copy-start.3
  239.0 1.9 copy-start.2
